TPU v7x, 32 devices: a whole 2x2x4 slice. The times are simulated.
32 devices in a mesh: dp: 8 (over z, y), row: 2 (over x), col: 2 (over core).
Axes of the slice: x: 2, y: 2, z: 4, core: 2. Of those that a mesh axis runs over, the one named last changes fastest.
Arguments:
- tokens: bfloat16 [16384, 1024], P('dp', 'row'), may hold values from -6 to 6
- seq_lengths: int32 [8, 2], P('dp'), may hold values from 0 to 2048, as said below
- query_weight: bfloat16 [1024, 1024], P('row', 'col'), may hold values from -0.1875 to 0.1875
- key_matrix: bfloat16 [1024, 512], P('row', 'col'), may hold values from -0.1875 to 0.1875
- value_matrix: bfloat16 [1024, 512], P('row', 'col'), may hold values from -0.1875 to 0.1875
- out_weight: bfloat16 [1024, 1024], P('col', 'row'), may hold values from -3 to 3
- gate_weight: bfloat16 [1024, 4608], P('row', 'col'), may hold values from -0.1875 to 0.1875
- up_weight: bfloat16 [1024, 4608], P('row', 'col'), may hold values from -0.1875 to 0.1875
- down_weight: bfloat16 [4608, 1024], P('col', 'row'), may hold values from -0.09375 to 0.09375
- attn_gain: float32 [1024], P('row'), may hold values from 0.5 to 2
- ffn_gain: float32 [1024], P('row'), may hold values from 0.5 to 2
- query_gain: float32 [64], replicated, may hold values from 0.5 to 2
- key_gain: float32 [64], replicated, may hold values from 0.5 to 2
- cotangent: bfloat16 [16384, 1024], P('dp', 'row'), may hold values from -6 to 6
Outputs:
- output: bfloat16 [16384, 1024], P('dp', 'row')
- grad_tokens: bfloat16 [16384, 1024], P('dp', 'row')
- grad_query_weight: float32 [1024, 1024], P('row', 'col')
- grad_key_weight: float32 [1024, 512], P('row', 'col')
- grad_value_weight: float32 [1024, 512], P('row', 'col')
- grad_out_weight: float32 [1024, 1024], P('col', 'row')
- grad_gate_weight: float32 [1024, 4608], P('row', 'col')
- grad_up_weight: float32 [1024, 4608], P('row', 'col')
- grad_down_weight: float32 [4608, 1024], P('col', 'row')
- grad_attn_gain: float32 [1024], P('row')
- grad_ffn_gain: float32 [1024], P('row')
- grad_query_gain: float32 [64], replicated
- grad_key_gain: float32 [64], replicated
Inputs may be any that keep to these rules, and one draw needn't show every extreme that they name: `seq_lengths`: each row sums to 2048; a present sequence has 1024 tokens or more, a zero stands only after a sequence of 2048 tokens.
All inputs are finite; a program needn't handle non-finite values.
Results may differ from a plain program's by a relative error of at most 0.015.
The roundings to bfloat16 on the way count: a program that leaves them out, or rounds other values in their place, can miss the bound.
Values may be sent and summed in bfloat16 or wider, within the bound.
A program may use at most 256 MiB of HBM per device.

v0:
```python
import math

import jax
import jax.numpy as jnp
from jax import lax
from jax.sharding import PartitionSpec as P

MODEL_WIDTH = 1024
HEAD_SIZE = 64


EPSILON = 1e-05
ROPE_BASE = 1000000.0
NEGATIVE = -1e30


def for_sending(x):

    def short(part):
        return part.astype(jnp.bfloat16) if part.dtype == jnp.float32 else part

    return jax.tree.map(short, x)


def layout(lengths, packed_length):
    seq_ends = jnp.cumsum(lengths)
    starts = seq_ends - lengths
    places = jnp.arange(packed_length, dtype=jnp.int32)
    member = jnp.sum((places[:, None] >= seq_ends[None, :]).astype(jnp.int32), axis=1)
    picked = member[:, None] == jnp.arange(lengths.shape[0], dtype=jnp.int32)[None, :]
    offset = jnp.sum(jnp.where(picked, starts[None, :], 0), axis=1)
    return (member, places - offset)


def rotate(operand, position):
    half_width = operand.shape[-1] // 2
    freq_index = jnp.arange(half_width, dtype=jnp.float32)
    inverse = jnp.exp(freq_index * (-2.0 * math.log(ROPE_BASE) / operand.shape[-1]))
    angles = position.astype(jnp.float32)[:, None] * inverse[None, :]
    cosine = jnp.cos(angles)[:, None, :]
    sine_part = jnp.sin(angles)[:, None, :]
    first_half = operand[..., :half_width]
    second = operand[..., half_width:]
    return jnp.concatenate(
        [first_half * cosine - second * sine_part, second * cosine + first_half * sine_part],
        axis=-1,
    )


def head_prepare(raw_in, gain_in, position):
    head_rows = raw_in.reshape(raw_in.shape[0], -1, HEAD_SIZE)
    normed_inputs = (
        head_rows
        * lax.rsqrt(jnp.mean(head_rows * head_rows, axis=-1, keepdims=True) + EPSILON)
        * gain_in
    )
    return rotate(normed_inputs, position)


def feature_total(operand):
    return lax.psum(operand, "row")


def column_total(operand):
    return lax.psum(operand, "col")


def column_grads(operand):
    return lax.psum(operand, "col")


def scatter_back(operand):
    return lax.psum_scatter(operand, "row", scatter_dimension=1, tiled=True)


def gather_grads(operand):
    return jax.tree.map(
        lambda part, own: part.astype(own.dtype),
        lax.all_gather(for_sending(operand), "row", axis=1, tiled=True),
        operand,
    )


def contract_rows(left_side, right_side):
    return lax.dot_general(
        left_side, right_side, (((0,), (0,)), ((), ())), preferred_element_type=jnp.float32
    )


def times_transpose(left_side, right_side):
    return lax.dot_general(
        left_side, right_side, (((1,), (1,)), ((), ())), preferred_element_type=jnp.float32
    )


def block_scores(query_block, key_block):
    return jnp.einsum(
        "ikgd,jkd->kgij", query_block, key_block, preferred_element_type=jnp.float32
    ) * HEAD_SIZE ** (-0.5)


def block_mask(member, query_start, key_start, block_rows):
    offsets = jnp.arange(block_rows, dtype=jnp.int32)
    query_doc = lax.dynamic_slice_in_dim(member, query_start, block_rows)
    key_doc = lax.dynamic_slice_in_dim(member, key_start, block_rows)
    causal = (key_start + offsets)[None, :] <= (query_start + offsets)[:, None]
    return causal & (key_doc[None, :] == query_doc[:, None])


def guarded(query_index, key_index, update, loop_state):
    needed = key_index <= query_index
    return lax.cond(needed, update, lambda unchanged: unchanged, loop_state)


def add_block(buffer, addend, start_row):
    current = lax.dynamic_slice_in_dim(buffer, start_row, addend.shape[0])
    return lax.dynamic_update_slice_in_dim(buffer, current + addend, start_row, 0)


def attend(query_rows, keys, values, member, block_rows):
    packed_length = query_rows.shape[0]
    blocks = packed_length // block_rows
    kv_heads, group_size = (query_rows.shape[1], query_rows.shape[2])

    def query_step(query_index, carried):
        outputs, totals = carried
        query_start = query_index * block_rows
        query_block = lax.dynamic_slice_in_dim(query_rows, query_start, block_rows)

        def stats_step(key_index, loop_state):

            def update(running):
                run_peak, run_mass = running
                key_start = key_index * block_rows
                allowed = block_mask(member, query_start, key_start, block_rows)
                scores = jnp.where(
                    allowed,
                    block_scores(
                        query_block, lax.dynamic_slice_in_dim(keys, key_start, block_rows)
                    ),
                    NEGATIVE,
                )
                new_peak = jnp.maximum(run_peak, jnp.max(scores, axis=-1))
                new_mass = run_mass * jnp.exp(run_peak - new_peak) + jnp.sum(
                    jnp.where(allowed, jnp.exp(scores - new_peak[..., None]), 0.0), axis=-1
                )
                return (new_peak, new_mass)

            return guarded(query_index, key_index, update, loop_state)

        start_state = (
            jnp.full((kv_heads, group_size, block_rows), NEGATIVE, jnp.float32),
            jnp.zeros((kv_heads, group_size, block_rows), jnp.float32),
        )
        run_peak, run_mass = lax.fori_loop(0, blocks, stats_step, start_state)
        log_total = run_peak + jnp.log(run_mass)

        def value_step(key_index, loop_state):

            def update(running):
                key_start = key_index * block_rows
                allowed = block_mask(member, query_start, key_start, block_rows)
                scores = block_scores(
                    query_block, lax.dynamic_slice_in_dim(keys, key_start, block_rows)
                )
                probs_low = jnp.where(allowed, jnp.exp(scores - log_total[..., None]), 0.0).astype(
                    jnp.bfloat16
                )
                return running + jnp.einsum(
                    "kgij,jkd->ikgd",
                    probs_low,
                    lax.dynamic_slice_in_dim(values, key_start, block_rows),
                    preferred_element_type=jnp.float32,
                )

            return guarded(query_index, key_index, update, loop_state)

        block_out = lax.fori_loop(
            0,
            blocks,
            value_step,
            jnp.zeros((block_rows, kv_heads, group_size, HEAD_SIZE), jnp.float32),
        )
        outputs = lax.dynamic_update_slice_in_dim(outputs, block_out, query_start, 0)
        totals = lax.dynamic_update_slice_in_dim(totals, log_total, query_start, 2)
        return (outputs, totals)

    initial = (
        jnp.zeros((packed_length, kv_heads, group_size, HEAD_SIZE), jnp.float32),
        jnp.zeros((kv_heads, group_size, packed_length), jnp.float32),
    )
    return lax.fori_loop(0, blocks, query_step, initial)


def attend_back(query_rows, keys, values, outputs, totals, grad_out, member, block_rows):
    packed_length = query_rows.shape[0]
    blocks = packed_length // block_rows
    kv_heads, group_size = (query_rows.shape[1], query_rows.shape[2])
    balance = jnp.einsum("ikgd,ikgd->kgi", grad_out.astype(jnp.float32), outputs)

    def query_step(query_index, carried):
        grad_queries, grad_keys, grad_values = carried
        query_start = query_index * block_rows
        query_block = lax.dynamic_slice_in_dim(query_rows, query_start, block_rows)
        query_wide = query_block.astype(jnp.float32)
        grad_block = lax.dynamic_slice_in_dim(grad_out, query_start, block_rows)
        log_total = lax.dynamic_slice_in_dim(totals, query_start, block_rows, 2)
        balance_block = lax.dynamic_slice_in_dim(balance, query_start, block_rows, 2)

        def key_step(key_index, loop_state):

            def update(running):
                grad_query, grad_keys, grad_values = running
                key_start = key_index * block_rows
                key_block = lax.dynamic_slice_in_dim(keys, key_start, block_rows)
                value_block = lax.dynamic_slice_in_dim(values, key_start, block_rows)
                allowed = block_mask(member, query_start, key_start, block_rows)
                probs = jnp.where(
                    allowed,
                    jnp.exp(block_scores(query_block, key_block) - log_total[..., None]),
                    0.0,
                )
                probs_low = probs.astype(jnp.bfloat16)
                value_part = jnp.einsum(
                    "kgij,ikgd->jkd", probs_low, grad_block, preferred_element_type=jnp.float32
                )
                grad_probs = jnp.einsum(
                    "ikgd,jkd->kgij", grad_block, value_block, preferred_element_type=jnp.float32
                )
                grad_scores = probs * (grad_probs - balance_block[..., None])
                grad_query = grad_query + jnp.einsum(
                    "kgij,jkd->ikgd",
                    grad_scores,
                    key_block.astype(jnp.float32),
                    precision=lax.Precision.HIGHEST,
                    preferred_element_type=jnp.float32,
                ) * HEAD_SIZE ** (-0.5)
                key_part = jnp.einsum(
                    "kgij,ikgd->jkd",
                    grad_scores,
                    query_wide,
                    precision=lax.Precision.HIGHEST,
                    preferred_element_type=jnp.float32,
                ) * HEAD_SIZE ** (-0.5)
                return (
                    grad_query,
                    add_block(grad_keys, key_part, key_start),
                    add_block(grad_values, value_part, key_start),
                )

            return guarded(query_index, key_index, update, loop_state)

        start_state = (
            jnp.zeros((block_rows, kv_heads, group_size, HEAD_SIZE), jnp.float32),
            grad_keys,
            grad_values,
        )
        grad_query, grad_keys, grad_values = lax.fori_loop(0, blocks, key_step, start_state)
        grad_queries = lax.dynamic_update_slice_in_dim(grad_queries, grad_query, query_start, 0)
        return (grad_queries, grad_keys, grad_values)

    initial = (
        jnp.zeros((packed_length, kv_heads, group_size, HEAD_SIZE), jnp.float32),
        jnp.zeros((packed_length, kv_heads, HEAD_SIZE), jnp.float32),
        jnp.zeros((packed_length, kv_heads, HEAD_SIZE), jnp.float32),
    )
    return lax.fori_loop(0, blocks, query_step, initial)


def shards(
    tokens,
    seq_lengths,
    query_weight,
    key_matrix,
    value_matrix,
    out_weight,
    gate_weight,
    up_weight,
    down_weight,
    attn_gain,
    ffn_gain,
    query_gain,
    key_gain,
    cotangent,
):
    packed_length = tokens.shape[0]
    block_rows = min(512, packed_length)
    row_parts = lax.axis_size("row")
    member, position = layout(seq_lengths[0], packed_length)
    inputs = tokens.astype(jnp.float32)
    inverse_one = lax.rsqrt(feature_total(jnp.sum(inputs * inputs, axis=1)) / MODEL_WIDTH + EPSILON)
    normal_one = inputs * inverse_one[:, None]
    hidden_one = (normal_one * attn_gain).astype(jnp.bfloat16)
    query_part = jnp.dot(hidden_one, query_weight, preferred_element_type=jnp.float32).reshape(
        packed_length, row_parts, -1
    )
    key_part = jnp.dot(hidden_one, key_matrix, preferred_element_type=jnp.float32).reshape(
        packed_length, row_parts, -1
    )
    value_part = jnp.dot(hidden_one, value_matrix, preferred_element_type=jnp.float32).reshape(
        packed_length, row_parts, -1
    )
    query_raw, key_unnormed, value_unnormed = (
        lax.psum_scatter(query_part, "row", scatter_dimension=1, tiled=True),
        lax.psum_scatter(key_part, "row", scatter_dimension=1, tiled=True),
        lax.psum_scatter(value_part, "row", scatter_dimension=1, tiled=True),
    )
    query_raw = query_raw.reshape(packed_length, -1)
    key_unnormed = key_unnormed.reshape(packed_length, -1)
    value_unnormed = value_unnormed.reshape(packed_length, -1)
    kv_local = key_unnormed.shape[1] // HEAD_SIZE
    query_rows, query_back = jax.vjp(
        lambda raw_in, gain_in: head_prepare(raw_in, gain_in, position), query_raw, query_gain
    )
    keys, key_back = jax.vjp(
        lambda raw_in, gain_in: head_prepare(raw_in, gain_in, position), key_unnormed, key_gain
    )
    query_low = query_rows.astype(jnp.bfloat16).reshape(packed_length, kv_local, -1, HEAD_SIZE)
    key_low = keys.astype(jnp.bfloat16)
    value_low = value_unnormed.astype(jnp.bfloat16).reshape(packed_length, kv_local, HEAD_SIZE)
    outputs, totals = attend(query_low, key_low, value_low, member, block_rows)
    attended = outputs.reshape(packed_length, -1).astype(jnp.bfloat16)
    attended_all = lax.all_gather(attended, "row", axis=1, tiled=True)
    branch = column_total(jnp.dot(attended_all, out_weight, preferred_element_type=jnp.float32))
    middle = inputs + branch
    inverse_two = lax.rsqrt(feature_total(jnp.sum(middle * middle, axis=1)) / MODEL_WIDTH + EPSILON)
    normal_two = middle * inverse_two[:, None]
    hidden_two = (normal_two * ffn_gain).astype(jnp.bfloat16)
    gate_part = jnp.dot(hidden_two, gate_weight, preferred_element_type=jnp.float32).reshape(
        packed_length, row_parts, -1
    )
    up_part = jnp.dot(hidden_two, up_weight, preferred_element_type=jnp.float32).reshape(
        packed_length, row_parts, -1
    )
    gate_raw, up_raw = (
        lax.psum_scatter(gate_part, "row", scatter_dimension=1, tiled=True),
        lax.psum_scatter(up_part, "row", scatter_dimension=1, tiled=True),
    )
    gate_raw = gate_raw.reshape(packed_length, -1)
    up_raw = up_raw.reshape(packed_length, -1)
    active, active_back = jax.vjp(
        lambda gate_in, upward_in: jax.nn.silu(gate_in) * upward_in, gate_raw, up_raw
    )
    active_all = lax.all_gather(active.astype(jnp.bfloat16), "row", axis=1, tiled=True)
    result = middle + column_total(
        jnp.dot(active_all, down_weight, preferred_element_type=jnp.float32)
    )
    output = result.astype(jnp.bfloat16)
    grad_down = contract_rows(active_all, cotangent)
    grad_active = scatter_back(times_transpose(cotangent, down_weight))
    grad_gate, grad_up = active_back(grad_active)
    gate_all, up_all = gather_grads((grad_gate.astype(jnp.bfloat16), grad_up.astype(jnp.bfloat16)))
    grad_gate_w = contract_rows(hidden_two, gate_all)
    grad_up_w = contract_rows(hidden_two, up_all)
    grad_hidden_two = column_grads(
        times_transpose(gate_all, gate_weight) + times_transpose(up_all, up_weight)
    )
    grad_ffn_gain = jnp.sum(grad_hidden_two * normal_two, axis=0)
    grad_normal_two = grad_hidden_two * ffn_gain
    stat_two = feature_total(jnp.sum(grad_normal_two * normal_two, axis=1))
    grad_middle = inverse_two[:, None] * (
        grad_normal_two - normal_two * (stat_two / MODEL_WIDTH)[:, None]
    ) + cotangent.astype(jnp.float32)
    branch_low = grad_middle.astype(jnp.bfloat16)
    grad_out_w = contract_rows(attended_all, branch_low)
    attended_grad = scatter_back(times_transpose(branch_low, out_weight))
    grad_attended = attended_grad.astype(jnp.bfloat16).reshape(
        packed_length, kv_local, -1, HEAD_SIZE
    )
    grad_queries, grad_keys, grad_values = attend_back(
        query_low, key_low, value_low, outputs, totals, grad_attended, member, block_rows
    )
    grad_query_raw, grad_query_gain = query_back(grad_queries.reshape(packed_length, -1, HEAD_SIZE))
    grad_key_raw, grad_key_gain = key_back(grad_keys)
    query_all, key_all, value_all = gather_grads(
        (
            grad_query_raw.astype(jnp.bfloat16),
            grad_key_raw.astype(jnp.bfloat16),
            grad_values.reshape(packed_length, -1).astype(jnp.bfloat16),
        )
    )
    grad_query_w = contract_rows(hidden_one, query_all)
    grad_key_w = contract_rows(hidden_one, key_all)
    grad_value_w = contract_rows(hidden_one, value_all)
    hidden_sum = (
        times_transpose(query_all, query_weight)
        + times_transpose(key_all, key_matrix)
        + times_transpose(value_all, value_matrix)
    )
    grad_hidden_one, query_gain_col, key_gain_col = column_grads(
        (hidden_sum, grad_query_gain, grad_key_gain)
    )
    grad_attn_gain = jnp.sum(grad_hidden_one * normal_one, axis=0)
    grad_normal_one = grad_hidden_one * attn_gain
    stat_one, query_gain_row, key_gain_row = feature_total(
        (jnp.sum(grad_normal_one * normal_one, axis=1), query_gain_col, key_gain_col)
    )
    grad_inputs = (
        inverse_one[:, None] * (grad_normal_one - normal_one * (stat_one / MODEL_WIDTH)[:, None])
        + grad_middle
    )
    (
        grad_query_w,
        grad_key_w,
        grad_value_w,
        grad_out_w,
        grad_gate_w,
        grad_up_w,
        grad_down,
        grad_attn_gain,
        grad_ffn_gain,
        query_gain_row,
        key_gain_row,
    ) = lax.psum(
        (
            grad_query_w,
            grad_key_w,
            grad_value_w,
            grad_out_w,
            grad_gate_w,
            grad_up_w,
            grad_down,
            grad_attn_gain,
            grad_ffn_gain,
            query_gain_row,
            key_gain_row,
        ),
        "dp",
    )
    return (
        output,
        grad_inputs.astype(jnp.bfloat16),
        grad_query_w,
        grad_key_w,
        grad_value_w,
        grad_out_w,
        grad_gate_w,
        grad_up_w,
        grad_down,
        grad_attn_gain,
        grad_ffn_gain,
        query_gain_row,
        key_gain_row,
    )


def solution(mesh):
    return jax.shard_map(
        shards,
        mesh=mesh,
        in_specs=(
            P("dp", "row"),
            P("dp", None),
            P("row", "col"),
            P("row", "col"),
            P("row", "col"),
            P("col", "row"),
            P("row", "col"),
            P("row", "col"),
            P("col", "row"),
            P("row"),
            P("row"),
            P(),
            P(),
            P("dp", "row"),
        ),
        out_specs=(
            P("dp", "row"),
            P("dp", "row"),
            P("row", "col"),
            P("row", "col"),
            P("row", "col"),
            P("col", "row"),
            P("row", "col"),
            P("row", "col"),
            P("col", "row"),
            P("row"),
            P("row"),
            P(),
            P(),
        ),
        check_vma=False,
    )
```

profile of v0, /device:TPU:0, one launch (start us, length us, event | category | flops | bytes accessed | tf_op | source)
XLA Modules:
  0.0 2164.0 jit_solution(7526656655737362226)
XLA Ops:
  30.7 22.5 %reduce-scatter.12.cloned.1.call-done = f32[2048,1,128]{0,2,1:T(8,128)} async-done(((f32[2048,2,128]{0,2,1:T(8,128)}), f32[2048,1,128]{0,2,1:T(8,128)}) %reduce-scatter.12.cloned.1.call-update) | async-done | bytes 1048592 | tf_op jit(solution)/shard_map/reduce_scatter | solution.py:306
  55.3 32.7 %reduce-scatter.10.cloned.1.call-done = f32[2048,1,128]{0,2,1:T(8,128)} async-done(((f32[2048,2,128]{0,2,1:T(8,128)}), f32[2048,1,128]{0,2,1:T(8,128)}) %reduce-scatter.10.cloned.1.call-update) | async-done | bytes 1048592 | tf_op jit(solution)/shard_map/reduce_scatter | solution.py:305
  91.0 54.2 %reduce-scatter.8.cloned.1.call-done = f32[2048,1,256]{0,2,1:T(8,128)} async-done(((f32[2048,2,256]{0,2,1:T(8,128)}), f32[2048,1,256]{0,2,1:T(8,128)}) %reduce-scatter.8.cloned.1.call-update) | async-done | bytes 2097168 | tf_op jit(solution)/shard_map/reduce_scatter | solution.py:304
  153.1 75.2 %while.126 = (s32[]{:T(128)}, f32[2048,2,2,64]{0,3,2,1:T(8,128)}, f32[2,2,2048]{2,1,0:T(2,128)S(1)}, bf16[2048,2,2,64]{0,3,2,1:T(8,128)(2,1)}, s32[2048]{0:T(102...) while((s32[]{:T(128)}, f32[2048,2,2,64]{0,3,2,1:T(8,128)}, ...), condition=%wide.region_21.22_spmd, body=%wide.region_10.21_spmd.sunk | while | flops 416948224 | bytes 13969349 | solution.py:192
  169.8 7.2 while.130
  179.8 7.3 while.129
  188.0 10.7 while.130
  201.6 9.7 while.129
  212.2 14.3 while.130
  231.4 33.0 %all-gather.8.cloned.1.call-done = bf16[2048,512]{0,1:T(8,128)(2,1)} async-done(((bf16[2048,256]{0,1:T(8,128)(2,1)}), bf16[2048,512]{0,1:T(8,128)(2,1)}) %all-gather.8.cloned.1.call-update) | async-done | bytes 2097168 | tf_op jit(solution)/shard_map/all_gather | solution.py:323
  269.4 12.7 fusion.106
  282.3 15.7 all-reduce.14.cloned.1.call-done
  316.2 6.8 copy.79
  323.3 7.5 fusion.104
  330.8 6.9 copy.78
  337.7 175.3 %reduce-scatter.18.cloned.1.call-done = f32[2048,1152]{1,0:T(8,128)} async-done(((f32[2048,2304]{1,0:T(8,128)}), f32[2048,1152]{1,0:T(8,128)}) %reduce-scatter.18.cloned.1.call-update) | async-done | bytes 9437200 | tf_op jit(solution)/shard_map/reduce_scatter | solution.py:73
  513.0 214.1 %reduce-scatter.14.cloned.1.call-done = f32[2048,1,1152]{2,0,1:T(8,128)} async-done(((f32[2048,2,1152]{2,0,1:T(8,128)}), f32[2048,1,1152]{2,0,1:T(8,128)}) %reduce-scatter.14.cloned.1.call-update) | async-done | bytes 9437200 | tf_op jit(solution)/shard_map/reduce_scatter | solution.py:336
  727.1 214.0 %reduce-scatter.16.cloned.1.call-done = f32[2048,1,1152]{2,0,1:T(8,128)} async-done(((f32[2048,2,1152]{2,0,1:T(8,128)}), f32[2048,1,1152]{2,0,1:T(8,128)}) %reduce-scatter.16.cloned.1.call-update) | async-done | bytes 9437200 | tf_op jit(solution)/shard_map/reduce_scatter | solution.py:337
  941.1 17.2 multiply_convert_fusion
  959.4 117.0 %all-gather.12.cloned.1.call-done = bf16[2048,2304]{1,0:T(8,128)(2,1)} async-done(((bf16[2048,1152]{1,0:T(8,128)(2,1)}), bf16[2048,2304]{1,0:T(8,128)(2,1)}) %all-gather.12.cloned.1.call-update) | async-done | bytes 9437200 | tf_op jit(solution)/shard_map/all_gather | solution.py:79
  1076.5 10.4 fusion.107
  1086.8 109.7 %all-gather.14.cloned.1.call-done = bf16[2048,2304]{1,0:T(8,128)(2,1)} async-done(((bf16[2048,1152]{1,0:T(8,128)(2,1)}), bf16[2048,2304]{1,0:T(8,128)(2,1)}) %all-gather.14.cloned.1.call-update) | async-done | bytes 9437200 | tf_op jit(solution)/shard_map/all_gather | solution.py:79
  1196.5 11.4 convolution_add_fusion
  1207.9 28.5 %all-reduce.16.cloned.1.call-done = f32[2048,512]{1,0:T(8,128)} async-done(((f32[2048,512]{1,0:T(8,128)}), f32[2048,512]{1,0:T(8,128)}) %all-reduce.16.cloned.1.call-update) | async-done | bytes 4194320 | tf_op jit(solution)/shard_map/psum | solution.py:69
  1256.5 54.7 %reduce-scatter.20.cloned.1.call-done = f32[2048,256]{1,0:T(8,128)} async-done(((f32[2048,512]{1,0:T(8,128)}), f32[2048,256]{1,0:T(8,128)}) %reduce-scatter.20.cloned.1.call-update) | async-done | bytes 2097168 | tf_op jit(solution)/shard_map/reduce_scatter | solution.py:73
  1321.4 148.0 %while.128 = (s32[]{:T(128)}, f32[2048,2,2,64]{0,3,2,1:T(8,128)}, f32[2048,2,64]{0,2,1:T(8,128)}, f32[2048,2,64]{0,2,1:T(8,128)}, bf16[2048,2,2,64]{0,3,2,1:T(8,...) while((s32[]{:T(128)}, f32[2048,2,2,64]{0,3,2,1:T(8,128)}, ...), condition=%wide.region_38.39_spmd, body=%wide.region_33.38_spmd.sunk | while | flops 2024080384 | bytes 32977676 | solution.py:267
  1322.8 14.1 while.131
  1322.8 14.0 conditional.6
  1338.9 28.0 %while.131 = (s32[]{:T(128)}, f32[512,2,2,64]{0,3,2,1:T(8,128)S(1)}, f32[2048,2,64]{0,2,1:T(8,128)}, f32[2048,2,64]{0,2,1:T(8,128)}, s32[]{:T(128)}, /*index=5*/...) while((s32[]{:T(128)}, f32[512,2,2,64]{0,3,2,1:T(8,128)S(1)}, ...), condition=%wide.region_37.37_spmd, body=%wide.region_34.36_spmd.sunk | while | flops 2023949312 | bytes 29798832 | solution.py:258
  1338.9 14.0 conditional.6
  1352.9 13.9 conditional.6
  1368.9 41.9 %while.131 = (s32[]{:T(128)}, f32[512,2,2,64]{0,3,2,1:T(8,128)S(1)}, f32[2048,2,64]{0,2,1:T(8,128)}, f32[2048,2,64]{0,2,1:T(8,128)}, s32[]{:T(128)}, /*index=5*/...) while((s32[]{:T(128)}, f32[512,2,2,64]{0,3,2,1:T(8,128)S(1)}, ...), condition=%wide.region_37.37_spmd, body=%wide.region_34.36_spmd.sunk | while | flops 2023949312 | bytes 29798832 | solution.py:258
  1368.9 14.0 conditional.6
  1382.9 13.9 conditional.6
  1396.8 13.9 conditional.6
  1412.8 55.8 %while.131 = (s32[]{:T(128)}, f32[512,2,2,64]{0,3,2,1:T(8,128)S(1)}, f32[2048,2,64]{0,2,1:T(8,128)}, f32[2048,2,64]{0,2,1:T(8,128)}, s32[]{:T(128)}, /*index=5*/...) while((s32[]{:T(128)}, f32[512,2,2,64]{0,3,2,1:T(8,128)S(1)}, ...), condition=%wide.region_37.37_spmd, body=%wide.region_34.36_spmd.sunk | while | flops 2023949312 | bytes 29798832 | solution.py:258
  1412.8 14.0 conditional.6
  1426.8 13.9 conditional.6
  1440.7 13.9 conditional.6
  1454.7 13.9 conditional.6
  1483.4 9.6 fusion.105
  1499.1 19.3 all-gather.20.cloned.1.call-done
  1522.4 31.1 %all-gather.16.cloned.1.call-done = bf16[2048,512]{0,1:T(8,128)(2,1)} async-done(((bf16[2048,256]{0,1:T(8,128)(2,1)}), bf16[2048,512]{0,1:T(8,128)(2,1)}) %all-gather.16.cloned.1.call-update) | async-done | bytes 2097168 | tf_op jit(solution)/shard_map/all_gather | solution.py:79
  1553.6 7.4 add_add_fusion
  1562.5 10.5 fusion.110
  1573.1 11.6 fusion.111
  1611.2 23.2 %all-reduce.4 = (f32[512]{0:T(512)}, f32[512]{0:T(512)}, f32[64]{0:T(128)}, f32[64]{0:T(128)}) all-reduce(f32[512]{0:T(512)S(1)} %get-tuple-element.1092, f32[512]{0:T(512)S(1)} %copy-done.46, f32[64]{0:T(128)S(1)} %get-tuple-element.1212, f32[64]{0:T(128)S(1)} %get-tuple-element.1213), channel_id=1, replica_groups=mesh['dp'=8,'row'=2,'col'=2] {'dp'}, use_global_device_ids=true, to_apply=%region_52.53 | all-reduce | flops 1152 | bytes 9216 | tf_op jit(solution)/shard_map/psum | solution.py:414
  1643.4 496.3 %all-reduce.18.cloned.1.call-done = (f32[512,512]{1,0:T(8,128)}, f32[512,256]{1,0:T(8,128)}, f32[512,256]{1,0:T(8,128)}, f32[512,512]{1,0:T(8,128)}, f32[512,230...) async-done(((f32[512,512]{1,0:T(8,128)}, f32[512,256]{1,0:T(8,128)}, f32[512,256]{1,0:T(8,128)}, f32[512,512]{1,0:T(8,128)}, f32[512,2304]{1,0:T(8,128)}, ...) | async-done | bytes 17301520 | tf_op jit(solution)/shard_map/psum | solution.py:414
  (509 shorter events, 464.2 us)
Async XLA Ops:
  7.2 303.9 %copy-start = (bf16[512,2304]{1,0:T(8,128)(2,1)S(1)}, bf16[512,2304]{1,0:T(8,128)(2,1)}, u32[]{:S(2)}) copy-start(bf16[512,2304]{1,0:T(8,128)(2,1)} %param.36) | copy-start | bytes 7077892
  7.2 12.3 copy-start.43
  7.2 12.3 copy-start.38
  7.2 46.0 %reduce-scatter.12.cloned.1.call-start = ((), (), s32[]{:S(2)}) async-start(), calls=%async_computation.9 | async-start | bytes 3145728 | tf_op jit(solution)/shard_map/reduce_scatter | solution.py:306
  15.4 8.1 copy-start.34
  19.4 68.5 %reduce-scatter.10.cloned.1.call-start = ((), (), s32[]{:S(2)}) async-start(), calls=%async_computation.8 | async-start | bytes 3145728 | tf_op jit(solution)/shard_map/reduce_scatter | solution.py:305
  23.5 121.7 %reduce-scatter.8.cloned.1.call-start = ((), (), s32[]{:S(2)}) async-start(), calls=%async_computation.7 | async-start | bytes 6291456 | tf_op jit(solution)/shard_map/reduce_scatter | solution.py:304
  28.6 60.7 %copy-start.49 = (f32[64]{0:T(128)S(1)}, f32[64]{0:T(128)}, u32[]{:S(2)}) copy-start(f32[64]{0:T(128)} %param.42) | copy-start | bytes 772
  28.6 235.7 %all-gather.8.cloned.1.call-start = ((), (), s32[]{:S(2)}) async-start(), calls=%async_computation.10 | async-start | bytes 3145728 | tf_op jit(solution)/shard_map/all_gather | solution.py:323
  30.7 119.5 %copy-start.12 = (f32[2048,32]{0,1:T(8,128)}, f32[2048,32]{0,1:T(8,128)S(1)}, u32[]{:S(2)}) copy-start(f32[2048,32]{0,1:T(8,128)S(1)} %get-tuple-element.1245) | copy-start | bytes 786436
  30.7 119.5 %copy-start.14 = (f32[2048,32]{0,1:T(8,128)}, f32[2048,32]{0,1:T(8,128)S(1)}, u32[]{:S(2)}) copy-start(f32[2048,32]{0,1:T(8,128)S(1)} %get-tuple-element.1246) | copy-start | bytes 786436
  87.9 60.3 %copy-start.47 = (f32[64]{0:T(128)S(1)}, f32[64]{0:T(128)}, u32[]{:S(2)}) copy-start(f32[64]{0:T(128)} %param.41) | copy-start | bytes 772
  231.1 66.9 %all-reduce.14.cloned.1.call-start = ((), (), s32[]{:S(2)}) async-start(), calls=%async_computation.11 | async-start | bytes 8388608 | tf_op jit(solution)/shard_map/psum | solution.py:65
  269.4 243.6 %reduce-scatter.18.cloned.1.call-start = ((), (), s32[]{:S(2)}) async-start(), calls=%async_computation.15 | async-start | bytes 28311552 | tf_op jit(solution)/shard_map/reduce_scatter | solution.py:73
  282.2 26.2 %copy-start.45 = (f32[512]{0:T(512)S(1)}, f32[512]{0:T(512)}, u32[]{:S(2)}) copy-start(f32[512]{0:T(512)} %param.40) | copy-start | bytes 6148
  282.2 444.9 %reduce-scatter.14.cloned.1.call-start = ((), (), s32[]{:S(2)}) async-start(), calls=%async_computation.12 | async-start | bytes 28311552 | tf_op jit(solution)/shard_map/reduce_scatter | solution.py:336
  323.0 618.1 %reduce-scatter.16.cloned.1.call-start = ((), (), s32[]{:S(2)}) async-start(), calls=%async_computation.13 | async-start | bytes 28311552 | tf_op jit(solution)/shard_map/reduce_scatter | solution.py:337
  337.7 738.8 %all-gather.12.cloned.1.call-start = ((), (), s32[]{:S(2)}) async-start(), calls=%async_computation.16 | async-start | bytes 14155776 | tf_op jit(solution)/shard_map/all_gather | solution.py:79
  958.3 238.2 %all-gather.14.cloned.1.call-start = ((), (), s32[]{:S(2)}) async-start(), calls=%async_computation.17 | async-start | bytes 14155776 | tf_op jit(solution)/shard_map/all_gather | solution.py:79
  958.9 277.6 %all-reduce.16.cloned.1.call-start = ((), (), s32[]{:S(2)}) async-start(), calls=%async_computation.18 | async-start | bytes 8388608 | tf_op jit(solution)/shard_map/psum | solution.py:69
  1207.9 38.2 %copy-start.21 = (bf16[2048,512]{1,0:T(8,128)(2,1)S(1)}, bf16[2048,512]{1,0:T(8,128)(2,1)}, u32[]{:S(2)}) copy-start(bf16[2048,512]{1,0:T(8,128)(2,1)} %param.43) | copy-start | bytes 6291460
  1207.9 103.3 %reduce-scatter.20.cloned.1.call-start = ((), (), s32[]{:S(2)}) async-start(), calls=%async_computation.19 | async-start | bytes 6291456 | tf_op jit(solution)/shard_map/reduce_scatter | solution.py:73
  1246.1 6.1 copy-start.27
  1255.5 227.9 %all-gather.10.cloned.1.call-start = ((), (), s32[]{:S(2)}) async-start(), calls=%async_computation.14 | async-start | bytes 14155776 | tf_op jit(solution)/shard_map/all_gather | solution.py:344
  1255.6 60.5 %copy-start.7 = (f32[2048,2,2,64]{0,3,2,1:T(8,128)S(1)}, f32[2048,2,2,64]{0,3,2,1:T(8,128)}, u32[]{:S(2)}) copy-start(f32[2048,2,2,64]{0,3,2,1:T(8,128)} %get-tuple-element.1044) | copy-start | bytes 6291460
  1256.3 238.8 %all-gather.18.cloned.1.call-start = ((), (), s32[]{:S(2)}) async-start(), calls=%async_computation.21 | async-start | bytes 1572864 | tf_op jit(solution)/shard_map/all_gather | solution.py:79
  1321.4 148.1 %copy-start.13 = (f32[2048,32]{0,1:T(8,128)S(1)}, f32[2048,32]{0,1:T(8,128)}, u32[]{:S(2)}) copy-start(f32[2048,32]{0,1:T(8,128)} %copy-done.12) | copy-start | bytes 786436
  1321.4 148.1 %copy-start.15 = (f32[2048,32]{0,1:T(8,128)S(1)}, f32[2048,32]{0,1:T(8,128)}, u32[]{:S(2)}) copy-start(f32[2048,32]{0,1:T(8,128)} %copy-done.14) | copy-start | bytes 786436
  1321.4 149.5 %copy-start.37 = (f32[2048,2]{0,1:T(2,128)S(1)}, f32[2048,2]{0,1:T(2,128)}, u32[]{:S(2)}) copy-start(f32[2048,2]{0,1:T(2,128)} %copy-done.36) | copy-start | bytes 49156
  1321.4 149.5 %copy-start.50 = (f32[64]{0:T(128)S(1)}, f32[64]{0:T(128)}, u32[]{:S(2)}) copy-start(f32[64]{0:T(128)} %param.42) | copy-start | bytes 772
  1473.7 44.8 %all-gather.20.cloned.1.call-start = ((), (), s32[]{:S(2)}) async-start(), calls=%async_computation.22 | async-start | bytes 1572864 | tf_op jit(solution)/shard_map/all_gather | solution.py:79
  1479.2 74.3 %all-gather.16.cloned.1.call-start = ((), (), s32[]{:S(2)}) async-start(), calls=%async_computation.20 | async-start | bytes 3145728 | tf_op jit(solution)/shard_map/all_gather | solution.py:79
  1483.4 11.8 copy-start.39
  1483.4 119.9 %all-reduce.20.cloned.1.call-start = ((), (), s32[]{:S(2)}) async-start(), calls=%async_computation.24 | async-start | bytes 16777216 | tf_op jit(solution)/shard_map/psum | solution.py:65
  1493.0 25.4 %copy-start.40 = (bf16[512,256]{1,0:T(8,128)(2,1)S(1)}, bf16[512,256]{1,0:T(8,128)(2,1)}, u32[]{:S(2)}) copy-start(bf16[512,256]{1,0:T(8,128)(2,1)} %param.34) | copy-start | bytes 786436
  1499.1 54.4 %copy-start.29 = (bf16[512,512]{1,0:T(8,128)(2,1)S(1)}, bf16[512,512]{1,0:T(8,128)(2,1)}, u32[]{:S(2)}) copy-start(bf16[512,512]{1,0:T(8,128)(2,1)} %param.32) | copy-start | bytes 1572868
  1561.0 578.7 %all-reduce.18.cloned.1.call-start = ((), (), s32[]{:S(2)}) async-start(), calls=%async_computation.23 | async-start | bytes 34603008 | tf_op jit(solution)/shard_map/psum | solution.py:414
  1562.5 10.6 copy-start.25
  1562.5 22.1 %slice-start.2 = ((s8[9437184]{0:T(1024)(128)(4,1)}), s8[4194304]{0:T(1024)(128)(4,1)S(1)}, s32[]{:S(2)}) async-start(s8[9437184]{0:T(1024)(128)(4,1)} %bitcast.237), calls=%async_computation.27 | async-start | bytes 8388608
  1562.5 22.1 %slice-start.3 = ((s8[9437184]{0:T(1024)(128)(4,1)}), s8[4194304]{0:T(1024)(128)(4,1)S(1)}, s32[]{:S(2)}) async-start(s8[9437184]{0:T(1024)(128)(4,1)} %bitcast.237), calls=%async_computation.28 | async-start | bytes 8388608
  1573.1 11.6 copy-start.22
  1573.1 11.6 slice-start.4
  1584.7 6.8 copy-start.4
  1584.7 6.8 copy-start.18
  1600.7 10.5 copy-start.46
  1634.4 6.7 copy-start.9
  2139.6 8.4 copy-start.17
  2148.1 6.4 slice-start
  (27 other events, 82.6 us)
Sparse Core Ops, SparseCore 0:
  19.5 33.6 reduce-scatter.11
  56.1 31.8 reduce-scatter.9
  90.8 54.3 reduce-scatter.7
  231.2 33.1 all-gather.7
  269.5 28.4 all-reduce.13
  300.1 212.8 reduce-scatter.17
  515.3 211.7 reduce-scatter.13
  729.4 211.6 reduce-scatter.15
  958.4 117.9 all-gather.11
  1078.5 117.9 all-gather.13
  1208.0 28.4 all-reduce.15
  1255.7 55.4 reduce-scatter.19
  1313.3 117.9 all-gather.9
  1473.8 21.2 all-gather.17
  1497.1 21.2 all-gather.19
  1520.4 33.1 all-gather.15
  1561.1 38.8 all-reduce.19
  1606.8 532.8 all-reduce.17
where the time goes:
time: 2170 us; the launch traced here: 2160 us
  waiting for transfers between devices  1620 us (75%)
  matrix products  308 us (14%)
  other arithmetic  105 us (5%)
  local copies, waits for them, and re-layouts  63.3 us (3%)
  blocking collectives  46.6 us (2%)
    psum x1, waiting for transfers between devices, shards(): lax.psum((grad_query_w, grad_key_w, grad_value_w, grad_out_w, grad_gate_w...  496 us
    all_gather x5, waiting for transfers between devices, gather_grads(): lax.all_gather(for_sending(operand), 'row', axis=1, tiled=True)  279 us
    reduce_scatter x2, waiting for transfers between devices, scatter_back(): return lax.psum_scatter(operand, 'row', scatter_dimension=1, tiled=True)  230 us
    reduce_scatter x1, waiting for transfers between devices, shards(): lax.psum_scatter(gate_part, 'row', scatter_dimension=1, tiled=True)  214 us
    reduce_scatter x1, waiting for transfers between devices, shards(): lax.psum_scatter(up_part, 'row', scatter_dimension=1, tiled=True)  214 us
    dot_general x10, matrix products, update(): jnp.einsum('kgij,ikgd->jkd', grad_scores, query_wide, precision=lax.Preci...  58.5 us
    reduce_scatter x1, waiting for transfers between devices, shards(): lax.psum_scatter(query_part, 'row', scatter_dimension=1, tiled=True)  54.2 us
    dot_general x7, matrix products, times_transpose(): lax.dot_general(left_side, right_side, (((1,), (1,)), ((), ())), preferre...  53.2 us
  transfers between devices with their start and end apart: 18, of which 16 were waited for; matrix products, arithmetic and copies ran while one was open for 14% of the time, Pallas kernels for 0%

commit v1 on v0

--- a/solution.py
+++ b/solution.py
@@ -23,7 +23,8 @@
 
 
 def layout(lengths, packed_length):
-    seq_ends = jnp.cumsum(lengths)
+    numbers = jnp.arange(lengths.shape[0], dtype=jnp.int32)
+    seq_ends = jnp.sum(jnp.where(numbers[None, :] <= numbers[:, None], lengths[None, :], 0), axis=1)
     starts = seq_ends - lengths
     places = jnp.arange(packed_length, dtype=jnp.int32)
     member = jnp.sum((places[:, None] >= seq_ends[None, :]).astype(jnp.int32), axis=1)

time: 2170 us -> 2170 us (level)
  no operation moved by 1% of the time
where the time goes in v1:
time: 2170 us; the launch traced here: 2160 us
  waiting for transfers between devices  1620 us (75%)
  matrix products  308 us (14%)
  other arithmetic  105 us (5%)
  local copies, waits for them, and re-layouts  63.2 us (3%)
  blocking collectives  46.6 us (2%)
    psum x1, waiting for transfers between devices, shards(): lax.psum((grad_query_w, grad_key_w, grad_value_w, grad_out_w, grad_gate_w...  496 us
    all_gather x5, waiting for transfers between devices, gather_grads(): lax.all_gather(for_sending(operand), 'row', axis=1, tiled=True)  279 us
    reduce_scatter x2, waiting for transfers between devices, scatter_back(): return lax.psum_scatter(operand, 'row', scatter_dimension=1, tiled=True)  230 us
    reduce_scatter x1, waiting for transfers between devices, shards(): lax.psum_scatter(gate_part, 'row', scatter_dimension=1, tiled=True)  214 us
    reduce_scatter x1, waiting for transfers between devices, shards(): lax.psum_scatter(up_part, 'row', scatter_dimension=1, tiled=True)  214 us
    dot_general x10, matrix products, update(): jnp.einsum('kgij,ikgd->jkd', grad_scores, query_wide, precision=lax.Preci...  58.5 us
    reduce_scatter x1, waiting for transfers between devices, shards(): lax.psum_scatter(query_part, 'row', scatter_dimension=1, tiled=True)  54.2 us
    dot_general x7, matrix products, times_transpose(): lax.dot_general(left_side, right_side, (((1,), (1,)), ((), ())), preferre...  53.2 us
  transfers between devices with their start and end apart: 18, of which 16 were waited for; matrix products, arithmetic and copies ran while one was open for 14% of the time, Pallas kernels for 0%

profile of v1, /device:TPU:0, one launch (start us, length us, event | category | flops | bytes accessed | tf_op | source)
XLA Modules:
  0.0 2164.0 jit_solution(7812021034418014256)
XLA Ops:
  30.6 22.6 %reduce-scatter.12.cloned.1.call-done = f32[2048,1,128]{0,2,1:T(8,128)} async-done(((f32[2048,2,128]{0,2,1:T(8,128)}), f32[2048,1,128]{0,2,1:T(8,128)}) %reduce-scatter.12.cloned.1.call-update) | async-done | bytes 1048592 | tf_op jit(solution)/shard_map/reduce_scatter | solution.py:307
  55.3 32.7 %reduce-scatter.10.cloned.1.call-done = f32[2048,1,128]{0,2,1:T(8,128)} async-done(((f32[2048,2,128]{0,2,1:T(8,128)}), f32[2048,1,128]{0,2,1:T(8,128)}) %reduce-scatter.10.cloned.1.call-update) | async-done | bytes 1048592 | tf_op jit(solution)/shard_map/reduce_scatter | solution.py:306
  91.0 54.2 %reduce-scatter.8.cloned.1.call-done = f32[2048,1,256]{0,2,1:T(8,128)} async-done(((f32[2048,2,256]{0,2,1:T(8,128)}), f32[2048,1,256]{0,2,1:T(8,128)}) %reduce-scatter.8.cloned.1.call-update) | async-done | bytes 2097168 | tf_op jit(solution)/shard_map/reduce_scatter | solution.py:305
  153.1 75.2 %while.126 = (s32[]{:T(128)}, f32[2048,2,2,64]{0,3,2,1:T(8,128)}, f32[2,2,2048]{2,1,0:T(2,128)S(1)}, bf16[2048,2,2,64]{0,3,2,1:T(8,128)(2,1)}, s32[2048]{0:T(102...) while((s32[]{:T(128)}, f32[2048,2,2,64]{0,3,2,1:T(8,128)}, ...), condition=%wide.region_21.22_spmd, body=%wide.region_10.21_spmd.sunk | while | flops 416948224 | bytes 13969349 | solution.py:193
  169.8 7.2 while.130
  179.8 7.3 while.129
  188.0 10.7 while.130
  201.6 9.7 while.129
  212.2 14.3 while.130
  231.4 33.0 %all-gather.8.cloned.1.call-done = bf16[2048,512]{0,1:T(8,128)(2,1)} async-done(((bf16[2048,256]{0,1:T(8,128)(2,1)}), bf16[2048,512]{0,1:T(8,128)(2,1)}) %all-gather.8.cloned.1.call-update) | async-done | bytes 2097168 | tf_op jit(solution)/shard_map/all_gather | solution.py:324
  269.4 12.7 fusion.107
  282.3 15.7 all-reduce.14.cloned.1.call-done
  316.2 6.8 copy.79
  323.3 7.5 fusion.105
  330.8 6.9 copy.78
  337.7 175.3 %reduce-scatter.18.cloned.1.call-done = f32[2048,1152]{1,0:T(8,128)} async-done(((f32[2048,2304]{1,0:T(8,128)}), f32[2048,1152]{1,0:T(8,128)}) %reduce-scatter.18.cloned.1.call-update) | async-done | bytes 9437200 | tf_op jit(solution)/shard_map/reduce_scatter | solution.py:74
  513.0 214.1 %reduce-scatter.14.cloned.1.call-done = f32[2048,1,1152]{2,0,1:T(8,128)} async-done(((f32[2048,2,1152]{2,0,1:T(8,128)}), f32[2048,1,1152]{2,0,1:T(8,128)}) %reduce-scatter.14.cloned.1.call-update) | async-done | bytes 9437200 | tf_op jit(solution)/shard_map/reduce_scatter | solution.py:337
  727.1 214.0 %reduce-scatter.16.cloned.1.call-done = f32[2048,1,1152]{2,0,1:T(8,128)} async-done(((f32[2048,2,1152]{2,0,1:T(8,128)}), f32[2048,1,1152]{2,0,1:T(8,128)}) %reduce-scatter.16.cloned.1.call-update) | async-done | bytes 9437200 | tf_op jit(solution)/shard_map/reduce_scatter | solution.py:338
  941.1 17.2 multiply_convert_fusion
  959.4 117.0 %all-gather.12.cloned.1.call-done = bf16[2048,2304]{1,0:T(8,128)(2,1)} async-done(((bf16[2048,1152]{1,0:T(8,128)(2,1)}), bf16[2048,2304]{1,0:T(8,128)(2,1)}) %all-gather.12.cloned.1.call-update) | async-done | bytes 9437200 | tf_op jit(solution)/shard_map/all_gather | solution.py:80
  1076.5 10.4 fusion.108
  1086.8 109.7 %all-gather.14.cloned.1.call-done = bf16[2048,2304]{1,0:T(8,128)(2,1)} async-done(((bf16[2048,1152]{1,0:T(8,128)(2,1)}), bf16[2048,2304]{1,0:T(8,128)(2,1)}) %all-gather.14.cloned.1.call-update) | async-done | bytes 9437200 | tf_op jit(solution)/shard_map/all_gather | solution.py:80
  1196.5 11.4 convolution_add_fusion
  1207.9 28.5 %all-reduce.16.cloned.1.call-done = f32[2048,512]{1,0:T(8,128)} async-done(((f32[2048,512]{1,0:T(8,128)}), f32[2048,512]{1,0:T(8,128)}) %all-reduce.16.cloned.1.call-update) | async-done | bytes 4194320 | tf_op jit(solution)/shard_map/psum | solution.py:70
  1256.5 54.7 %reduce-scatter.20.cloned.1.call-done = f32[2048,256]{1,0:T(8,128)} async-done(((f32[2048,512]{1,0:T(8,128)}), f32[2048,256]{1,0:T(8,128)}) %reduce-scatter.20.cloned.1.call-update) | async-done | bytes 2097168 | tf_op jit(solution)/shard_map/reduce_scatter | solution.py:74
  1321.4 148.0 %while.128 = (s32[]{:T(128)}, f32[2048,2,2,64]{0,3,2,1:T(8,128)}, f32[2048,2,64]{0,2,1:T(8,128)}, f32[2048,2,64]{0,2,1:T(8,128)}, bf16[2048,2,2,64]{0,3,2,1:T(8,...) while((s32[]{:T(128)}, f32[2048,2,2,64]{0,3,2,1:T(8,128)}, ...), condition=%wide.region_38.39_spmd, body=%wide.region_33.38_spmd.sunk | while | flops 2024080384 | bytes 32977676 | solution.py:268
  1322.8 14.1 while.131
  1322.8 14.0 conditional.6
  1338.9 28.0 %while.131 = (s32[]{:T(128)}, f32[512,2,2,64]{0,3,2,1:T(8,128)S(1)}, f32[2048,2,64]{0,2,1:T(8,128)}, f32[2048,2,64]{0,2,1:T(8,128)}, s32[]{:T(128)}, /*index=5*/...) while((s32[]{:T(128)}, f32[512,2,2,64]{0,3,2,1:T(8,128)S(1)}, ...), condition=%wide.region_37.37_spmd, body=%wide.region_34.36_spmd.sunk | while | flops 2023949312 | bytes 29798832 | solution.py:259
  1338.9 14.0 conditional.6
  1352.9 13.9 conditional.6
  1368.9 41.9 %while.131 = (s32[]{:T(128)}, f32[512,2,2,64]{0,3,2,1:T(8,128)S(1)}, f32[2048,2,64]{0,2,1:T(8,128)}, f32[2048,2,64]{0,2,1:T(8,128)}, s32[]{:T(128)}, /*index=5*/...) while((s32[]{:T(128)}, f32[512,2,2,64]{0,3,2,1:T(8,128)S(1)}, ...), condition=%wide.region_37.37_spmd, body=%wide.region_34.36_spmd.sunk | while | flops 2023949312 | bytes 29798832 | solution.py:259
  1368.9 14.0 conditional.6
  1382.9 13.9 conditional.6
  1396.8 13.9 conditional.6
  1412.8 55.8 %while.131 = (s32[]{:T(128)}, f32[512,2,2,64]{0,3,2,1:T(8,128)S(1)}, f32[2048,2,64]{0,2,1:T(8,128)}, f32[2048,2,64]{0,2,1:T(8,128)}, s32[]{:T(128)}, /*index=5*/...) while((s32[]{:T(128)}, f32[512,2,2,64]{0,3,2,1:T(8,128)S(1)}, ...), condition=%wide.region_37.37_spmd, body=%wide.region_34.36_spmd.sunk | while | flops 2023949312 | bytes 29798832 | solution.py:259
  1412.8 14.0 conditional.6
  1426.8 13.9 conditional.6
  1440.7 13.9 conditional.6
  1454.7 13.9 conditional.6
  1483.4 9.6 fusion.106
  1499.1 19.3 all-gather.20.cloned.1.call-done
  1522.4 31.1 %all-gather.16.cloned.1.call-done = bf16[2048,512]{0,1:T(8,128)(2,1)} async-done(((bf16[2048,256]{0,1:T(8,128)(2,1)}), bf16[2048,512]{0,1:T(8,128)(2,1)}) %all-gather.16.cloned.1.call-update) | async-done | bytes 2097168 | tf_op jit(solution)/shard_map/all_gather | solution.py:80
  1553.6 7.4 add_add_fusion
  1562.5 10.5 fusion.111
  1573.1 11.6 fusion.112
  1611.2 23.2 %all-reduce.4 = (f32[512]{0:T(512)}, f32[512]{0:T(512)}, f32[64]{0:T(128)}, f32[64]{0:T(128)}) all-reduce(f32[512]{0:T(512)S(1)} %get-tuple-element.1092, f32[512]{0:T(512)S(1)} %copy-done.46, f32[64]{0:T(128)S(1)} %get-tuple-element.1212, f32[64]{0:T(128)S(1)} %get-tuple-element.1213), channel_id=1, replica_groups=mesh['dp'=8,'row'=2,'col'=2] {'dp'}, use_global_device_ids=true, to_apply=%region_52.53 | all-reduce | flops 1152 | bytes 9216 | tf_op jit(solution)/shard_map/psum | solution.py:415
  1643.4 496.3 %all-reduce.18.cloned.1.call-done = (f32[512,512]{1,0:T(8,128)}, f32[512,256]{1,0:T(8,128)}, f32[512,256]{1,0:T(8,128)}, f32[512,512]{1,0:T(8,128)}, f32[512,230...) async-done(((f32[512,512]{1,0:T(8,128)}, f32[512,256]{1,0:T(8,128)}, f32[512,256]{1,0:T(8,128)}, f32[512,512]{1,0:T(8,128)}, f32[512,2304]{1,0:T(8,128)}, ...) | async-done | bytes 17301520 | tf_op jit(solution)/shard_map/psum | solution.py:415
  (509 shorter events, 464.2 us)
Async XLA Ops:
  7.2 303.9 %copy-start = (bf16[512,2304]{1,0:T(8,128)(2,1)S(1)}, bf16[512,2304]{1,0:T(8,128)(2,1)}, u32[]{:S(2)}) copy-start(bf16[512,2304]{1,0:T(8,128)(2,1)} %param.36) | copy-start | bytes 7077892
  7.2 12.3 copy-start.43
  7.2 12.3 copy-start.38
  7.2 46.0 %reduce-scatter.12.cloned.1.call-start = ((), (), s32[]{:S(2)}) async-start(), calls=%async_computation.9 | async-start | bytes 3145728 | tf_op jit(solution)/shard_map/reduce_scatter | solution.py:307
  15.4 8.1 copy-start.34
  19.4 68.5 %reduce-scatter.10.cloned.1.call-start = ((), (), s32[]{:S(2)}) async-start(), calls=%async_computation.8 | async-start | bytes 3145728 | tf_op jit(solution)/shard_map/reduce_scatter | solution.py:306
  23.5 121.7 %reduce-scatter.8.cloned.1.call-start = ((), (), s32[]{:S(2)}) async-start(), calls=%async_computation.7 | async-start | bytes 6291456 | tf_op jit(solution)/shard_map/reduce_scatter | solution.py:305
  28.6 60.7 %copy-start.49 = (f32[64]{0:T(128)S(1)}, f32[64]{0:T(128)}, u32[]{:S(2)}) copy-start(f32[64]{0:T(128)} %param.42) | copy-start | bytes 772
  28.6 235.7 %all-gather.8.cloned.1.call-start = ((), (), s32[]{:S(2)}) async-start(), calls=%async_computation.10 | async-start | bytes 3145728 | tf_op jit(solution)/shard_map/all_gather | solution.py:324
  30.6 119.6 %copy-start.12 = (f32[2048,32]{0,1:T(8,128)}, f32[2048,32]{0,1:T(8,128)S(1)}, u32[]{:S(2)}) copy-start(f32[2048,32]{0,1:T(8,128)S(1)} %get-tuple-element.1245) | copy-start | bytes 786436
  30.6 119.6 %copy-start.14 = (f32[2048,32]{0,1:T(8,128)}, f32[2048,32]{0,1:T(8,128)S(1)}, u32[]{:S(2)}) copy-start(f32[2048,32]{0,1:T(8,128)S(1)} %get-tuple-element.1246) | copy-start | bytes 786436
  87.9 60.3 %copy-start.47 = (f32[64]{0:T(128)S(1)}, f32[64]{0:T(128)}, u32[]{:S(2)}) copy-start(f32[64]{0:T(128)} %param.41) | copy-start | bytes 772
  231.1 66.9 %all-reduce.14.cloned.1.call-start = ((), (), s32[]{:S(2)}) async-start(), calls=%async_computation.11 | async-start | bytes 8388608 | tf_op jit(solution)/shard_map/psum | solution.py:66
  269.4 243.6 %reduce-scatter.18.cloned.1.call-start = ((), (), s32[]{:S(2)}) async-start(), calls=%async_computation.15 | async-start | bytes 28311552 | tf_op jit(solution)/shard_map/reduce_scatter | solution.py:74
  282.2 26.2 %copy-start.45 = (f32[512]{0:T(512)S(1)}, f32[512]{0:T(512)}, u32[]{:S(2)}) copy-start(f32[512]{0:T(512)} %param.40) | copy-start | bytes 6148
  282.2 444.9 %reduce-scatter.14.cloned.1.call-start = ((), (), s32[]{:S(2)}) async-start(), calls=%async_computation.12 | async-start | bytes 28311552 | tf_op jit(solution)/shard_map/reduce_scatter | solution.py:337
  323.0 618.1 %reduce-scatter.16.cloned.1.call-start = ((), (), s32[]{:S(2)}) async-start(), calls=%async_computation.13 | async-start | bytes 28311552 | tf_op jit(solution)/shard_map/reduce_scatter | solution.py:338
  337.7 738.8 %all-gather.12.cloned.1.call-start = ((), (), s32[]{:S(2)}) async-start(), calls=%async_computation.16 | async-start | bytes 14155776 | tf_op jit(solution)/shard_map/all_gather | solution.py:80
  958.3 238.2 %all-gather.14.cloned.1.call-start = ((), (), s32[]{:S(2)}) async-start(), calls=%async_computation.17 | async-start | bytes 14155776 | tf_op jit(solution)/shard_map/all_gather | solution.py:80
  958.9 277.6 %all-reduce.16.cloned.1.call-start = ((), (), s32[]{:S(2)}) async-start(), calls=%async_computation.18 | async-start | bytes 8388608 | tf_op jit(solution)/shard_map/psum | solution.py:70
  1207.9 38.2 %copy-start.21 = (bf16[2048,512]{1,0:T(8,128)(2,1)S(1)}, bf16[2048,512]{1,0:T(8,128)(2,1)}, u32[]{:S(2)}) copy-start(bf16[2048,512]{1,0:T(8,128)(2,1)} %param.43) | copy-start | bytes 6291460
  1207.9 103.3 %reduce-scatter.20.cloned.1.call-start = ((), (), s32[]{:S(2)}) async-start(), calls=%async_computation.19 | async-start | bytes 6291456 | tf_op jit(solution)/shard_map/reduce_scatter | solution.py:74
  1246.1 6.1 copy-start.27
  1255.5 227.9 %all-gather.10.cloned.1.call-start = ((), (), s32[]{:S(2)}) async-start(), calls=%async_computation.14 | async-start | bytes 14155776 | tf_op jit(solution)/shard_map/all_gather | solution.py:345
  1255.6 60.5 %copy-start.7 = (f32[2048,2,2,64]{0,3,2,1:T(8,128)S(1)}, f32[2048,2,2,64]{0,3,2,1:T(8,128)}, u32[]{:S(2)}) copy-start(f32[2048,2,2,64]{0,3,2,1:T(8,128)} %get-tuple-element.1044) | copy-start | bytes 6291460
  1256.3 238.8 %all-gather.18.cloned.1.call-start = ((), (), s32[]{:S(2)}) async-start(), calls=%async_computation.21 | async-start | bytes 1572864 | tf_op jit(solution)/shard_map/all_gather | solution.py:80
  1321.4 148.1 %copy-start.13 = (f32[2048,32]{0,1:T(8,128)S(1)}, f32[2048,32]{0,1:T(8,128)}, u32[]{:S(2)}) copy-start(f32[2048,32]{0,1:T(8,128)} %copy-done.12) | copy-start | bytes 786436
  1321.4 148.1 %copy-start.15 = (f32[2048,32]{0,1:T(8,128)S(1)}, f32[2048,32]{0,1:T(8,128)}, u32[]{:S(2)}) copy-start(f32[2048,32]{0,1:T(8,128)} %copy-done.14) | copy-start | bytes 786436
  1321.4 149.5 %copy-start.37 = (f32[2048,2]{0,1:T(2,128)S(1)}, f32[2048,2]{0,1:T(2,128)}, u32[]{:S(2)}) copy-start(f32[2048,2]{0,1:T(2,128)} %copy-done.36) | copy-start | bytes 49156
  1321.4 149.5 %copy-start.50 = (f32[64]{0:T(128)S(1)}, f32[64]{0:T(128)}, u32[]{:S(2)}) copy-start(f32[64]{0:T(128)} %param.42) | copy-start | bytes 772
  1473.7 44.8 %all-gather.20.cloned.1.call-start = ((), (), s32[]{:S(2)}) async-start(), calls=%async_computation.22 | async-start | bytes 1572864 | tf_op jit(solution)/shard_map/all_gather | solution.py:80
  1479.2 74.3 %all-gather.16.cloned.1.call-start = ((), (), s32[]{:S(2)}) async-start(), calls=%async_computation.20 | async-start | bytes 3145728 | tf_op jit(solution)/shard_map/all_gather | solution.py:80
  1483.4 11.8 copy-start.39
  1483.4 119.9 %all-reduce.20.cloned.1.call-start = ((), (), s32[]{:S(2)}) async-start(), calls=%async_computation.24 | async-start | bytes 16777216 | tf_op jit(solution)/shard_map/psum | solution.py:66
  1493.0 25.4 %copy-start.40 = (bf16[512,256]{1,0:T(8,128)(2,1)S(1)}, bf16[512,256]{1,0:T(8,128)(2,1)}, u32[]{:S(2)}) copy-start(bf16[512,256]{1,0:T(8,128)(2,1)} %param.34) | copy-start | bytes 786436
  1499.1 54.4 %copy-start.29 = (bf16[512,512]{1,0:T(8,128)(2,1)S(1)}, bf16[512,512]{1,0:T(8,128)(2,1)}, u32[]{:S(2)}) copy-start(bf16[512,512]{1,0:T(8,128)(2,1)} %param.32) | copy-start | bytes 1572868
  1561.0 578.7 %all-reduce.18.cloned.1.call-start = ((), (), s32[]{:S(2)}) async-start(), calls=%async_computation.23 | async-start | bytes 34603008 | tf_op jit(solution)/shard_map/psum | solution.py:415
  1562.5 10.6 copy-start.25
  1562.5 22.1 %slice-start.2 = ((s8[9437184]{0:T(1024)(128)(4,1)}), s8[4194304]{0:T(1024)(128)(4,1)S(1)}, s32[]{:S(2)}) async-start(s8[9437184]{0:T(1024)(128)(4,1)} %bitcast.235), calls=%async_computation.27 | async-start | bytes 8388608
  1562.5 22.1 %slice-start.3 = ((s8[9437184]{0:T(1024)(128)(4,1)}), s8[4194304]{0:T(1024)(128)(4,1)S(1)}, s32[]{:S(2)}) async-start(s8[9437184]{0:T(1024)(128)(4,1)} %bitcast.235), calls=%async_computation.28 | async-start | bytes 8388608
  1573.1 11.6 copy-start.22
  1573.1 11.6 slice-start.4
  1584.7 6.8 copy-start.4
  1584.7 6.8 copy-start.18
  1600.7 10.5 copy-start.46
  1634.4 6.7 copy-start.9
  2139.6 8.4 copy-start.17
  2148.1 6.4 slice-start
  (27 other events, 82.6 us)
Sparse Core Ops, SparseCore 0:
  19.5 33.6 reduce-scatter.11
  56.1 31.8 reduce-scatter.9
  90.8 54.3 reduce-scatter.7
  231.2 33.1 all-gather.7
  269.5 28.4 all-reduce.13
  300.1 212.8 reduce-scatter.17
  515.3 211.7 reduce-scatter.13
  729.4 211.6 reduce-scatter.15
  958.4 117.9 all-gather.11
  1078.5 117.9 all-gather.13
  1208.0 28.4 all-reduce.15
  1255.7 55.4 reduce-scatter.19
  1313.3 117.9 all-gather.9
  1473.8 21.2 all-gather.17
  1497.1 21.2 all-gather.19
  1520.4 33.1 all-gather.15
  1561.1 38.8 all-reduce.19
  1606.8 532.8 all-reduce.17

commit v2 on v0

v2 whole, which is shorter than its diff:
```python
import functools
import math

import jax
import jax.numpy as jnp
from jax import lax
from jax.experimental import pallas as pl
from jax.experimental.pallas import tpu as pltpu
from jax.sharding import PartitionSpec as P

HEAD_SIZE = 64
EPSILON = 1e-05
ROPE_BASE = 1000000.0
F32, BF16 = jnp.float32, jnp.bfloat16


def dot(a, b, dims=(((1,), (0,)), ((), ()))):
    return lax.dot_general(a, b, dims, preferred_element_type=F32)


NT = (((1,), (1,)), ((), ()))

def stacked(x):
    first = lax.broadcasted_iota(jnp.int32, x.shape, 1) < 64
    zero = jnp.zeros_like(x)
    return jnp.concatenate([jnp.where(first, x, zero), jnp.where(first, zero, x)], axis=0)

def attend_kernel(bq, bk, first_ref, last_ref, q_ref, k_ref, v_ref, start_ref, low_ref, raw_ref, lse_ref, acc_ref, mass_ref):
    i = pl.program_id(1)
    qs = stacked(q_ref[...])
    starts = start_ref[...]
    starts = jnp.concatenate([starts, starts], axis=0)
    acc_ref[...] = jnp.zeros_like(acc_ref)
    mass_ref[...] = jnp.zeros_like(mass_ref)
    rows = i * bq + lax.rem(lax.broadcasted_iota(jnp.int32, (2 * bq, 1), 0), bq)

    def step(j, masked):
        k0 = pl.multiple_of(j * bk, bk)
        s = dot(qs, k_ref[pl.ds(k0, bk), :], NT)
        p = jnp.exp(s)
        if masked:
            cols = j * bk + lax.broadcasted_iota(jnp.int32, (1, bk), 1)
            p = jnp.where((cols <= rows) & (cols >= starts), p, 0.0)
        mass = p[:, :128]
        for n in range(1, bk // 128):
            mass = mass + p[:, n * 128:(n + 1) * 128]
        mass_ref[...] += mass
        acc_ref[...] += dot(p.astype(BF16), v_ref[pl.ds(k0, bk), :])

    low = first_ref[i] // bk
    clear = jnp.maximum((last_ref[i] + bk - 1) // bk, low)
    diagonal = (i * bq) // bk
    end = ((i + 1) * bq + bk - 1) // bk
    clear = jnp.minimum(clear, diagonal)

    @pl.loop(low, clear)
    def _(j):
        step(j, True)

    @pl.loop(clear, diagonal)
    def _(j):
        step(j, False)

    @pl.loop(diagonal, end)
    def _(j):
        step(j, True)

    mass = jnp.sum(mass_ref[...], axis=1, keepdims=True)
    out = acc_ref[...] / mass
    first = lax.broadcasted_iota(jnp.int32, (bq, 128), 1) < 64
    out = jnp.where(first, out[:bq], out[bq:])
    raw_ref[...] = out
    low_ref[...] = out.astype(BF16)
    total = jnp.log(jnp.sum(mass_ref[...].T, axis=0, keepdims=True))
    lse_ref[0, 0:1, :] = total[:, :bq]
    lse_ref[0, 1:2, :] = total[:, bq:]

def attend(q, k, v, starts, bq=512, bk=512):
    T, width = q.shape
    groups = width // 128
    first, last = starts[::bq], starts[bq - 1::bq]
    kern = functools.partial(attend_kernel, bq, bk)
    pairs = T * (T + bk) // 2
    return pl.pallas_call(
        kern,
        out_shape=(jax.ShapeDtypeStruct((T, width), BF16), jax.ShapeDtypeStruct((T, width), F32),
                   jax.ShapeDtypeStruct((groups, 2, T), F32)),
        grid_spec=pltpu.PrefetchScalarGridSpec(
            num_scalar_prefetch=2, grid=(groups, T // bq),
            in_specs=[
                pl.BlockSpec((bq, 128), lambda g, i, *_: (i, g)),
                pl.BlockSpec((T, 128), lambda g, i, *_: (0, g)),
                pl.BlockSpec((T, 128), lambda g, i, *_: (0, g)),
                pl.BlockSpec((bq, 1), lambda g, i, *_: (i, 0)),
            ],
            out_specs=[
                pl.BlockSpec((bq, 128), lambda g, i, *_: (i, g)),
                pl.BlockSpec((bq, 128), lambda g, i, *_: (i, g)),
                pl.BlockSpec((1, 2, bq), lambda g, i, *_: (g, 0, i)),
            ],
            scratch_shapes=[pltpu.VMEM((2 * bq, 128), F32), pltpu.VMEM((2 * bq, 128), F32)],
        ),
        compiler_params=pltpu.CompilerParams(vmem_limit_bytes=40 << 20),
        cost_estimate=pl.CostEstimate(flops=4 * groups * 2 * pairs * 256, transcendentals=2 * groups * pairs,
                                      bytes_accessed=10 * T * width),
        name="attend",
    )(first, last, q, k, v, starts[:, None])

def attend_back_kernel(b, T, first_ref, last_ref, q_ref, k_ref, v_ref, grad_ref, raw_ref, lse_ref, start_ref,
                       dq_ref, dk_ref, dv_ref, qs_ref, gs_ref, stat_ref, dqt_ref, dk_acc, dv_acc):
    j = pl.program_id(1)
    blocks = T // b

    @pl.when(j == 0)
    def _():
        dqt_ref[...] = jnp.zeros_like(dqt_ref)
        for i in range(blocks):
            rows = slice(i * b, (i + 1) * b)
            both = slice(i * 2 * b, (i + 1) * 2 * b)
            qs_ref[both, :] = stacked(q_ref[rows, :])
            grad = grad_ref[rows, :]
            gs_ref[both, :] = stacked(grad)
            prod = (grad.astype(F32) * raw_ref[rows, :]).T
            stat_ref[i, 0:1, 0:b] = lse_ref[0, 0:1, rows]
            stat_ref[i, 0:1, b:2 * b] = lse_ref[0, 1:2, rows]
            stat_ref[i, 1:2, 0:b] = jnp.sum(prod[:64], axis=0, keepdims=True)
            stat_ref[i, 1:2, b:2 * b] = jnp.sum(prod[64:], axis=0, keepdims=True)

    k = k_ref[...]
    v = v_ref[...]
    kt = k.T[:64]
    dk_acc[...] = jnp.zeros_like(dk_acc)
    dv_acc[...] = jnp.zeros_like(dv_acc)
    keys = j * b + lax.broadcasted_iota(jnp.int32, (b, 1), 0)

    def step(i, masked):
        at = pl.ds(pl.multiple_of(i * 2 * b, 2 * b), 2 * b)
        qs = qs_ref[at, :]
        gs = gs_ref[at, :]
        st = dot(k, qs, NT)
        pt = jnp.exp(st - stat_ref[i, 0:1, :])
        if masked:
            cols = i * b + lax.rem(lax.broadcasted_iota(jnp.int32, (1, 2 * b), 1), b)
            begin = start_ref[0:1, pl.ds(pl.multiple_of(i * b, b), b)]
            begin = jnp.concatenate([begin, begin], axis=1)
            pt = jnp.where((keys <= cols) & (keys >= begin), pt, 0.0)
        dv_acc[...] += dot(pt.astype(BF16), gs)
        dpt = dot(v, gs, NT)
        dst = (pt * (dpt - stat_ref[i, 1:2, :])).astype(BF16)
        dk_acc[...] += dot(dst, qs)
        part = dot(kt, dst)
        to = pl.ds(pl.multiple_of(i * b, b), b)
        dqt_ref[0:64, to] += part[:, :b]
        dqt_ref[64:128, to] += part[:, b:]

    step(j, True)

    @pl.loop(j + 1, blocks)
    def _(i):
        whole = last_ref[i] <= j * b
        none = first_ref[i] >= (j + 1) * b

        @pl.when(whole)
        def _():
            step(i, False)

        @pl.when(jnp.logical_not(whole | none))
        def _():
            step(i, True)

    dk = dk_acc[...]
    dv = dv_acc[...]
    dk_ref[...] = dk + pltpu.roll(dk, 64, 1)
    dv_ref[...] = dv + pltpu.roll(dv, 64, 1)
    dq_ref[...] = dqt_ref[:, pl.ds(pl.multiple_of(j * b, b), b)].T * 0.125

def attend_back(q, k, v, grad, raw, lse, starts, b=512):
    T, width = q.shape
    groups = width // 128
    first, last = starts[::b], starts[b - 1::b]
    blocks = T // b
    col = pl.BlockSpec((T, 128), lambda g, j, *_: (0, g))
    blk = pl.BlockSpec((b, 128), lambda g, j, *_: (j, g))
    out = jax.ShapeDtypeStruct((T, width), F32)
    pairs = T * (T + b) // 2
    return pl.pallas_call(
        functools.partial(attend_back_kernel, b, T),
        out_shape=(out, out, out),
        grid_spec=pltpu.PrefetchScalarGridSpec(
            num_scalar_prefetch=2, grid=(groups, blocks),
            in_specs=[col, blk, blk, col, col,
                      pl.BlockSpec((1, 2, T), lambda g, j, *_: (g, 0, 0)),
                      pl.BlockSpec((1, T), lambda g, j, *_: (0, 0))],
            out_specs=[blk, blk, blk],
            scratch_shapes=[pltpu.VMEM((2 * T, 128), BF16), pltpu.VMEM((2 * T, 128), BF16),
                            pltpu.VMEM((blocks, 2, 2 * b), F32), pltpu.VMEM((128, T), F32),
                            pltpu.VMEM((b, 128), F32), pltpu.VMEM((b, 128), F32)],
        ),
        compiler_params=pltpu.CompilerParams(vmem_limit_bytes=48 << 20),
        cost_estimate=pl.CostEstimate(flops=10 * groups * 2 * pairs * 256, transcendentals=2 * groups * pairs,
                                      bytes_accessed=20 * T * width),
        name="attend_back",
    )(first, last, q, k, v, grad, raw, lse, starts[None, :])


def head_sums(x):
    first = lax.broadcasted_iota(jnp.int32, x.shape, 1) < HEAD_SIZE
    one = jnp.sum(jnp.where(first, x, 0.0), axis=1, keepdims=True)
    two = jnp.sum(jnp.where(first, 0.0, x), axis=1, keepdims=True)
    return jnp.where(first, one, two)


def swapped(x):
    low = lax.rem(lax.broadcasted_iota(jnp.int32, x.shape, 1), HEAD_SIZE) < HEAD_SIZE // 2
    return jnp.where(low, pltpu.roll(x, 96, 1), pltpu.roll(x, 32, 1))


def doubled(x):
    first = lax.broadcasted_iota(jnp.int32, x.shape, 1) < HEAD_SIZE
    other = pltpu.roll(x, HEAD_SIZE, 1)
    return jnp.where(first, x, other), jnp.where(first, other, x)


def project_kernel(groups, near_ref, far_ref, gain_near_ref, gain_far_ref, w_near_ref, w_far_ref, q_gain_ref, k_gain_ref,
                   cos_ref, sin_ref, hid_near_ref, hid_far_ref, raw_ref, q_ref, k_ref, v_ref):
    near = near_ref[...].astype(F32)
    far = far_ref[...].astype(F32)
    width = near.shape[1] + far.shape[1]
    total = jnp.sum(near * near, axis=1, keepdims=True) + jnp.sum(far * far, axis=1, keepdims=True)
    inverse = lax.rsqrt(total / width + EPSILON)
    hid_near = (near * inverse * gain_near_ref[...]).astype(BF16)
    hid_far = (far * inverse * gain_far_ref[...]).astype(BF16)
    hid_near_ref[...] = hid_near
    hid_far_ref[...] = hid_far
    raw = dot(hid_near, w_near_ref[...]) + dot(hid_far, w_far_ref[...])
    cosine, sine = cos_ref[...], sin_ref[...]

    def prepared(x, gain):
        normed = x * lax.rsqrt(head_sums(x * x) / HEAD_SIZE + EPSILON) * gain
        return normed * cosine + swapped(normed) * sine

    lanes = 2 * HEAD_SIZE
    kv = groups * HEAD_SIZE
    raw_ref[...] = raw[:, :groups * lanes + kv]
    for n in range(groups):
        cut = slice(n * lanes, (n + 1) * lanes)
        q_ref[:, cut] = (prepared(raw[:, cut], q_gain_ref[...]).astype(BF16) * HEAD_SIZE ** (-0.5)).astype(BF16)
    for n in range(groups // 2):
        at = groups * lanes + n * lanes
        twice = doubled(prepared(raw[:, at:at + lanes], k_gain_ref[...]))
        for m in range(2):
            k_ref[:, (2 * n + m) * lanes:(2 * n + m + 1) * lanes] = twice[m].astype(BF16)
        at += kv
        twice = doubled(raw[:, at:at + lanes])
        for m in range(2):
            v_ref[:, (2 * n + m) * lanes:(2 * n + m + 1) * lanes] = twice[m].astype(BF16)


def project(near, far, gain_near, gain_far, w_near, w_far, q_gain, k_gain, cosine, sine, rows=512):
    packed, half = near.shape
    columns = w_near.shape[1]
    groups = columns // (4 * HEAD_SIZE)
    width = groups * 2 * HEAD_SIZE
    kv = groups * HEAD_SIZE
    rows = min(rows, packed)

    def tile(n):
        return pl.BlockSpec((rows, n), lambda i: (i, 0))

    def whole(x):
        return pl.BlockSpec(x.shape, lambda i: (0, 0))

    def out(n, dtype):
        return jax.ShapeDtypeStruct((packed, n), dtype)

    small = (gain_near, gain_far, w_near, w_far, q_gain, k_gain)
    return pl.pallas_call(
        functools.partial(project_kernel, groups),
        out_shape=(out(half, BF16), out(half, BF16), out(width + kv, F32), out(width, BF16), out(width, BF16), out(width, BF16)),
        grid=(packed // rows,),
        in_specs=[tile(half), tile(half), *map(whole, small), tile(2 * HEAD_SIZE), tile(2 * HEAD_SIZE)],
        out_specs=(tile(half), tile(half), tile(width + kv), tile(width), tile(width), tile(width)),
        compiler_params=pltpu.CompilerParams(vmem_limit_bytes=40 << 20),
        cost_estimate=pl.CostEstimate(flops=4 * packed * half * columns, transcendentals=packed * 8,
                                      bytes_accessed=packed * (8 * half + 10 * width)),
        name="project",
    )(near, far, *small, cosine, sine)


def project_back_kernel(groups, dq_ref, dk_ref, dv_ref, raw_ref, near_ref, far_ref, gain_near_ref, gain_far_ref,
                        w_near_ref, w_far_ref, q_gain_ref, k_gain_ref, cos_ref, sin_ref,
                        grads_ref, to_near_ref, to_far_ref, stat_ref, q_sum_ref, k_sum_ref, near_sum_ref, far_sum_ref):
    @pl.when(pl.program_id(0) == 0)
    def _():
        for ref in (q_sum_ref, k_sum_ref, near_sum_ref, far_sum_ref):
            ref[...] = jnp.zeros_like(ref)

    cosine, sine = cos_ref[...], sin_ref[...]
    lanes = 2 * HEAD_SIZE
    first = lax.broadcasted_iota(jnp.int32, cosine.shape, 1) < HEAD_SIZE

    def back(grad, x, gain):
        inverse = lax.rsqrt(head_sums(x * x) / HEAD_SIZE + EPSILON)
        normed = x * inverse
        turned = grad * cosine - swapped(grad) * sine
        inner = turned * gain
        part = inverse * (inner - normed * (head_sums(inner * normed) / HEAD_SIZE))
        return part, jnp.sum(turned * normed, axis=0, keepdims=True)

    grads = []
    for n in range(groups):
        cut = slice(n * lanes, (n + 1) * lanes)
        part, total = back(dq_ref[:, cut], raw_ref[:, cut], q_gain_ref[...])
        q_sum_ref[...] += total
        grads.append(part.astype(BF16))
    for n in range(groups // 2):
        one = slice(2 * n * lanes, (2 * n + 1) * lanes)
        two = slice((2 * n + 1) * lanes, (2 * n + 2) * lanes)
        at = groups * lanes + n * lanes
        part, total = back(jnp.where(first, dk_ref[:, one], dk_ref[:, two]), raw_ref[:, at:at + lanes], k_gain_ref[...])
        k_sum_ref[...] += total
        grads.append(part.astype(BF16))
    for n in range(groups // 2):
        one = slice(2 * n * lanes, (2 * n + 1) * lanes)
        two = slice((2 * n + 1) * lanes, (2 * n + 2) * lanes)
        grads.append(jnp.where(first, dv_ref[:, one], dv_ref[:, two]).astype(BF16))
    grads = jnp.concatenate(grads, axis=1)
    grads_ref[...] = grads
    to_near = dot(grads, w_near_ref[...], NT)
    to_far = dot(grads, w_far_ref[...], NT)
    to_near_ref[...] = to_near.astype(BF16)
    to_far_ref[...] = to_far.astype(BF16)
    near = near_ref[...].astype(F32)
    far = far_ref[...].astype(F32)
    width = near.shape[1] + far.shape[1]
    total = jnp.sum(near * near, axis=1, keepdims=True) + jnp.sum(far * far, axis=1, keepdims=True)
    inverse = lax.rsqrt(total / width + EPSILON)
    near = to_near * (near * inverse)
    far = to_far * (far * inverse)
    near_sum_ref[...] += jnp.sum(near, axis=0, keepdims=True)
    far_sum_ref[...] += jnp.sum(far, axis=0, keepdims=True)
    stat = jnp.sum(near * gain_near_ref[...], axis=1, keepdims=True) + jnp.sum(far * gain_far_ref[...], axis=1, keepdims=True)
    stat_ref[...] = jnp.broadcast_to(stat, stat_ref.shape)


def project_back(dq, dk, dv, raw, near, far, gain_near, gain_far, w_near, w_far, q_gain, k_gain, cosine, sine, rows=512):
    packed, half = near.shape
    columns = w_near.shape[1]
    groups = columns // (4 * HEAD_SIZE)
    width = groups * 2 * HEAD_SIZE
    rows = min(rows, packed)

    def tile(n):
        return pl.BlockSpec((rows, n), lambda i: (i, 0))

    def whole(x):
        return pl.BlockSpec(x.shape, lambda i: (0, 0))

    def kept(n):
        return pl.BlockSpec((1, n), lambda i: (0, 0))

    def out(n, dtype, many=packed):
        return jax.ShapeDtypeStruct((many, n), dtype)

    small = (gain_near, gain_far, w_near, w_far, q_gain, k_gain)
    lanes = 2 * HEAD_SIZE
    return pl.pallas_call(
        functools.partial(project_back_kernel, groups),
        out_shape=(out(columns, BF16), out(half, BF16), out(half, BF16), out(lanes, F32), out(lanes, F32, 1), out(lanes, F32, 1),
                   out(half, F32, 1), out(half, F32, 1)),
        grid=(packed // rows,),
        in_specs=[tile(width), tile(width), tile(width), tile(raw.shape[1]), tile(half), tile(half), *map(whole, small),
                  tile(lanes), tile(lanes)],
        out_specs=(tile(columns), tile(half), tile(half), tile(lanes), kept(lanes), kept(lanes), kept(half), kept(half)),
        compiler_params=pltpu.CompilerParams(vmem_limit_bytes=44 << 20),
        cost_estimate=pl.CostEstimate(flops=4 * packed * half * columns, transcendentals=packed * 8,
                                      bytes_accessed=packed * (8 * half + 18 * width)),
        name="project_back",
    )(dq, dk, dv, raw, near, far, *small, cosine, sine)


def layout(lengths, packed):
    count = lengths.shape[0]
    numbers = jnp.arange(count, dtype=jnp.int32)
    ends = jnp.sum(jnp.where(numbers[None, :] <= numbers[:, None], lengths[None, :], 0), axis=1)
    begins = ends - lengths
    places = jnp.arange(packed, dtype=jnp.int32)
    member = jnp.sum((places[:, None] >= ends[None, :]).astype(jnp.int32), axis=1)
    return jnp.sum(jnp.where(member[:, None] == numbers[None, :], begins[None, :], 0), axis=1)


def rope_tables(position):
    half = HEAD_SIZE // 2
    inverse = jnp.exp(jnp.arange(half, dtype=F32) * (-2.0 * math.log(ROPE_BASE) / HEAD_SIZE))
    angles = position.astype(F32)[:, None] * inverse[None, :]
    cosine, sine = jnp.cos(angles), jnp.sin(angles)
    return jnp.concatenate([cosine] * 4, axis=1), jnp.concatenate([-sine, sine] * 2, axis=1)


def swap(x, axis):
    return jax.tree.map(lambda part: lax.ppermute(part, axis, [(0, 1), (1, 0)]), x)


def ordered(own, other, index, axis=0):
    return jnp.where(index == 0, jnp.concatenate([own, other], axis), jnp.concatenate([other, own], axis))


def part_of(x, index, axis, parts=2):
    size = x.shape[axis] // parts
    return lax.dynamic_slice_in_dim(x, index * size, size, axis)


def over_t(left, right):
    return dot(left, right, (((0,), (0,)), ((), ())))


def shards(
    tokens,
    seq_lengths,
    query_weight,
    key_matrix,
    value_matrix,
    out_weight,
    gate_weight,
    up_weight,
    down_weight,
    attn_gain,
    ffn_gain,
    query_gain,
    key_gain,
    cotangent,
):
    packed, half = tokens.shape
    row, col, group = lax.axis_index("row"), lax.axis_index("col"), lax.axis_index("dp")
    parts = lax.axis_size("dp")
    width = 2 * half

    near_own = part_of(tokens, col, 0)
    far_own = swap(near_own, "row")
    qkv = jnp.concatenate(
        [part_of(w, row, 1) for w in (query_weight, key_matrix, value_matrix)], axis=1)
    qkv_sent = jnp.concatenate(
        [part_of(w, 1 - row, 1) for w in (query_weight, key_matrix, value_matrix)], axis=1)
    qkv_far = swap(qkv_sent, "row")
    gains = jnp.stack([attn_gain, ffn_gain])
    gains_far = swap(gains, "row")
    far_other = swap(far_own, "col")
    far = ordered(far_own, far_other, col)
    cot_own = part_of(cotangent, col, 0)

    def far_weight(sent):
        piece = swap(part_of(sent, group, 0, parts), "row")
        return lax.all_gather(piece, "dp", axis=0, tiled=True)

    gate_up_near = jnp.concatenate([part_of(gate_weight, row, 1), part_of(up_weight, row, 1)], axis=1)
    gate_up_far = far_weight(jnp.concatenate([part_of(gate_weight, 1 - row, 1), part_of(up_weight, 1 - row, 1)], axis=1))
    down_near = part_of(down_weight, row, 0)
    down_far = far_weight(part_of(down_weight, 1 - row, 0))
    units = down_near.shape[0]

    out_far = swap(out_weight, "row")
    out_c = jnp.concatenate([out_weight, out_far], axis=1)
    out_n = swap(out_c, "col")
    out_own = part_of(out_c, row, 0)
    out_all = jnp.concatenate(
        [out_own, part_of(out_n, row, 0), part_of(out_c, 1 - row, 0), part_of(out_n, 1 - row, 0)], axis=0)

    cot_far_own = swap(cot_own, "row")
    cot_o = swap(jnp.concatenate([cot_own, cot_far_own], axis=1), "col")
    cot_c = jnp.concatenate([cot_own, cot_far_own], axis=1)

    starts = layout(seq_lengths[0], packed)
    cosine, sine = rope_tables(jnp.arange(packed, dtype=jnp.int32) - starts)
    q_gain = jnp.tile(query_gain, 2)[None, :]
    k_gain = jnp.tile(key_gain, 2)[None, :]
    small = (attn_gain[None, :], gains_far[0][None, :], qkv, qkv_far, q_gain, k_gain)
    hid_near, hid_far, raw, q, k, v = project(tokens, far, *small, cosine, sine)
    low, attended_raw, totals = attend(q, k, v, starts)

    chip = jnp.concatenate([part_of(low, col, 0), swap(part_of(low, 1 - col, 0), "col")], axis=1)
    attended = jnp.concatenate([chip, swap(chip, "row")], axis=1)
    mine = jnp.concatenate([near_own, far_own], axis=1)
    middle = mine.astype(F32) + dot(attended, out_all)
    inverse_two = lax.rsqrt(jnp.sum(middle * middle, axis=1, keepdims=True) / width + EPSILON)
    normal_two = middle * inverse_two
    gain_two = jnp.concatenate([ffn_gain, gains_far[1]])[None, :]
    hidden_c = (normal_two * gain_two).astype(BF16)
    hidden_o = swap(hidden_c, "col")
    gate_up = jnp.concatenate([gate_up_near, gate_up_far], axis=0)
    down = jnp.concatenate([down_near, down_far], axis=1)

    def feed(hidden, cot):
        both = dot(hidden, gate_up)
        grad_active = dot(cot, down, NT)
        gate, upward = both[:, :units], both[:, units:]
        sig = 1.0 / (1.0 + jnp.exp(-gate))
        lifted = gate * sig
        active = (lifted * upward).astype(BF16)
        grad_gate = (grad_active * upward * (sig * (1.0 + gate * (1.0 - sig)))).astype(BF16)
        grad_up = (grad_active * lifted).astype(BF16)
        return active, jnp.concatenate([grad_gate, grad_up], axis=1)

    active_o, grads_o = feed(hidden_o, cot_o)
    active_c, grads_c = feed(hidden_c, cot_c)
    back_o = swap(dot(grads_o, gate_up, NT).astype(BF16), "col")
    back_c = dot(grads_c, gate_up, NT) + back_o.astype(F32)
    back_low = back_c.astype(BF16)
    grad_hidden = back_c + jnp.concatenate(swap((back_low[:, half:], back_low[:, :half]), "row"), axis=1).astype(F32)

    grad_down = over_t(active_c, cot_c) + over_t(active_o, cot_o)
    grad_gate_up = over_t(hidden_c, grads_c) + over_t(hidden_o, grads_o)

    result_o = swap(dot(active_o, down).astype(BF16), "col")
    result_c = dot(active_c, down) + result_o.astype(F32)
    result = middle[:, :half] + result_c[:, :half] + swap(result_c[:, half:].astype(BF16), "row").astype(F32)
    result = result.astype(BF16)
    output = ordered(result, swap(result, "col"), col)

    ffn_gain_sum = jnp.sum(grad_hidden * normal_two, axis=0)
    inner = grad_hidden * gain_two
    stat = jnp.sum(inner * normal_two, axis=1, keepdims=True) / width
    grad_middle = cot_c.astype(F32) + inverse_two * (inner - normal_two * stat)
    branch_c = grad_middle.astype(BF16)
    branch_o = swap(branch_c, "col")
    grad_attended = ordered(dot(branch_c, out_own, NT).astype(BF16), dot(branch_o, out_own, NT).astype(BF16), col)
    grad_out = over_t(attended, branch_c[:, :half])
    quarter = grad_out.shape[0] // 4
    kept = jnp.concatenate([grad_out[:quarter], grad_out[2 * quarter:3 * quarter]], axis=0)
    sent = jnp.concatenate([grad_out[quarter:2 * quarter], grad_out[3 * quarter:]], axis=0)
    grad_out = kept + swap(sent.astype(BF16), "col").astype(F32)
    grad_out = ordered(grad_out[:quarter], grad_out[quarter:], row).astype(BF16)

    dq, dk, dv = attend_back(q, k, v, grad_attended, attended_raw, totals, starts)
    grads, to_near, to_far, stat_one, q_sum, k_sum, near_sum, far_sum = project_back(
        dq, dk, dv, raw, tokens, far, *small, cosine, sine)
    grad_qkv = jnp.concatenate([over_t(hid_near, grads), over_t(hid_far, grads)], axis=0)

    to_all = jnp.concatenate([to_near, to_far], axis=1)
    stat_one = stat_one[:, 0]
    sent_o, sent_stat = swap((part_of(to_all, 1 - col, 0), part_of(stat_one, 1 - col, 0)), "col")
    chip_sum = part_of(to_all, col, 0).astype(F32) + sent_o.astype(F32)
    chip_stat = part_of(stat_one, col, 0) + sent_stat
    other_sum, other_stat = swap((chip_sum[:, half:].astype(BF16), chip_stat), "row")
    inner_one = (chip_sum[:, :half] + other_sum.astype(F32)) * attn_gain[None, :]
    mine = mine.astype(F32)
    inverse_one = lax.rsqrt(jnp.sum(mine * mine, axis=1, keepdims=True) / width + EPSILON)
    stat_one = (chip_stat + other_stat)[:, None] / width
    grad_inputs = inverse_one * (inner_one - mine[:, :half] * inverse_one * stat_one) + grad_middle[:, :half]
    grad_inputs = grad_inputs.astype(BF16)
    grad_tokens = ordered(grad_inputs, swap(grad_inputs, "col"), col)

    def reduced(x, axis):
        return lax.psum_scatter(x, "dp", scatter_dimension=axis, tiled=True)

    def gathered(x, axis):
        return lax.all_gather(x, "dp", axis=axis, tiled=True)

    def columns_split(grad):
        piece = reduced(grad.astype(BF16).reshape(2, half, -1), 1)
        other = swap(piece[1], "row")
        full = gathered(ordered(piece[0][None], other[None], row), 1)
        return full.astype(F32)

    def rows_split(grad):
        piece = reduced(grad.astype(BF16), 0)
        other = swap(piece[:, half:], "row")
        full = gathered(ordered(piece[:, :half][None], other[None], row), 1)
        return full.astype(F32).reshape(-1, half)

    def side(full, begin, end):
        return jnp.concatenate([full[0][:, begin:end], full[1][:, begin:end]], axis=1)

    down_full = rows_split(grad_down)
    gate_up_full = columns_split(grad_gate_up)
    qkv_full = columns_split(grad_qkv)
    out_full = lax.psum(grad_out, "dp").astype(F32)
    q_cols, k_cols = query_weight.shape[1] // 2, key_matrix.shape[1] // 2

    def slots(x_near, x_far):
        return ordered(x_near, x_far, row)

    def folded(x):
        return x[0, :HEAD_SIZE] + x[0, HEAD_SIZE:]

    ffn_slots = slots(ffn_gain_sum[:half], ffn_gain_sum[half:]) * 0.5
    sums = lax.psum(
        jnp.concatenate([slots(near_sum[0], far_sum[0]), ffn_slots, folded(q_sum), folded(k_sum)]), ("dp", "row", "col"))
    attn_sum = part_of(sums[:width], row, 0)
    ffn_sum = part_of(sums[width:2 * width], row, 0)
    return (
        output,
        grad_tokens,
        side(qkv_full, 0, q_cols),
        side(qkv_full, q_cols, q_cols + k_cols),
        side(qkv_full, q_cols + k_cols, q_cols + 2 * k_cols),
        out_full,
        side(gate_up_full, 0, units),
        side(gate_up_full, units, 2 * units),
        down_full,
        attn_sum,
        ffn_sum,
        sums[2 * width:2 * width + HEAD_SIZE],
        sums[2 * width + HEAD_SIZE:],
    )


def solution(mesh):
    return jax.shard_map(
        shards,
        mesh=mesh,
        in_specs=(
            P("dp", "row"),
            P("dp", None),
            P("row", "col"),
            P("row", "col"),
            P("row", "col"),
            P("col", "row"),
            P("row", "col"),
            P("row", "col"),
            P("col", "row"),
            P("row"),
            P("row"),
            P(),
            P(),
            P("dp", "row"),
        ),
        out_specs=(
            P("dp", "row"),
            P("dp", "row"),
            P("row", "col"),
            P("row", "col"),
            P("row", "col"),
            P("col", "row"),
            P("row", "col"),
            P("row", "col"),
            P("col", "row"),
            P("row"),
            P("row"),
            P(),
            P(),
        ),
        check_vma=False,
    )
```

time: 2170 us -> 842 us (0.39)
  waiting for transfers between devices: 1620 us -> 421 us
  matrix products: 308 us -> 115 us
  Pallas kernels: 0 us -> 85.2 us
  other arithmetic: 105 us -> 70.2 us
  starting transfers between devices: 2.05 us -> 26 us
    reduce_scatter x7 -> x3, waiting for transfers between devices: 767 us -> 122 us  [reduced(): return lax.psum_scatter(x, 'dp', scatter_dimension=axis, tiled=True)]
    psum x4 -> x1, waiting for transfers between devices: 541 us -> 27.8 us  [shards(): out_full = lax.psum(grad_out, 'dp').astype(F32)]
    all_gather x7 -> x5, waiting for transfers between devices: 312 us -> 118 us  [the longest x3 92.4 us: gathered(): return lax.all_gather(x, 'dp', axis=axis, tiled=True)]
    dot_general x91 -> x18, matrix products: 308 us -> 115 us  [dot(): return lax.dot_general(a, b, dims, preferred_element_type=F32)]
    ppermute x0 -> x29, waiting for transfers between devices: none -> 153 us  [swap(): lax.ppermute(part, axis, [(0, 1), (1, 0)])]
    pallas_call x0 -> x4, Pallas kernels: none -> 85.2 us  [the longest x1 37.4 us: attend_back(): pl.pallas_call(functools.partial(attend_back_kernel, b, T), out_shape=(ou...]
    reduce_sum x20 -> x5, other arithmetic: 33.1 us -> 4.16 us  [the longest x1 2.14 us: shards(): ffn_gain_sum = jnp.sum(grad_hidden * normal_two, axis=0)]
    ppermute x0 -> x29, starting transfers between devices: none -> 24.6 us  [swap(): lax.ppermute(part, axis, [(0, 1), (1, 0)])]
  transfers between devices with their start and end apart: 18 -> 38, of which waited for: 16 -> 16; matrix products, arithmetic and copies ran while one was open for 14% -> 20% of each run, Pallas kernels for 0% -> 10%
where the time goes in v2:
time: 842 us; the launch traced here: 832 us
  waiting for transfers between devices  421 us (50%)
  matrix products  115 us (14%)
  Pallas kernels  85.2 us (10%)
  other arithmetic  70.2 us (8%)
  blocking collectives  54.6 us (6%)
  local copies, waits for them, and re-layouts  45.4 us (5%)
  starting transfers between devices  26 us (3%)
  between operations  15.1 us (2%)
    ppermute x29, waiting for transfers between devices, swap(): lax.ppermute(part, axis, [(0, 1), (1, 0)])  153 us
    reduce_scatter x3, waiting for transfers between devices, reduced(): return lax.psum_scatter(x, 'dp', scatter_dimension=axis, tiled=True)  122 us
    dot_general x18, matrix products, dot(): return lax.dot_general(a, b, dims, preferred_element_type=F32)  115 us
    all_gather x3, waiting for transfers between devices, gathered(): return lax.all_gather(x, 'dp', axis=axis, tiled=True)  92.4 us
    psum x1, blocking collectives, shards(): lax.psum(jnp.concatenate([slots(near_sum[0], far_sum[0]), ffn_slots, fold...  54.6 us
    pallas_call x1, Pallas kernels, attend_back(): pl.pallas_call(functools.partial(attend_back_kernel, b, T), out_shape=(ou...  37.4 us
    psum x1, waiting for transfers between devices, shards(): out_full = lax.psum(grad_out, 'dp').astype(F32)  27.8 us
    all_gather x2, waiting for transfers between devices, far_weight(): return lax.all_gather(piece, 'dp', axis=0, tiled=True)  25.6 us
  transfers between devices with their start and end apart: 38, of which 16 were waited for; matrix products, arithmetic and copies ran while one was open for 20% of the time, Pallas kernels for 10%

profile of v2, /device:TPU:0, one launch (start us, length us, event | category | flops | bytes accessed | tf_op | source)
XLA Modules:
  0.0 832.5 jit_solution(14569872235837870417)
XLA Ops:
  11.8 2.9 collective-permute-start.3
  18.9 4.1 constant_dynamic-slice_fusion.6
  26.0 24.3 %collective-permute-done = bf16[1024,512]{1,0:T(8,128)(2,1)} collective-permute-done((bf16[1024,512]{1,0:T(8,128)(2,1)S(1)}, bf16[1024,512]{1,0:T(8,128)(2,1)}, u32[]{:S(2)}, u32[]{:S(2)}) %collective-permute-start) | collective-permute-done | bytes 1048608 | tf_op jit(solution)/shard_map/ppermute | solution.py:401
  50.3 3.7 fusion.28
  61.4 4.3 maximum_select_fusion.far_ref
  65.8 10.7 %project.1 = (bf16[2048,512]{1,0:T(8,128)(2,1)S(1)}, bf16[2048,512]{1,0:T(8,128)(2,1)S(1)}, f32[2048,384]{1,0:T(8,128)}, bf16[2048,256]{1,0:T(8,128)(2,1)S(1)}, ...) custom-call(bf16[2048,512]{1,0:T(8,128)(2,1)S(1)} %copy-done.2, ...), custom_call_target="tpu_custom_call" | custom-call | flops 2147483648 | bytes 13631488 | tf_op jit(solution)/shard_map/project/pallas_call | solution.py:277
  79.2 21.7 %attend.1 = (bf16[2048,256]{1,0:T(8,128)(2,1)S(1)}, f32[2048,256]{1,0:T(8,128)S(1)}, f32[2,2,2048]{2,1,0:T(2,128)S(1)}) custom-call(s32[4]{0:T(128)S(1)} %slice.179.first_ref, s32[4]{0:T(128)S(1)} %slice.180.last_ref, bf16[2048,256]{1,0:T(8,128)(2,1)S(1)} %get-tuple-element.33.q_ref, bf16[2048,256]{1,0:T(8,128)(2,1)S(1)} %get-tuple-element.34.k_ref, ...), custom_call_target="tpu_custom_call" | custom-call | flops 10737418240 | bytes 5242880 | tf_op jit(solution)/shard_map/attend/pallas_call | solution.py:84
  109.0 23.6 %collective-permute-done.5 = bf16[1024,512]{1,0:T(8,128)(2,1)S(1)} collective-permute-done((bf16[1024,512]{1,0:T(8,128)(2,1)S(1)}, bf16[1024,512]{1,0:T(8,128)(2,1)S(1)}, u32[]{:S(2)}, u32[]{:S(2)}) %collective-permute-start.5) | collective-permute-done | bytes 1048608 | tf_op jit(solution)/shard_map/ppermute | solution.py:401
  132.7 4.3 multiply_reduce_fusion.3
  143.3 24.2 %collective-permute-done.14 = bf16[1024,512]{1,0:T(8,128)(2,1)} collective-permute-done((bf16[1024,512]{1,0:T(8,128)(2,1)}, bf16[1024,512]{1,0:T(8,128)(2,1)}, u32[]{:S(2)}, u32[]{:S(2)}) %collective-permute-start.14) | collective-permute-done | bytes 1048608 | tf_op jit(solution)/shard_map/ppermute | solution.py:401
  167.4 3.1 pad_maximum_fusion.11
  172.2 11.7 %fusion.43 = f32[1024,2304]{1,0:T(8,128)} fusion(bf16[1024,1024]{1,0:T(8,128)(2,1)} %collective-permute-done.10, bf16[512,2304]{1,0:T(8,128)(2,1)} %all-gather.6.cloned.1.call-done, bf16[512,1152]{1,0:T(8,128)(2,1)} %get-tuple-element.73, bf16[512,1152]{1,0:T(8,128)(2,1)} %get-tuple-element.129), kind=kOutput, calls=%fused_computation.155 | convolution fusion | flops 4845993984 | bytes 16252928 | tf_op jit(solution)/shard_map/dot_general | solution.py:18
  183.9 25.6 %all-gather.8.cloned.1.call-done = bf16[1152,512]{1,0:T(8,128)(2,1)} async-done(((bf16[144,512]{1,0:T(8,128)(2,1)}), bf16[1152,512]{1,0:T(8,128)(2,1)}) %all-gather.8.cloned.1.call-update) | async-done | bytes 1179664 | tf_op jit(solution)/shard_map/all_gather | solution.py:453
  209.5 10.8 %multiply_convert_fusion.1 = (bf16[1024,1152]{1,0:T(8,128)(2,1)S(1)}, bf16[1024,1152]{1,0:T(8,128)(2,1)S(1)}, bf16[1024,1152]{1,0:T(8,128)(2,1)}) fusion(f32[1024,2304]{1,0:T(8,128)} %fusion.43, bf16[1024,1024]{1,0:T(8,128)(2,1)} %collective-permute-done.15, bf16[1152,512]{1,0:T(8,128)(2,1)} %all-gather.8.cloned.1.call-done, ...), kind=kOutput, calls=%fused_computation.10 | convolution fusion | flops 2438332416 | bytes 20971520 | tf_op jit(solution)/shard_map/dot_general | solution.py:18
  221.7 5.1 fusion.24
  226.9 15.0 %fusion.44 = f32[1024,2304]{1,0:T(8,128)} fusion(bf16[1024,1024]{1,0:T(8,128)(2,1)} %multiply_convert_fusion.6, bf16[512,2304]{1,0:T(8,128)(2,1)S(1)} %copy-done.51, bf16[512,1152]{1,0:T(8,128)(2,1)S(1)} %copy-done.39, bf16[512,1152]{1,0:T(8,128)(2,1)S(1)} %copy-done.40), kind=kOutput, calls=%fused_computation.156 | convolution fusion | flops 4845993984 | bytes 16252928 | tf_op jit(solution)/shard_map/dot_general | solution.py:18
  241.9 10.4 %multiply_convert_fusion.3 = (bf16[1024,1152]{1,0:T(8,128)(2,1)}, bf16[1024,1152]{1,0:T(8,128)(2,1)}, bf16[1024,1152]{1,0:T(8,128)(2,1)}) fusion(f32[1024,2304]{1,0:T(8,128)} %fusion.44, bf16[1152,512]{1,0:T(8,128)(2,1)S(1)} %copy-done.52, bf16[1152,512]{1,0:T(8,128)(2,1)S(1)} %copy-done.41, bf16[1024,512]{1,0:T(8,128)(2,1)} %collective-permute-done.14, ...), kind=kOutput, calls=%fused_computation.12 | convolution fusion | flops 2442526720 | bytes 20971520 | tf_op jit(solution)/shard_map/dot_general | solution.py:18
  252.3 7.4 fusion.5
  262.0 24.0 %collective-permute-done.17 = bf16[1024,512]{1,0:T(8,128)(2,1)S(1)} collective-permute-done((bf16[1024,512]{1,0:T(8,128)(2,1)S(1)}, bf16[1024,512]{1,0:T(8,128)(2,1)S(1)}, u32[]{:S(2)}, u32[]{:S(2)}) %collective-permute-start.17) | collective-permute-done | bytes 1048608 | tf_op jit(solution)/shard_map/ppermute | solution.py:401
  286.0 21.9 %collective-permute-done.18 = bf16[1024,512]{1,0:T(8,128)(2,1)S(1)} collective-permute-done((bf16[1024,512]{1,0:T(8,128)(2,1)S(1)}, bf16[1024,512]{1,0:T(8,128)(2,1)S(1)}, u32[]{:S(2)}, u32[]{:S(2)}) %collective-permute-start.18) | collective-permute-done | bytes 1048608 | tf_op jit(solution)/shard_map/ppermute | solution.py:401
  310.0 5.3 fusion.45
  315.4 4.4 fusion.61
  319.8 5.6 add_convert_fusion.1
  331.7 37.4 %attend_back.1 = (f32[2048,256]{1,0:T(8,128)}, f32[2048,256]{1,0:T(8,128)}, f32[2048,256]{1,0:T(8,128)}) custom-call(s32[4]{0:T(128)S(1)} %slice.179.first_ref, s32[4]{0:T(128)S(1)} %slice.180.last_ref, bf16[2048,256]{1,0:T(8,128)(2,1)S(1)} %copy-done.18, bf16[2048,256]{1,0:T(8,128)(2,1)S(1)} %copy-done.20, bf16[2048,256]{1,0:T(8,128)(2,1)S(1)} %copy-done.22, ...), custom_call_target="tpu_custom_call" | custom-call | flops 26843545600 | bytes 10485760 | tf_op jit(solution)/shard_map/attend_back/pallas_call | solution.py:186
  369.2 15.3 %project_back.1 = (bf16[2048,512]{1,0:T(8,128)(2,1)S(1)}, bf16[2048,512]{1,0:T(8,128)(2,1)S(1)}, bf16[2048,512]{1,0:T(8,128)(2,1)}, f32[2048,128]{1,0:T(8,128)S(...) custom-call(f32[2048,256]{1,0:T(8,128)} %get-tuple-element.39.dq_ref, ...), custom_call_target="tpu_custom_call" | custom-call | flops 2147483648 | bytes 17825792 | tf_op jit(solution)/shard_map/project_back/pallas_call | solution.py:367
  390.1 8.3 %fusion.3 = f32[1024,2304]{1,0:T(8,128)S(1)} fusion(bf16[1024,1024]{1,0:T(8,128)(2,1)} %multiply_convert_fusion.6, bf16[1024,1152]{1,0:T(8,128)(2,1)} %get-tuple-element.62, bf16[1024,1152]{1,0:T(8,128)(2,1)} %get-tuple-element.61), kind=kOutput, calls=%fused_computation.30 | convolution fusion | flops 4841275392 | bytes 16252928 | tf_op jit(solution)/shard_map/dot_general | solution.py:18
  398.4 9.2 %add_convert_fusion = bf16[1024,2304]{1,0:T(8,128)(2,1)} fusion(f32[1024,2304]{1,0:T(8,128)S(1)} %fusion.3, bf16[1024,1024]{1,0:T(8,128)(2,1)} %collective-permute-done.10, bf16[1024,1152]{1,0:T(8,128)(2,1)S(1)} %copy-done.35, bf16[1024,1152]{1,0:T(8,128)(2,1)S(1)} %copy-done.33), kind=kOutput, calls=%fused_computation | convolution fusion | flops 4845993984 | bytes 20971520 | tf_op jit(solution)/shard_map/dot_general | solution.py:18
  409.0 4.0 fusion.60
  419.0 4.6 collective-permute-done.28
  424.5 35.5 %reduce-scatter.4.cloned.1.call-done = bf16[2,64,512]{2,1,0:T(8,128)(2,1)} async-done(((bf16[2,512,512]{2,1,0:T(8,128)(2,1)}), bf16[2,64,512]{2,1,0:T(8,128)(2,1)}) %reduce-scatter.4.cloned.1.call-update) | async-done | bytes 131088 | tf_op jit(solution)/shard_map/reduce_scatter | solution.py:553
  462.4 2.8 collective-permute-done.25
  466.2 5.9 convolution_convert_fusion
  472.1 86.7 %reduce-scatter.6.cloned.1.call-done = bf16[2,64,2304]{2,1,0:T(8,128)(2,1)} async-done(((bf16[2,512,2304]{2,1,0:T(8,128)(2,1)}), bf16[2,64,2304]{2,1,0:T(8,128)(2,1)}) %reduce-scatter.6.cloned.1.call-update) | async-done | bytes 589840 | tf_op jit(solution)/shard_map/reduce_scatter | solution.py:553
  561.4 7.3 collective-permute-done.27
  569.6 5.2 convert_add_fusion.3
  578.9 20.2 %collective-permute-done.12 = bf16[1024,512]{1,0:T(8,128)(2,1)S(1)} collective-permute-done((bf16[1024,512]{1,0:T(8,128)(2,1)S(1)}, bf16[1024,512]{1,0:T(8,128)(2,1)S(1)}, u32[]{:S(2)}, u32[]{:S(2)}) %collective-permute-start.12) | collective-permute-done | bytes 1048608 | tf_op jit(solution)/shard_map/ppermute | solution.py:401
  601.5 3.8 maximum_convert_fusion
  607.3 27.8 %all-reduce.2.cloned.1.call-done = bf16[512,512]{1,0:T(8,128)(2,1)} async-done(((bf16[512,512]{1,0:T(8,128)(2,1)}), bf16[512,512]{1,0:T(8,128)(2,1)}) %all-reduce.2.cloned.1.call-update) | async-done | bytes 524304 | tf_op jit(solution)/shard_map/psum | solution.py:576
  637.2 3.1 convert_add_fusion
  643.0 54.6 %psum.15 = f32[2176]{0:T(1024)S(1)} all-reduce(f32[2176]{0:T(1024)S(1)} %concatenate.189), channel_id=1, replica_groups=mesh['dp'=8,'row'=2,'col'=2] {'dp','row','col'}, use_global_device_ids=true, to_apply=%region_11.12 | all-reduce | flops 2176 | bytes 17408 | tf_op jit(solution)/shard_map/psum | solution.py:586
  702.8 3.7 fusion.6
  706.7 4.5 bitcast_convert_fusion
  711.2 19.7 %all-gather.10.cloned.1.call-done = bf16[2,512,512]{2,1,0:T(8,128)(2,1)} async-done(((bf16[2,64,512]{2,1,0:T(8,128)(2,1)}), bf16[2,512,512]{2,1,0:T(8,128)(2,1)}) %all-gather.10.cloned.1.call-update) | async-done | bytes 1048592 | tf_op jit(solution)/shard_map/all_gather | solution.py:556
  735.6 3.6 maximum_select_fusion.2
  739.1 72.7 %all-gather.12.cloned.1.call-done = bf16[2,512,2304]{2,1,0:T(8,128)(2,1)} async-done(((bf16[2,64,2304]{2,1,0:T(8,128)(2,1)}), bf16[2,512,2304]{2,1,0:T(8,128)(2,1)}) %all-gather.12.cloned.1.call-update) | async-done | bytes 4718608 | tf_op jit(solution)/shard_map/all_gather | solution.py:556
  811.8 3.0 convert_element_type.145
  814.9 2.8 slice_bitcast_fusion.1
  817.7 2.7 fusion.46
  (277 shorter events, 98.7 us)
Async XLA Ops:
  7.2 135.7 %copy-start = (bf16[2304,512]{1,0:T(8,128)(2,1)S(1)}, bf16[2304,512]{1,0:T(8,128)(2,1)}, u32[]{:S(2)}) copy-start(bf16[2304,512]{1,0:T(8,128)(2,1)} %param.22) | copy-start | bytes 7077892
  7.2 165.0 %all-gather.6.cloned.1.call-start = ((), (), s32[]{:S(2)}) async-start(), calls=%async_computation.3 | async-start | bytes 2654208 | tf_op jit(solution)/shard_map/all_gather | solution.py:453
  11.8 53.9 %collective-permute-start.3 = (bf16[512,512]{1,0:T(8,128)(2,1)}, bf16[512,512]{1,0:T(8,128)(2,1)}, u32[]{:S(2)}, u32[]{:S(2)}) collective-permute-start(bf16[512,512]{1,0:T(8,128)(2,1)} %pad_maximum_fusion.22), channel_id=1, source_target_pairs={{0,2},{2,0},{1,3},{3,1},{4,6},{6,4},{5,7},{7,5},{8,10},{10,8},{9,1... | collective-permute-start | bytes 1572872 | tf_op jit(solution)/shard_map/ppermute | solution.py:401
  16.1 34.2 %collective-permute-start = (bf16[1024,512]{1,0:T(8,128)(2,1)S(1)}, bf16[1024,512]{1,0:T(8,128)(2,1)}, u32[]{:S(2)}, u32[]{:S(2)}) collective-permute-start(bf16[1024,512]{1,0:T(8,128)(2,1)S(1)} %constant_dynamic-slice_fusion.20), channel_id=1, source_target_pairs={{0,2},{2,0},{1,3},{3,1},{4,6},{6,4},{5,7},{7,5},{8,10},{10,8},{9,1... | collective-permute-start | bytes 3145736 | tf_op jit(solution)/shard_map/ppermute | solution.py:401
  16.9 43.7 %collective-permute-start.2 = (f32[2,512]{1,0:T(2,128)}, f32[2,512]{1,0:T(2,128)}, u32[]{:S(2)}, u32[]{:S(2)}) collective-permute-start(f32[2,512]{1,0:T(2,128)} %pad_maximum_fusion.26), channel_id=1, source_target_pairs={{0,2},{2,0},{1,3},{3,1},{4,6},{6,4},{5,7},{7,5},{8,10},{10,8},{9,1... | collective-permute-start | bytes 12296 | tf_op jit(solution)/shard_map/ppermute | solution.py:401
  18.8 85.6 %collective-permute-start.6 = (bf16[512,512]{1,0:T(8,128)(2,1)}, bf16[512,512]{1,0:T(8,128)(2,1)}, u32[]{:S(2)}, u32[]{:S(2)}) collective-permute-start(bf16[512,512]{1,0:T(8,128)(2,1)} %param.19), channel_id=1, source_target_pairs={{0,2},{2,0},{1,3},{3,1},{4,6},{6,4},{5,7},{7,5},{8,10},{10,8},{9,1... | collective-permute-start | bytes 1572872 | tf_op jit(solution)/shard_map/ppermute | solution.py:401
  23.8 79.3 %collective-permute-start.8 = (bf16[64,2304]{1,0:T(8,128)(2,1)}, bf16[64,2304]{1,0:T(8,128)(2,1)}, u32[]{:S(2)}, u32[]{:S(2)}) collective-permute-start(bf16[64,2304]{1,0:T(8,128)(2,1)} %fusion.29), channel_id=1, source_target_pairs={{0,2},{2,0},{1,3},{3,1},{4,6},{6,4},{5,7},{7,5},{8,10},{10,8},{9,1... | collective-permute-start | bytes 884744 | tf_op jit(solution)/shard_map/ppermute | solution.py:401
  50.3 11.1 %collective-permute-start.1 = (bf16[1024,512]{1,0:T(8,128)(2,1)}, bf16[1024,512]{1,0:T(8,128)(2,1)}, u32[]{:S(2)}, u32[]{:S(2)}) collective-permute-start(bf16[1024,512]{1,0:T(8,128)(2,1)} %collective-permute-done), channel_id=1, source_target_pairs={{0,1},{1,0},{2,3},{3,2},{4,5},{5,4},{6,7},{7,6},{8,9},{9,8},{10,11... | collective-permute-start | bytes 3145736 | tf_op jit(solution)/shard_map/ppermute | solution.py:401
  79.2 21.8 %copy-start.21 = (bf16[2048,256]{1,0:T(8,128)(2,1)}, bf16[2048,256]{1,0:T(8,128)(2,1)S(1)}, u32[]{:S(2)}) copy-start(bf16[2048,256]{1,0:T(8,128)(2,1)S(1)} %get-tuple-element.35.v_ref) | copy-start | bytes 3145732
  102.7 2.9 collective-permute-start.4
  103.2 106.3 %all-gather.8.cloned.1.call-start = ((), (), s32[]{:S(2)}) async-start(), calls=%async_computation.4 | async-start | bytes 1327104 | tf_op jit(solution)/shard_map/all_gather | solution.py:453
  105.5 3.5 collective-permute-start.7
  106.7 25.9 %copy-start.30 = (bf16[1024,512]{1,0:T(8,128)(2,1)S(1)}, bf16[1024,512]{1,0:T(8,128)(2,1)}, u32[]{:S(2)}) copy-start(bf16[1024,512]{1,0:T(8,128)(2,1)} %copy-done.29) | copy-start | bytes 3145732
  106.7 25.9 %collective-permute-start.5 = (bf16[1024,512]{1,0:T(8,128)(2,1)S(1)}, bf16[1024,512]{1,0:T(8,128)(2,1)S(1)}, u32[]{:S(2)}, u32[]{:S(2)}) collective-permute-start(bf16[1024,512]{1,0:T(8,128)(2,1)S(1)} %pad_maximum_fusion.16), channel_id=1, source_target_pairs={{0,2},{2,0},{1,3},{3,1},{4,6},{6,4},{5,7},{7,5},{8,10},{10,8},{9,1... | collective-permute-start | bytes 3145736 | tf_op jit(solution)/shard_map/ppermute | solution.py:401
  108.9 28.0 %copy-start.46 = (bf16[256,1024]{1,0:T(8,128)(2,1)}, bf16[256,1024]{1,0:T(8,128)(2,1)S(1)}, u32[]{:S(2)}) copy-start(bf16[256,1024]{1,0:T(8,128)(2,1)S(1)} %get-tuple-element.89) | copy-start | bytes 1572868
  139.7 32.4 %collective-permute-start.10 = (bf16[1024,1024]{1,0:T(8,128)(2,1)}, bf16[1024,1024]{1,0:T(8,128)(2,1)}, u32[]{:S(2)}, u32[]{:S(2)}) collective-permute-start(bf16[1024,1024]{1,0:T(8,128)(2,1)} %multiply_convert_fusion.6), channel_id=1, source_target_pairs={{0,1},{1,0},{2,3},{3,2},{4,5},{5,4},{6,7},{7,6},{8,9},{9,8},{10,11... | collective-permute-start | bytes 6291464 | tf_op jit(solution)/shard_map/ppermute | solution.py:401
  141.1 26.3 %collective-permute-start.14 = (bf16[1024,512]{1,0:T(8,128)(2,1)}, bf16[1024,512]{1,0:T(8,128)(2,1)}, u32[]{:S(2)}, u32[]{:S(2)}) collective-permute-start(bf16[1024,512]{1,0:T(8,128)(2,1)} %constant_dynamic-slice_fusion.1), channel_id=1, source_target_pairs={{0,2},{2,0},{1,3},{3,1},{4,6},{6,4},{5,7},{7,5},{8,10},{10,8},{9,1... | collective-permute-start | bytes 3145736 | tf_op jit(solution)/shard_map/ppermute | solution.py:401
  142.9 27.7 %collective-permute-start.9 = (bf16[144,512]{1,0:T(8,128)(2,1)S(1)}, bf16[144,512]{1,0:T(8,128)(2,1)}, u32[]{:S(2)}, u32[]{:S(2)}) collective-permute-start(bf16[144,512]{1,0:T(8,128)(2,1)S(1)} %constant_dynamic-slice_fusion.2), channel_id=1, source_target_pairs={{0,2},{2,0},{1,3},{3,1},{4,6},{6,4},{5,7},{7,5},{8,10},{10,8},{9,1... | collective-permute-start | bytes 442376 | tf_op jit(solution)/shard_map/ppermute | solution.py:401
  170.6 38.9 %collective-permute-start.15 = (bf16[1024,1024]{1,0:T(8,128)(2,1)}, bf16[1024,1024]{1,0:T(8,128)(2,1)}, u32[]{:S(2)}, u32[]{:S(2)}) collective-permute-start(bf16[1024,1024]{1,0:T(8,128)(2,1)} %pad_maximum_fusion.11), channel_id=1, source_target_pairs={{0,1},{1,0},{2,3},{3,2},{4,5},{5,4},{6,7},{7,6},{8,9},{9,8},{10,11... | collective-permute-start | bytes 6291464 | tf_op jit(solution)/shard_map/ppermute | solution.py:401
  170.6 245.9 %reduce-scatter.8.cloned.1.call-start = ((), (), s32[]{:S(2)}) async-start(), calls=%async_computation.10 | async-start | bytes 2654208 | tf_op jit(solution)/shard_map/reduce_scatter | solution.py:553
  226.8 25.5 %collective-permute-start.16 = (bf16[1024,1024]{1,0:T(8,128)(2,1)S(1)}, bf16[1024,1024]{1,0:T(8,128)(2,1)S(1)}, u32[]{:S(2)}, u32[]{:S(2)}) collective-permute-start(bf16[1024,1024]{1,0:T(8,128)(2,1)S(1)} %fusion.24), channel_id=1, source_target_pairs={{0,1},{1,0},{2,3},{3,2},{4,5},{5,4},{6,7},{7,6},{8,9},{9,8},{10,11... | collective-permute-start | bytes 6291464 | tf_op jit(solution)/shard_map/ppermute | solution.py:401
  259.7 48.1 %copy-start.25 = (f32[1024,1024]{1,0:T(8,128)S(1)}, f32[1024,1024]{1,0:T(8,128)}, u32[]{:S(2)}) copy-start(f32[1024,1024]{1,0:T(8,128)} %copy-done.24) | copy-start | bytes 12582916
  259.9 26.0 %collective-permute-start.17 = (bf16[1024,512]{1,0:T(8,128)(2,1)S(1)}, bf16[1024,512]{1,0:T(8,128)(2,1)S(1)}, u32[]{:S(2)}, u32[]{:S(2)}) collective-permute-start(bf16[1024,512]{1,0:T(8,128)(2,1)S(1)} %get-tuple-element.79), channel_id=1, source_target_pairs={{0,2},{2,0},{1,3},{3,1},{4,6},{6,4},{5,7},{7,5},{8,10},{10,8},{9,1... | collective-permute-start | bytes 3145736 | tf_op jit(solution)/shard_map/ppermute | solution.py:401
  261.5 46.4 %collective-permute-start.18 = (bf16[1024,512]{1,0:T(8,128)(2,1)S(1)}, bf16[1024,512]{1,0:T(8,128)(2,1)S(1)}, u32[]{:S(2)}, u32[]{:S(2)}) collective-permute-start(bf16[1024,512]{1,0:T(8,128)(2,1)S(1)} %get-tuple-element.80), channel_id=1, source_target_pairs={{0,2},{2,0},{1,3},{3,1},{4,6},{6,4},{5,7},{7,5},{8,10},{10,8},{9,1... | collective-permute-start | bytes 3145736 | tf_op jit(solution)/shard_map/ppermute | solution.py:401
  315.3 13.6 %collective-permute-start.19 = (bf16[1024,1024]{1,0:T(8,128)(2,1)}, bf16[1024,1024]{1,0:T(8,128)(2,1)}, u32[]{:S(2)}, u32[]{:S(2)}) collective-permute-start(bf16[1024,1024]{1,0:T(8,128)(2,1)} %get-tuple-element.57), channel_id=1, source_target_pairs={{0,1},{1,0},{2,3},{3,2},{4,5},{5,4},{6,7},{7,6},{8,9},{9,8},{10,11... | collective-permute-start | bytes 6291464 | tf_op jit(solution)/shard_map/ppermute | solution.py:401
  325.5 134.5 %reduce-scatter.4.cloned.1.call-start = ((), (), s32[]{:S(2)}) async-start(), calls=%async_computation.5 | async-start | bytes 1179648 | tf_op jit(solution)/shard_map/reduce_scatter | solution.py:553
  331.7 37.4 %copy-start.4 = (f32[2048,128]{1,0:T(8,128)S(1)}, f32[2048,128]{1,0:T(8,128)}, u32[]{:S(2)}) copy-start(f32[2048,128]{1,0:T(8,128)} %get-tuple-element.127.sin_ref) | copy-start | bytes 3145732
  331.7 37.4 %copy-start.6 = (bf16[512,512]{1,0:T(8,128)(2,1)S(1)}, bf16[512,512]{1,0:T(8,128)(2,1)}, u32[]{:S(2)}) copy-start(bf16[512,512]{1,0:T(8,128)(2,1)} %pad_maximum_fusion.21.w_near_ref) | copy-start | bytes 1572868
  389.6 169.2 %reduce-scatter.6.cloned.1.call-start = ((), (), s32[]{:S(2)}) async-start(), calls=%async_computation.8 | async-start | bytes 5308416 | tf_op jit(solution)/shard_map/reduce_scatter | solution.py:553
  407.7 227.4 %all-reduce.2.cloned.1.call-start = ((), (), s32[]{:S(2)}) async-start(), calls=%async_computation.7 | async-start | bytes 1048576 | tf_op jit(solution)/shard_map/psum | solution.py:576
  413.1 2.0 collective-permute-start.26
  415.4 50.7 %copy-start.42 = (bf16[1152,512]{1,0:T(8,128)(2,1)S(1)}, bf16[1152,512]{1,0:T(8,128)(2,1)}, u32[]{:S(2)}) copy-start(bf16[1152,512]{1,0:T(8,128)(2,1)} %constant_dynamic-slice_fusion.3) | copy-start | bytes 3538948
  415.4 50.7 %copy-start.53 = (bf16[1152,512]{1,0:T(8,128)(2,1)S(1)}, bf16[1152,512]{1,0:T(8,128)(2,1)}, u32[]{:S(2)}) copy-start(bf16[1152,512]{1,0:T(8,128)(2,1)} %all-gather.8.cloned.1.call-done) | copy-start | bytes 3538948
  416.4 290.3 %all-gather.14.cloned.1.call-start = ((), (), s32[]{:S(2)}) async-start(), calls=%async_computation.11 | async-start | bytes 2654208 | tf_op jit(solution)/shard_map/all_gather | solution.py:556
  417.5 6.2 collective-permute-start.28
  424.4 306.5 %all-gather.10.cloned.1.call-start = ((), (), s32[]{:S(2)}) async-start(), calls=%async_computation.6 | async-start | bytes 1179648 | tf_op jit(solution)/shard_map/all_gather | solution.py:556
  460.9 4.3 collective-permute-start.25
  465.9 345.9 %all-gather.12.cloned.1.call-start = ((), (), s32[]{:S(2)}) async-start(), calls=%async_computation.9 | async-start | bytes 5308416 | tf_op jit(solution)/shard_map/all_gather | solution.py:556
  472.0 97.6 %collective-permute-start.11 = (bf16[1024,1024]{1,0:T(8,128)(2,1)}, bf16[1024,1024]{1,0:T(8,128)(2,1)}, u32[]{:S(2)}, u32[]{:S(2)}) collective-permute-start(bf16[1024,1024]{1,0:T(8,128)(2,1)} %convolution_convert_fusion), channel_id=1, source_target_pairs={{0,1},{1,0},{2,3},{3,2},{4,5},{5,4},{6,7},{7,6},{8,9},{9,8},{10,11... | collective-permute-start | bytes 6291464 | tf_op jit(solution)/shard_map/ppermute | solution.py:401
  559.9 8.8 %collective-permute-start.27 = (bf16[64,2304]{1,0:T(8,128)(2,1)S(1)}, bf16[64,2304]{1,0:T(8,128)(2,1)S(1)}, u32[]{:S(2)}, u32[]{:S(2)}) collective-permute-start(bf16[64,2304]{1,0:T(8,128)(2,1)S(1)} %get-tuple-element.94), channel_id=1, source_target_pairs={{0,2},{2,0},{1,3},{3,1},{4,6},{6,4},{5,7},{7,5},{8,10},{10,8},{9,1... | collective-permute-start | bytes 884744 | tf_op jit(solution)/shard_map/ppermute | solution.py:401
  575.0 24.1 %collective-permute-start.12 = (bf16[1024,512]{1,0:T(8,128)(2,1)S(1)}, bf16[1024,512]{1,0:T(8,128)(2,1)S(1)}, u32[]{:S(2)}, u32[]{:S(2)}) collective-permute-start(bf16[1024,512]{1,0:T(8,128)(2,1)S(1)} %slice.335), channel_id=1, source_target_pairs={{0,2},{2,0},{1,3},{3,1},{4,6},{6,4},{5,7},{7,5},{8,10},{10,8},{9,1... | collective-permute-start | bytes 3145736 | tf_op jit(solution)/shard_map/ppermute | solution.py:401
  577.3 22.3 %copy-start.28 = (bf16[2048,1024]{1,0:T(8,128)(2,1)}, bf16[2048,1024]{1,0:T(8,128)(2,1)S(1)}, u32[]{:S(2)}) copy-start(bf16[2048,1024]{1,0:T(8,128)(2,1)S(1)} %constant_dynamic-update-slice_fusion.2) | copy-start | bytes 12582916
  578.9 58.4 %collective-permute-start.20 = (bf16[1024,1024]{1,0:T(8,128)(2,1)}, bf16[1024,1024]{1,0:T(8,128)(2,1)}, u32[]{:S(2)}, u32[]{:S(2)}) collective-permute-start(bf16[1024,1024]{1,0:T(8,128)(2,1)} %constant_dynamic-slice_fusion), channel_id=1, source_target_pairs={{0,1},{1,0},{2,3},{3,2},{4,5},{5,4},{6,7},{7,6},{8,9},{9,8},{10,11... | collective-permute-start | bytes 6291464 | tf_op jit(solution)/shard_map/ppermute | solution.py:401
  599.7 5.6 collective-permute-start.13
  640.6 61.3 %collective-permute-start.21 = (bf16[1024,512]{1,0:T(8,128)(2,1)S(1)}, bf16[1024,512]{1,0:T(8,128)(2,1)S(1)}, u32[]{:S(2)}, u32[]{:S(2)}) collective-permute-start(bf16[1024,512]{1,0:T(8,128)(2,1)S(1)} %slice.334), channel_id=1, source_target_pairs={{0,2},{2,0},{1,3},{3,1},{4,6},{6,4},{5,7},{7,5},{8,10},{10,8},{9,1... | collective-permute-start | bytes 3145736 | tf_op jit(solution)/shard_map/ppermute | solution.py:401
  642.7 54.9 %collective-permute-start.22 = (f32[1024]{0:T(1024)S(1)}, f32[1024]{0:T(1024)S(1)}, u32[]{:S(2)}, u32[]{:S(2)}) collective-permute-start(f32[1024]{0:T(1024)S(1)} %get-tuple-element.55), channel_id=1, source_target_pairs={{0,1},{1,0},{2,3},{3,2},{4,5},{5,4},{6,7},{7,6},{8,9},{9,8},{10,11... | collective-permute-start | bytes 12296 | tf_op jit(solution)/shard_map/ppermute | solution.py:401
  697.6 4.2 collective-permute-start.23
  706.6 29.0 %collective-permute-start.24 = (bf16[1024,512]{1,0:T(8,128)(2,1)S(1)}, bf16[1024,512]{1,0:T(8,128)(2,1)}, u32[]{:S(2)}, u32[]{:S(2)}) collective-permute-start(bf16[1024,512]{1,0:T(8,128)(2,1)S(1)} %fusion.6), channel_id=1, source_target_pairs={{0,1},{1,0},{2,3},{3,2},{4,5},{5,4},{6,7},{7,6},{8,9},{9,8},{10,11... | collective-permute-start | bytes 3145736 | tf_op jit(solution)/shard_map/ppermute | solution.py:401
  (49 other events, 309.7 us)
Sparse Core Ops, SparseCore 0:
  103.3 49.8 all-gather.5
  170.7 38.6 all-gather.7
  325.6 68.0 reduce-scatter.7
  397.5 62.3 reduce-scatter.3
  464.5 94.2 reduce-scatter.5
  563.0 72.0 all-reduce.1
  637.9 51.9 all-gather.13
  692.0 38.8 all-gather.9
  733.1 78.6 all-gather.11

commit v3 on v2

--- a/solution.py
+++ b/solution.py
@@ -12,6 +12,7 @@
 EPSILON = 1e-05
 ROPE_BASE = 1000000.0
 F32, BF16 = jnp.float32, jnp.bfloat16
+MESH = pl.DeviceIdType.MESH
 
 
 def dot(a, b, dims=(((1,), (0,)), ((), ()))):
@@ -75,9 +76,9 @@
     lse_ref[0, 0:1, :] = total[:, :bq]
     lse_ref[0, 1:2, :] = total[:, bq:]
 
-def attend(q, k, v, starts, bq=512, bk=512):
-    T, width = q.shape
-    groups = width // 128
+def attend(q, k, v, starts, group, bq=512, bk=512):
+    T, width = q.shape[0], 128
+    groups = 1
     first, last = starts[::bq], starts[bq - 1::bq]
     kern = functools.partial(attend_kernel, bq, bk)
     pairs = T * (T + bk) // 2
@@ -88,9 +89,9 @@
         grid_spec=pltpu.PrefetchScalarGridSpec(
             num_scalar_prefetch=2, grid=(groups, T // bq),
             in_specs=[
-                pl.BlockSpec((bq, 128), lambda g, i, *_: (i, g)),
-                pl.BlockSpec((T, 128), lambda g, i, *_: (0, g)),
-                pl.BlockSpec((T, 128), lambda g, i, *_: (0, g)),
+                pl.BlockSpec((bq, 128), lambda g, i, *_: (i, group)),
+                pl.BlockSpec((T, 128), lambda g, i, *_: (0, group)),
+                pl.BlockSpec((T, 128), lambda g, i, *_: (0, group)),
                 pl.BlockSpec((bq, 1), lambda g, i, *_: (i, 0)),
             ],
             out_specs=[
@@ -174,13 +175,15 @@
     dv_ref[...] = dv + pltpu.roll(dv, 64, 1)
     dq_ref[...] = dqt_ref[:, pl.ds(pl.multiple_of(j * b, b), b)].T * 0.125
 
-def attend_back(q, k, v, grad, raw, lse, starts, b=512):
-    T, width = q.shape
-    groups = width // 128
+def attend_back(q, k, v, grad, raw, lse, starts, group, b=512):
+    T, width = q.shape[0], 128
+    groups = 1
     first, last = starts[::b], starts[b - 1::b]
     blocks = T // b
-    col = pl.BlockSpec((T, 128), lambda g, j, *_: (0, g))
-    blk = pl.BlockSpec((b, 128), lambda g, j, *_: (j, g))
+    own = pl.BlockSpec((T, 128), lambda g, j, *_: (0, 0))
+    blk = pl.BlockSpec((b, 128), lambda g, j, *_: (j, 0))
+    col = pl.BlockSpec((T, 128), lambda g, j, *_: (0, group))
+    part = pl.BlockSpec((b, 128), lambda g, j, *_: (j, group))
     out = jax.ShapeDtypeStruct((T, width), F32)
     pairs = T * (T + b) // 2
     return pl.pallas_call(
@@ -188,7 +191,7 @@
         out_shape=(out, out, out),
         grid_spec=pltpu.PrefetchScalarGridSpec(
             num_scalar_prefetch=2, grid=(groups, blocks),
-            in_specs=[col, blk, blk, col, col,
+            in_specs=[col, part, part, col, own,
                       pl.BlockSpec((1, 2, T), lambda g, j, *_: (g, 0, 0)),
                       pl.BlockSpec((1, T), lambda g, j, *_: (0, 0))],
             out_specs=[blk, blk, blk],
@@ -287,7 +290,12 @@
     )(near, far, *small, cosine, sine)
 
 
-def project_back_kernel(groups, dq_ref, dk_ref, dv_ref, raw_ref, near_ref, far_ref, gain_near_ref, gain_far_ref,
+def project_back_kernel(groups, *refs):
+    dq, dk, dv = refs[:groups], refs[groups:2 * groups], refs[2 * groups:3 * groups]
+    project_back_body(groups, dq, dk, dv, *refs[3 * groups:])
+
+
+def project_back_body(groups, dq_refs, dk_refs, dv_refs, raw_ref, near_ref, far_ref, gain_near_ref, gain_far_ref,
                         w_near_ref, w_far_ref, q_gain_ref, k_gain_ref, cos_ref, sin_ref,
                         grads_ref, to_near_ref, to_far_ref, stat_ref, q_sum_ref, k_sum_ref, near_sum_ref, far_sum_ref):
     @pl.when(pl.program_id(0) == 0)
@@ -310,20 +318,16 @@
     grads = []
     for n in range(groups):
         cut = slice(n * lanes, (n + 1) * lanes)
-        part, total = back(dq_ref[:, cut], raw_ref[:, cut], q_gain_ref[...])
+        part, total = back(dq_refs[n][...], raw_ref[:, cut], q_gain_ref[...])
         q_sum_ref[...] += total
         grads.append(part.astype(BF16))
     for n in range(groups // 2):
-        one = slice(2 * n * lanes, (2 * n + 1) * lanes)
-        two = slice((2 * n + 1) * lanes, (2 * n + 2) * lanes)
         at = groups * lanes + n * lanes
-        part, total = back(jnp.where(first, dk_ref[:, one], dk_ref[:, two]), raw_ref[:, at:at + lanes], k_gain_ref[...])
+        part, total = back(jnp.where(first, dk_refs[2 * n][...], dk_refs[2 * n + 1][...]), raw_ref[:, at:at + lanes], k_gain_ref[...])
         k_sum_ref[...] += total
         grads.append(part.astype(BF16))
     for n in range(groups // 2):
-        one = slice(2 * n * lanes, (2 * n + 1) * lanes)
-        two = slice((2 * n + 1) * lanes, (2 * n + 2) * lanes)
-        grads.append(jnp.where(first, dv_ref[:, one], dv_ref[:, two]).astype(BF16))
+        grads.append(jnp.where(first, dv_refs[2 * n][...], dv_refs[2 * n + 1][...]).astype(BF16))
     grads = jnp.concatenate(grads, axis=1)
     grads_ref[...] = grads
     to_near = dot(grads, w_near_ref[...], NT)
@@ -369,14 +373,14 @@
         out_shape=(out(columns, BF16), out(half, BF16), out(half, BF16), out(lanes, F32), out(lanes, F32, 1), out(lanes, F32, 1),
                    out(half, F32, 1), out(half, F32, 1)),
         grid=(packed // rows,),
-        in_specs=[tile(width), tile(width), tile(width), tile(raw.shape[1]), tile(half), tile(half), *map(whole, small),
+        in_specs=[tile(lanes)] * (3 * groups) + [tile(raw.shape[1]), tile(half), tile(half), *map(whole, small),
                   tile(lanes), tile(lanes)],
         out_specs=(tile(columns), tile(half), tile(half), tile(lanes), kept(lanes), kept(lanes), kept(half), kept(half)),
         compiler_params=pltpu.CompilerParams(vmem_limit_bytes=44 << 20),
         cost_estimate=pl.CostEstimate(flops=4 * packed * half * columns, transcendentals=packed * 8,
                                       bytes_accessed=packed * (8 * half + 18 * width)),
         name="project_back",
-    )(dq, dk, dv, raw, near, far, *small, cosine, sine)
+    )(*dq, *dk, *dv, raw, near, far, *small, cosine, sine)
 
 
 def layout(lengths, packed):
@@ -412,6 +416,192 @@
 
 def over_t(left, right):
     return dot(left, right, (((0,), (0,)), ((), ())))
+
+
+def ring_kernel(n, names, plan, *refs):
+    arrays = max(array for array, *_ in plan) + 1
+    inputs, refs = refs[:arrays], refs[arrays:]
+    gains_ref, give_ref, give_stat_ref, *refs = refs
+    outs = max(out for _, _, _, out, _ in plan) + 1
+    outputs, refs = refs[:outs], refs[outs:]
+    (sums_ref, take_ref, take_stat_ref, *refs) = refs
+    slots, refs = refs[:len(plan)], refs[len(plan):]
+    (group_in, ring_in, mine, rs_send, rs_recv, ag_send, ag_recv, cross_send, cross_recv, group_send, group_recv,
+     all_send, all_recv, give_send, give_recv) = refs
+    dp, row, col = (lax.axis_index(name) for name in names)
+    side = dp % 2
+    place = (dp // 2) * (1 - side) + (n - 1 - dp // 2) * side
+
+    def device(position):
+        position = (position + 2 * n) % n
+        back = position // (n // 2)
+        return (position * (1 - back) + (n - 1 - position) * back) * 2 + back
+
+    up, down = device(place + 1), device(place - 1)
+    streams = range(len(plan))
+    crossing = [s for s in streams if plan[s][4]]
+    staying = [s for s in streams if not plan[s][4]]
+
+    barrier = pltpu.get_barrier_semaphore()
+    others = [((dp + k) % n, row, col) for k in range(1, n)]
+    quad = [(dp, 1 - row, col), (dp, row, 1 - col), (dp, 1 - row, 1 - col)]
+    for target in others + quad:
+        pl.semaphore_signal(barrier, inc=1, device_id=target, device_id_type=MESH)
+    pl.semaphore_wait(barrier, n + 2)
+
+    def copy(src, dst, send, recv, target):
+        return pltpu.make_async_remote_copy(
+            src_ref=src, dst_ref=dst, send_sem=send, recv_sem=recv, device_id=target, device_id_type=MESH)
+
+    def toward(s):
+        return (up if s % 2 == 0 else down, row, col)
+
+    def local(s, chunk):
+        array, begin, columns, _, _ = plan[s]
+        return inputs[array].at[chunk, :, pl.ds(begin, columns)]
+
+    def result(s, chunk, quarter):
+        _, begin, columns, out, _ = plan[s]
+        if outputs[out].shape[0] == 1:
+            quarter = 0
+        return outputs[out].at[quarter, chunk, :, pl.ds(begin, columns)]
+
+    def final(s, chunk):
+        return result(s, chunk, 1 - row if plan[s][4] else row)
+
+    def own(s):
+        return (place + 1) % n if s % 2 == 0 else (place + n - 1) % n
+
+    def reduce_copy(s, t, src):
+        return copy(src, slots[s].at[t], rs_send.at[s, t], rs_recv.at[s, t], toward(s))
+
+    for s in streams:
+        reduce_copy(s, 0, local(s, place)).start()
+    gathers = [copy(gains_ref, group_in.at[k], group_send.at[k], group_recv.at[k], quad[k]) for k in range(3)]
+    for gather in gathers:
+        gather.start()
+    gives = [copy(give_ref, take_ref, give_send.at[0], give_recv.at[0], quad[0]),
+             copy(give_stat_ref, take_stat_ref, give_send.at[1], give_recv.at[1], quad[0])]
+    for give in gives:
+        give.start()
+
+    def reduce_step(t, carry):
+        for s in streams:
+            chunk = (place - t - 1 + 2 * n) % n if s % 2 == 0 else (place + t + 1) % n
+            slot = slots[s].at[t]
+            reduce_copy(s, t, slot).wait_recv()
+            slot[...] = (slot[...].astype(F32) + local(s, chunk)[...].astype(F32)).astype(BF16)
+
+            @pl.when(t < n - 2)
+            def _():
+                reduce_copy(s, t + 1, slot).start()
+        return carry
+
+    lax.fori_loop(0, n - 1, reduce_step, 0)
+
+    crosses = [copy(slots[s].at[n - 2], result(s, own(s), row), cross_send.at[k], cross_recv.at[k], quad[0])
+               for k, s in enumerate(crossing)]
+    for cross in crosses:
+        cross.start()
+
+    def gather_copy(s, t, chunk):
+        return copy(final(s, chunk), final(s, chunk), ag_send.at[s, t], ag_recv.at[s, t], toward(s))
+
+    for s in staying:
+        final(s, own(s))[...] = slots[s][n - 2]
+        gather_copy(s, 0, own(s)).start()
+
+    for gather in gathers:
+        gather.wait()
+    mine[...] = gains_ref[...] + group_in[0] + group_in[1] + group_in[2]
+    spreads = [copy(mine, ring_in.at[k - 1], all_send.at[k - 1], all_recv.at[k - 1], others[k - 1]) for k in range(1, n)]
+    for spread in spreads:
+        spread.start()
+
+    for k, s in enumerate(crossing):
+        crosses[k].wait()
+        gather_copy(s, 0, own(s)).start()
+
+    def gather_step(t, carry):
+        for s in staying + crossing:
+            chunk = (place - t + 2 * n) % n if s % 2 == 0 else (place + t) % n
+            gather_copy(s, t, chunk).wait_recv()
+
+            @pl.when(t < n - 2)
+            def _():
+                gather_copy(s, t + 1, chunk).start()
+        return carry
+
+    lax.fori_loop(0, n - 1, gather_step, 0)
+
+    total = mine[...]
+    for spread in spreads:
+        spread.wait()
+    for k in range(n - 1):
+        total = total + ring_in[k]
+    sums_ref[...] = total
+    for give in gives:
+        give.wait()
+
+    def finish(t, carry):
+        for s in streams:
+            reduce_copy(s, t, slots[s].at[t]).wait_send()
+            gather_copy(s, t, 0).wait_send()
+        return carry
+
+    lax.fori_loop(0, n - 1, finish, 0)
+
+
+def ring_sum(near, far, alone, gains, give, give_stat, names, n):
+    inputs, plan, out_shape = [], [], []
+
+    def lanes(k, x, out, crosses):
+        columns = x.shape[2] // 2
+        for begin in (0, columns):
+            plan.append((k, begin, columns, out, crosses))
+
+    for x in far:
+        lanes(len(inputs), x, len(inputs), True)
+        inputs.append(x)
+    for out, x in enumerate(near):
+        lanes(len(inputs), x, out, False)
+        inputs.append(x)
+        out_shape.append(jax.ShapeDtypeStruct((2, *x.shape), BF16))
+    for x in alone:
+        lanes(len(inputs), x, len(out_shape), False)
+        inputs.append(x)
+        out_shape.append(jax.ShapeDtypeStruct((1, *x.shape), BF16))
+    out_shape += [jax.ShapeDtypeStruct(gains.shape, F32), jax.ShapeDtypeStruct(give.shape, give.dtype),
+                  jax.ShapeDtypeStruct(give_stat.shape, F32)]
+    vmem = pl.BlockSpec(memory_space=pltpu.VMEM)
+    dma = pltpu.SemaphoreType.DMA
+    many, crosses = len(plan), 2 * len(far)
+    size = sum(x.size for x in inputs)
+    slots = [pltpu.VMEM((n - 1, inputs[array].shape[1], columns), BF16) for array, _, columns, _, _ in plan]
+    return pl.pallas_call(
+        functools.partial(ring_kernel, n, names, tuple(plan)),
+        out_shape=tuple(out_shape),
+        in_specs=[vmem] * (len(inputs) + 3),
+        out_specs=(vmem,) * len(out_shape),
+        scratch_shapes=[
+            *slots, pltpu.VMEM((3, *gains.shape), F32),
+            pltpu.VMEM((n - 1, *gains.shape), F32), pltpu.VMEM(gains.shape, F32),
+            dma((many, n - 1)), dma((many, n - 1)), dma((many, n - 1)), dma((many, n - 1)), dma((crosses,)), dma((crosses,)),
+            dma((3,)), dma((3,)), dma((n - 1,)), dma((n - 1,)), dma((2,)), dma((2,)),
+        ],
+        compiler_params=pltpu.CompilerParams(collective_id=0, has_side_effects=True, vmem_limit_bytes=58 << 20),
+        cost_estimate=pl.CostEstimate(flops=4 * size, transcendentals=0, bytes_accessed=60 * size),
+        name="ring_sum",
+    )(*inputs, gains, give, give_stat)
+
+
+def gated(x, *deps):
+    late = functools.reduce(jnp.logical_or, [dep != dep for dep in deps])
+    return jnp.where(late, jnp.zeros_like(x), x)
+
+
+def corner(x):
+    return x[(0,) * x.ndim].astype(F32)
 
 
 def shards(
@@ -444,30 +634,30 @@
     qkv_far = swap(qkv_sent, "row")
     gains = jnp.stack([attn_gain, ffn_gain])
     gains_far = swap(gains, "row")
-    far_other = swap(far_own, "col")
-    far = ordered(far_own, far_other, col)
-    cot_own = part_of(cotangent, col, 0)
+    far = ordered(far_own, swap(far_own, "col"), col)
 
     def far_weight(sent):
-        piece = swap(part_of(sent, group, 0, parts), "row")
-        return lax.all_gather(piece, "dp", axis=0, tiled=True)
+        piece = swap(gated(part_of(sent, group, 0, parts), corner(far_own)), "row")
+        return lax.all_gather(piece, "dp", axis=0, tiled=True), corner(piece)
 
     gate_up_near = jnp.concatenate([part_of(gate_weight, row, 1), part_of(up_weight, row, 1)], axis=1)
-    gate_up_far = far_weight(jnp.concatenate([part_of(gate_weight, 1 - row, 1), part_of(up_weight, 1 - row, 1)], axis=1))
+    gate_up_far, sign_one = far_weight(
+        jnp.concatenate([part_of(gate_weight, 1 - row, 1), part_of(up_weight, 1 - row, 1)], axis=1))
     down_near = part_of(down_weight, row, 0)
-    down_far = far_weight(part_of(down_weight, 1 - row, 0))
+    down_far, sign_two = far_weight(part_of(down_weight, 1 - row, 0))
     units = down_near.shape[0]
 
-    out_far = swap(out_weight, "row")
+    out_far = swap(gated(out_weight, sign_one, sign_two), "row")
     out_c = jnp.concatenate([out_weight, out_far], axis=1)
     out_n = swap(out_c, "col")
     out_own = part_of(out_c, row, 0)
     out_all = jnp.concatenate(
         [out_own, part_of(out_n, row, 0), part_of(out_c, 1 - row, 0), part_of(out_n, 1 - row, 0)], axis=0)
 
-    cot_far_own = swap(cot_own, "row")
-    cot_o = swap(jnp.concatenate([cot_own, cot_far_own], axis=1), "col")
+    cot_own = part_of(cotangent, col, 0)
+    cot_far_own = swap(gated(cot_own, corner(out_far)), "row")
     cot_c = jnp.concatenate([cot_own, cot_far_own], axis=1)
+    cot_o = swap(cot_c, "col")
 
     starts = layout(seq_lengths[0], packed)
     cosine, sine = rope_tables(jnp.arange(packed, dtype=jnp.int32) - starts)
@@ -475,12 +665,25 @@
     k_gain = jnp.tile(key_gain, 2)[None, :]
     small = (attn_gain[None, :], gains_far[0][None, :], qkv, qkv_far, q_gain, k_gain)
     hid_near, hid_far, raw, q, k, v = project(tokens, far, *small, cosine, sine)
-    low, attended_raw, totals = attend(q, k, v, starts)
-
-    chip = jnp.concatenate([part_of(low, col, 0), swap(part_of(low, 1 - col, 0), "col")], axis=1)
-    attended = jnp.concatenate([chip, swap(chip, "row")], axis=1)
+
+    groups = q.shape[1] // (2 * HEAD_SIZE)
+    attended, raws, totals = [], [], []
+    for n in range(groups):
+        low, attended_raw, total = attend(q, k, v, starts, n)
+        raws.append(attended_raw)
+        totals.append(total)
+        chip = jnp.concatenate([part_of(low, col, 0), swap(part_of(low, 1 - col, 0), "col")], axis=1)
+        attended.append(jnp.concatenate([chip, swap(chip, "row")], axis=1))
+    size = out_own.shape[0] // groups
+
+    def group_rows(n):
+        quarter = out_own.shape[0]
+        return jnp.concatenate([out_all[p * quarter + n * size:p * quarter + (n + 1) * size] for p in range(4)], axis=0)
+
     mine = jnp.concatenate([near_own, far_own], axis=1)
-    middle = mine.astype(F32) + dot(attended, out_all)
+    middle = mine.astype(F32)
+    for n in range(groups):
+        middle = middle + dot(attended[n], group_rows(n))
     inverse_two = lax.rsqrt(jnp.sum(middle * middle, axis=1, keepdims=True) / width + EPSILON)
     normal_two = middle * inverse_two
     gain_two = jnp.concatenate([ffn_gain, gains_far[1]])[None, :]
@@ -500,15 +703,19 @@
         grad_up = (grad_active * lifted).astype(BF16)
         return active, jnp.concatenate([grad_gate, grad_up], axis=1)
 
+    active_c, grads_c = feed(hidden_c, cot_c)
     active_o, grads_o = feed(hidden_o, cot_o)
-    active_c, grads_c = feed(hidden_c, cot_c)
+
+    grad_down = (over_t(active_c, cot_c) + over_t(active_o, cot_o)).astype(BF16)
+    grad_down = lax.psum(grad_down, "dp")
+
     back_o = swap(dot(grads_o, gate_up, NT).astype(BF16), "col")
     back_c = dot(grads_c, gate_up, NT) + back_o.astype(F32)
     back_low = back_c.astype(BF16)
-    grad_hidden = back_c + jnp.concatenate(swap((back_low[:, half:], back_low[:, :half]), "row"), axis=1).astype(F32)
-
-    grad_down = over_t(active_c, cot_c) + over_t(active_o, cot_o)
-    grad_gate_up = over_t(hidden_c, grads_c) + over_t(hidden_o, grads_o)
+    back_far = jnp.concatenate(swap((back_low[:, half:], back_low[:, :half]), "row"), axis=1)
+    grad_hidden = back_c + back_far.astype(F32)
+
+    grad_gate_up = (over_t(hidden_c, grads_c) + over_t(hidden_o, grads_o)).astype(BF16)
 
     result_o = swap(dot(active_o, down).astype(BF16), "col")
     result_c = dot(active_c, down) + result_o.astype(F32)
@@ -519,88 +726,79 @@
     ffn_gain_sum = jnp.sum(grad_hidden * normal_two, axis=0)
     inner = grad_hidden * gain_two
     stat = jnp.sum(inner * normal_two, axis=1, keepdims=True) / width
+    stat = gated(stat, corner(grad_gate_up), corner(result_c))
     grad_middle = cot_c.astype(F32) + inverse_two * (inner - normal_two * stat)
     branch_c = grad_middle.astype(BF16)
     branch_o = swap(branch_c, "col")
     grad_attended = ordered(dot(branch_c, out_own, NT).astype(BF16), dot(branch_o, out_own, NT).astype(BF16), col)
-    grad_out = over_t(attended, branch_c[:, :half])
-    quarter = grad_out.shape[0] // 4
-    kept = jnp.concatenate([grad_out[:quarter], grad_out[2 * quarter:3 * quarter]], axis=0)
-    sent = jnp.concatenate([grad_out[quarter:2 * quarter], grad_out[3 * quarter:]], axis=0)
+
+    grad_out = [over_t(attended[n], branch_c[:, :half]) for n in range(groups)]
+    kept = jnp.concatenate([g[p * size:(p + 1) * size] for p in (0, 2) for g in grad_out], axis=0)
+    sent = jnp.concatenate([g[p * size:(p + 1) * size] for p in (1, 3) for g in grad_out], axis=0)
     grad_out = kept + swap(sent.astype(BF16), "col").astype(F32)
+    quarter = out_own.shape[0]
     grad_out = ordered(grad_out[:quarter], grad_out[quarter:], row).astype(BF16)
 
-    dq, dk, dv = attend_back(q, k, v, grad_attended, attended_raw, totals, starts)
+    dq, dk, dv = zip(*(attend_back(q, k, v, grad_attended, raws[n], totals[n], starts, n) for n in range(groups)))
     grads, to_near, to_far, stat_one, q_sum, k_sum, near_sum, far_sum = project_back(
         dq, dk, dv, raw, tokens, far, *small, cosine, sine)
-    grad_qkv = jnp.concatenate([over_t(hid_near, grads), over_t(hid_far, grads)], axis=0)
 
     to_all = jnp.concatenate([to_near, to_far], axis=1)
-    stat_one = stat_one[:, 0]
     sent_o, sent_stat = swap((part_of(to_all, 1 - col, 0), part_of(stat_one, 1 - col, 0)), "col")
     chip_sum = part_of(to_all, col, 0).astype(F32) + sent_o.astype(F32)
     chip_stat = part_of(stat_one, col, 0) + sent_stat
-    other_sum, other_stat = swap((chip_sum[:, half:].astype(BF16), chip_stat), "row")
+
+    near_grads = jnp.concatenate([grad_gate_up[:half], over_t(hid_near, grads).astype(BF16)], axis=1)
+    far_grads = jnp.concatenate([grad_gate_up[half:], over_t(hid_far, grads).astype(BF16)], axis=1)
+
+    def folded(x):
+        return x[0, :HEAD_SIZE] + x[0, HEAD_SIZE:]
+
+    vector = jnp.concatenate([
+        ordered(near_sum[0], far_sum[0], row),
+        ordered(ffn_gain_sum[:half], ffn_gain_sum[half:], row) * 0.5,
+        folded(q_sum), folded(k_sum)])
+    length = vector.shape[0]
+    lines = -(-length // 1024) * 8
+    vector = jnp.concatenate([vector, jnp.zeros((lines * 128 - length,), F32)]).reshape(lines, 128)
+    near_grads, far_grads, grad_out = (
+        x.reshape(parts, half // parts, -1) for x in (near_grads, far_grads, grad_out))
+    full, out_full, sums, other_sum, other_stat = ring_sum(
+        [near_grads], [far_grads], [grad_out], vector, chip_sum[:, half:].astype(BF16), chip_stat,
+        ("dp", "row", "col"), parts)
+    full = full.reshape(2, half, -1)
+    sums = sums.reshape(-1)
+
+    def columns(begin, end):
+        return jnp.concatenate([full[0][:, begin:end], full[1][:, begin:end]], axis=1).astype(F32)
+
     inner_one = (chip_sum[:, :half] + other_sum.astype(F32)) * attn_gain[None, :]
     mine = mine.astype(F32)
     inverse_one = lax.rsqrt(jnp.sum(mine * mine, axis=1, keepdims=True) / width + EPSILON)
-    stat_one = (chip_stat + other_stat)[:, None] / width
+    stat_one = (chip_stat + other_stat)[:, :1] / width
     grad_inputs = inverse_one * (inner_one - mine[:, :half] * inverse_one * stat_one) + grad_middle[:, :half]
     grad_inputs = grad_inputs.astype(BF16)
     grad_tokens = ordered(grad_inputs, swap(grad_inputs, "col"), col)
 
-    def reduced(x, axis):
-        return lax.psum_scatter(x, "dp", scatter_dimension=axis, tiled=True)
-
-    def gathered(x, axis):
-        return lax.all_gather(x, "dp", axis=axis, tiled=True)
-
-    def columns_split(grad):
-        piece = reduced(grad.astype(BF16).reshape(2, half, -1), 1)
-        other = swap(piece[1], "row")
-        full = gathered(ordered(piece[0][None], other[None], row), 1)
-        return full.astype(F32)
-
-    def rows_split(grad):
-        piece = reduced(grad.astype(BF16), 0)
-        other = swap(piece[:, half:], "row")
-        full = gathered(ordered(piece[:, :half][None], other[None], row), 1)
-        return full.astype(F32).reshape(-1, half)
-
-    def side(full, begin, end):
-        return jnp.concatenate([full[0][:, begin:end], full[1][:, begin:end]], axis=1)
-
-    down_full = rows_split(grad_down)
-    gate_up_full = columns_split(grad_gate_up)
-    qkv_full = columns_split(grad_qkv)
-    out_full = lax.psum(grad_out, "dp").astype(F32)
+    grad_down = gated(grad_down, corner(q_sum))
+    down_other = swap(grad_down[:, half:], "row")
+    down_full = ordered(grad_down[:, :half], gated(down_other, sums[0]), row).astype(F32)
     q_cols, k_cols = query_weight.shape[1] // 2, key_matrix.shape[1] // 2
-
-    def slots(x_near, x_far):
-        return ordered(x_near, x_far, row)
-
-    def folded(x):
-        return x[0, :HEAD_SIZE] + x[0, HEAD_SIZE:]
-
-    ffn_slots = slots(ffn_gain_sum[:half], ffn_gain_sum[half:]) * 0.5
-    sums = lax.psum(
-        jnp.concatenate([slots(near_sum[0], far_sum[0]), ffn_slots, folded(q_sum), folded(k_sum)]), ("dp", "row", "col"))
-    attn_sum = part_of(sums[:width], row, 0)
-    ffn_sum = part_of(sums[width:2 * width], row, 0)
+    at_q, at_k, at_v = 2 * units, 2 * units + q_cols, 2 * units + q_cols + k_cols
     return (
         output,
         grad_tokens,
-        side(qkv_full, 0, q_cols),
-        side(qkv_full, q_cols, q_cols + k_cols),
-        side(qkv_full, q_cols + k_cols, q_cols + 2 * k_cols),
-        out_full,
-        side(gate_up_full, 0, units),
-        side(gate_up_full, units, 2 * units),
+        columns(at_q, at_k),
+        columns(at_k, at_v),
+        columns(at_v, at_v + k_cols),
+        out_full.reshape(half, -1).astype(F32),
+        columns(0, units),
+        columns(units, 2 * units),
         down_full,
-        attn_sum,
-        ffn_sum,
+        part_of(sums[:width], row, 0),
+        part_of(sums[width:2 * width], row, 0),
         sums[2 * width:2 * width + HEAD_SIZE],
-        sums[2 * width + HEAD_SIZE:],
+        sums[2 * width + HEAD_SIZE:2 * width + 2 * HEAD_SIZE],
     )
 
 

time: 842 us -> 635 us (0.75)
  waiting for transfers between devices: 421 us -> 129 us
  Pallas kernels: 85.2 us -> 221 us
  blocking collectives: 54.6 us -> 0 us
  between operations: 15.1 us -> 24.6 us
    pallas_call x0 -> x1, Pallas kernels: none -> 135 us  [ring_sum(): pl.pallas_call(functools.partial(ring_kernel, n, names, tuple(plan)), out...]
    reduce_scatter x3 -> x0, waiting for transfers between devices: 122 us -> none  [reduced(): return lax.psum_scatter(x, 'dp', scatter_dimension=axis, tiled=True)]
    all_gather x5 -> x2, waiting for transfers between devices: 118 us -> 17.7 us  [far_weight(): return (lax.all_gather(piece, 'dp', axis=0, tiled=True), corner(piece))]
    psum x1 -> x0, blocking collectives: 54.6 us -> none  [shards(): lax.psum(jnp.concatenate([slots(near_sum[0], far_sum[0]), ffn_slots, fold...]
    ppermute x29 -> x27, waiting for transfers between devices: 153 us -> 111 us  [swap(): lax.ppermute(part, axis, [(0, 1), (1, 0)])]
    psum x1, waiting for transfers between devices: 27.8 us -> 0.01 us  [shards(): grad_down = lax.psum(grad_down, 'dp')]
    slice x13 -> x25, local copies, waits for them, and re-layouts: 6.99 us -> 16.2 us  [the longest x6 5.74 us: corner(): return x[(0,) * x.ndim].astype(F32)]
    ppermute x29 -> x27, starting transfers between devices: 24.6 us -> 19 us  [swap(): lax.ppermute(part, axis, [(0, 1), (1, 0)])]
  transfers between devices with their start and end apart: 38 -> 30, of which waited for: 16 -> 11; matrix products, arithmetic and copies ran while one was open for 20% -> 31% of each run, Pallas kernels for 10% -> 35%
where the time goes in v3:
time: 635 us; the launch traced here: 628 us
  Pallas kernels  221 us (35%)
  waiting for transfers between devices  129 us (20%)
  matrix products  111 us (17%)
  other arithmetic  71.1 us (11%)
  local copies, waits for them, and re-layouts  52.9 us (8%)
  between operations  24.6 us (4%)
  starting transfers between devices  19.3 us (3%)
    pallas_call x1, Pallas kernels, ring_sum(): pl.pallas_call(functools.partial(ring_kernel, n, names, tuple(plan)), out...  135 us
    ppermute x27, waiting for transfers between devices, swap(): lax.ppermute(part, axis, [(0, 1), (1, 0)])  111 us
    dot_general x20, matrix products, dot(): return lax.dot_general(a, b, dims, preferred_element_type=F32)  111 us
    pallas_call x2, Pallas kernels, attend_back(): pl.pallas_call(functools.partial(attend_back_kernel, b, T), out_shape=(ou...  38.1 us
    pallas_call x2, Pallas kernels, attend(): pl.pallas_call(kern, out_shape=(jax.ShapeDtypeStruct((T, width), BF16), j...  21.9 us
    ppermute x27, starting transfers between devices, swap(): lax.ppermute(part, axis, [(0, 1), (1, 0)])  19 us
    all_gather x2, waiting for transfers between devices, far_weight(): return (lax.all_gather(piece, 'dp', axis=0, tiled=True), corner(piece))  17.7 us
    unnamed x161, local copies, waits for them, and re-layouts  16.7 us
  transfers between devices with their start and end apart: 30, of which 11 were waited for; matrix products, arithmetic and copies ran while one was open for 31% of the time, Pallas kernels for 35%

profile of v3, /device:TPU:0, one launch (start us, length us, event | category | flops | bytes accessed | tf_op | source)
XLA Modules:
  0.0 628.0 jit_solution(658288114457996085)
XLA Ops:
  11.2 2.9 collective-permute-start.3
  14.3 2.1 collective-permute-start.2
  16.7 4.1 constant_dynamic-slice_fusion.9
  20.9 28.0 %collective-permute-done = bf16[1024,512]{1,0:T(8,128)(2,1)} collective-permute-done((bf16[1024,512]{1,0:T(8,128)(2,1)S(1)}, bf16[1024,512]{1,0:T(8,128)(2,1)}, u32[]{:S(2)}, u32[]{:S(2)}) %collective-permute-start) | collective-permute-done | bytes 1048608 | tf_op jit(solution)/shard_map/ppermute | solution.py:405
  54.5 5.7 fusion.42
  60.2 2.6 collective-permute-done.7
  69.7 6.6 %pad_maximum_fusion.13 = (f32[2048,128]{1,0:T(8,128)S(1)}, f32[2048,128]{1,0:T(8,128)}) fusion(f32[2048,32]{1,0:T(8,128)} %get-tuple-element.143, f32[2048,32]{1,0:T(8,128)} %get-tuple-element.142, f32[2048,32]{1,0:T(8,128)} %get-tuple-element.141), kind=kLoop, calls=%fused_computation.67 | loop fusion | flops 1572864 | bytes 2883584 | tf_op jit(solution)/shard_map/concatenate | solution.py:401
  82.7 4.2 maximum_select_fusion.1.far_ref.refs_8_
  86.9 10.8 %project.1 = (bf16[2048,512]{1,0:T(8,128)(2,1)S(1)}, bf16[2048,512]{1,0:T(8,128)(2,1)S(1)}, f32[2048,384]{1,0:T(8,128)}, bf16[2048,256]{1,0:T(8,128)(2,1)S(1)}, ...) custom-call(bf16[2048,512]{1,0:T(8,128)(2,1)S(1)} %copy-done, ...), custom_call_target="tpu_custom_call" | custom-call | flops 2147483648 | bytes 13631488 | tf_op jit(solution)/shard_map/project/pallas_call | solution.py:280
  100.4 10.9 %attend.2 = (bf16[2048,128]{1,0:T(8,128)(2,1)S(1)}, f32[2048,128]{1,0:T(8,128)S(1)}, f32[1,2,2048]{2,1,0:T(2,128)S(1)}) custom-call(s32[4]{0:T(128)S(1)} %slice.245.first_ref, s32[4]{0:T(128)S(1)} %slice.246.last_ref, bf16[2048,256]{1,0:T(8,128)(2,1)S(1)} %get-tuple-element.44.q_ref, bf16[2048,256]{1,0:T(8,128)(2,1)S(1)} %get-tuple-element.45.k_ref, ...), custom_call_target="tpu_custom_call" | custom-call | flops 5368709120 | bytes 2621440 | tf_op jit(solution)/shard_map/attend/pallas_call | solution.py:85
  112.0 10.9 %attend.3 = (bf16[2048,128]{1,0:T(8,128)(2,1)S(1)}, f32[2048,128]{1,0:T(8,128)S(1)}, f32[1,2,2048]{2,1,0:T(2,128)S(1)}) custom-call(s32[4]{0:T(128)S(1)} %slice.245.first_ref, s32[4]{0:T(128)S(1)} %slice.246.last_ref, bf16[2048,256]{1,0:T(8,128)(2,1)S(1)} %get-tuple-element.44.q_ref, bf16[2048,256]{1,0:T(8,128)(2,1)S(1)} %get-tuple-element.45.k_ref, ...), custom_call_target="tpu_custom_call" | custom-call | flops 5368709120 | bytes 2621440 | tf_op jit(solution)/shard_map/attend/pallas_call | solution.py:85
  131.9 7.8 %collective-permute-done.5 = bf16[1024,256]{1,0:T(8,128)(2,1)} collective-permute-done((bf16[1024,256]{1,0:T(8,128)(2,1)S(1)}, bf16[1024,256]{1,0:T(8,128)(2,1)}, u32[]{:S(2)}, u32[]{:S(2)}) %collective-permute-start.5) | collective-permute-done | bytes 524320 | tf_op jit(solution)/shard_map/ppermute | solution.py:405
  139.8 2.4 fusion.15
  142.2 8.2 %collective-permute-done.11 = bf16[1024,256]{1,0:T(8,128)(2,1)S(1)} collective-permute-done((bf16[1024,256]{1,0:T(8,128)(2,1)S(1)}, bf16[1024,256]{1,0:T(8,128)(2,1)S(1)}, u32[]{:S(2)}, u32[]{:S(2)}) %collective-permute-start.11) | collective-permute-done | bytes 524320 | tf_op jit(solution)/shard_map/ppermute | solution.py:405
  150.4 3.0 multiply_reduce_fusion.3
  158.2 24.0 %collective-permute-done.16 = bf16[1024,512]{1,0:T(8,128)(2,1)S(1)} collective-permute-done((bf16[1024,512]{1,0:T(8,128)(2,1)S(1)}, bf16[1024,512]{1,0:T(8,128)(2,1)S(1)}, u32[]{:S(2)}, u32[]{:S(2)}) %collective-permute-start.16) | collective-permute-done | bytes 1048608 | tf_op jit(solution)/shard_map/ppermute | solution.py:405
  185.0 2.4 constant_dynamic-slice_fusion.8
  189.1 3.8 maximum_convert_fusion.2
  193.6 11.8 %fusion.62 = f32[1024,2304]{1,0:T(8,128)} fusion(bf16[1024,1024]{1,0:T(8,128)(2,1)} %collective-permute-done.12, bf16[512,2304]{1,0:T(8,128)(2,1)} %all-gather.3.cloned.1.call-done, bf16[512,1152]{1,0:T(8,128)(2,1)} %get-tuple-element.103, bf16[512,1152]{1,0:T(8,128)(2,1)} %get-tuple-element.157), kind=kOutput, calls=%fused_computation.181 | convolution fusion | flops 4845993984 | bytes 16252928 | tf_op jit(solution)/shard_map/dot_general | solution.py:19
  205.4 17.7 %all-gather.5.cloned.1.call-done = bf16[1152,512]{1,0:T(8,128)(2,1)} async-done(((bf16[144,512]{1,0:T(8,128)(2,1)}), bf16[1152,512]{1,0:T(8,128)(2,1)}) %all-gather.5.cloned.1.call-update) | async-done | bytes 1179664 | tf_op jit(solution)/shard_map/all_gather | solution.py:641
  223.2 9.0 %multiply_convert_fusion.1 = (bf16[1024,1152]{1,0:T(8,128)(2,1)S(1)}, bf16[1024,1152]{1,0:T(8,128)(2,1)S(1)}, bf16[1024,1152]{1,0:T(8,128)(2,1)S(1)}) fusion(f32[1024,2304]{1,0:T(8,128)} %fusion.62, bf16[1024,1024]{1,0:T(8,128)(2,1)} %collective-permute-done.17, bf16[1152,512]{1,0:T(8,128)(2,1)} %all-gather.5.cloned.1.call-done, ...), kind=kOutput, calls=%fused_computation.6 | convolution fusion | flops 2438332416 | bytes 20971520 | tf_op jit(solution)/shard_map/dot_general | solution.py:19
  232.2 4.7 convolution_convert_fusion
  237.0 6.4 %fusion.14 = bf16[1024,1024]{1,0:T(8,128)(2,1)} fusion(bf16[1024,1152]{1,0:T(8,128)(2,1)S(1)} %get-tuple-element.82, bf16[1024,1152]{1,0:T(8,128)(2,1)S(1)} %get-tuple-element.81, bf16[512,2304]{1,0:T(8,128)(2,1)S(1)} %copy-done.65, bf16[512,1152]{1,0:T(8,128)(2,1)S(1)} %copy-done.41, bf16[512,1152]{1,0:T(8,128)(2,1)S(1)} %copy-done.42), kind=kOutput, calls=%fused_computation.59 | convolution fusion | flops 4856479744 | bytes 11534336 | tf_op jit(solution)/shard_map/dot_general | solution.py:19
  243.9 14.7 %fusion.63 = f32[1024,2304]{1,0:T(8,128)} fusion(bf16[1024,1024]{1,0:T(8,128)(2,1)} %multiply_convert_fusion.6, bf16[512,2304]{1,0:T(8,128)(2,1)S(1)} %copy-done.65, bf16[512,1152]{1,0:T(8,128)(2,1)S(1)} %copy-done.41, bf16[512,1152]{1,0:T(8,128)(2,1)S(1)} %copy-done.42), kind=kOutput, calls=%fused_computation.182 | convolution fusion | flops 4845993984 | bytes 16252928 | tf_op jit(solution)/shard_map/dot_general | solution.py:19
  258.6 8.7 %multiply_convert_fusion.3 = (bf16[1024,1152]{1,0:T(8,128)(2,1)S(1)}, bf16[1024,1152]{1,0:T(8,128)(2,1)S(1)}, bf16[1024,1152]{1,0:T(8,128)(2,1)}) fusion(f32[1024,2304]{1,0:T(8,128)} %fusion.63, bf16[1152,512]{1,0:T(8,128)(2,1)S(1)} %copy-done.67, bf16[1152,512]{1,0:T(8,128)(2,1)S(1)} %copy-done.45, bf16[1024,512]{1,0:T(8,128)(2,1)S(1)} %copy-done.34, ...), kind=kOutput, calls=%fused_computation.8 | convolution fusion | flops 2442526720 | bytes 20971520 | tf_op jit(solution)/shard_map/dot_general | solution.py:19
  267.3 8.7 %fusion.3 = f32[1024,2304]{1,0:T(8,128)S(1)} fusion(bf16[1024,1024]{1,0:T(8,128)(2,1)} %multiply_convert_fusion.6, bf16[1024,1152]{1,0:T(8,128)(2,1)S(1)} %get-tuple-element.84, bf16[1024,1152]{1,0:T(8,128)(2,1)S(1)} %get-tuple-element.83), kind=kOutput, calls=%fused_computation.27 | convolution fusion | flops 4841275392 | bytes 16252928 | tf_op jit(solution)/shard_map/dot_general | solution.py:19
  276.1 6.5 %fusion.83 = f32[1152,1024]{1,0:T(8,128)} fusion(bf16[1024,1152]{1,0:T(8,128)(2,1)S(1)} %copy-done.78, bf16[1024,1024]{1,0:T(8,128)(2,1)} %collective-permute-done.17), kind=kOutput, calls=%fused_computation.202 | convolution fusion | flops 2415919104 | bytes 9175040 | tf_op jit(solution)/shard_map/dot_general | solution.py:19
  282.6 8.0 %add_convert_fusion = bf16[1024,2304]{1,0:T(8,128)(2,1)S(1)} fusion(f32[1024,2304]{1,0:T(8,128)S(1)} %fusion.3, bf16[1024,1024]{1,0:T(8,128)(2,1)} %collective-permute-done.12, bf16[1024,1152]{1,0:T(8,128)(2,1)} %copy-done.36, bf16[1024,1152]{1,0:T(8,128)(2,1)S(1)} %get-tuple-element.81), kind=kOutput, calls=%fused_computation | convolution fusion | flops 4845993984 | bytes 20971520 | tf_op jit(solution)/shard_map/dot_general | solution.py:19
  290.6 2.5 fusion.66
  293.1 2.1 copy-done.19
  297.3 7.1 %fusion.5 = (bf16[1024,1024]{1,0:T(8,128)(2,1)S(1)}, f32[1024,1024]{1,0:T(8,128)}) fusion(bf16[1024,1024]{1,0:T(8,128)(2,1)S(1)} %collective-permute-done.18, bf16[512,2304]{1,0:T(8,128)(2,1)S(1)} %copy-done.66, bf16[512,1152]{1,0:T(8,128)(2,1)S(1)} %copy-done.41, bf16[512,1152]{1,0:T(8,128)(2,1)S(1)} %copy-done.43, bf16[1024,1152]{1,0:T(8,128)(2,1)S(1)} %copy-done.76, ...), kind=kOutput, calls=%fused_computation.29 | convolution fusion | flops 4858576896 | bytes 17825792 | tf_op jit(solution)/shard_map/dot_general | solution.py:19
  307.9 5.8 add_convert_fusion.1
  316.2 6.1 convert_add_fusion.3
  325.8 6.3 %collective-permute-done.19 = bf16[1024,512]{1,0:T(8,128)(2,1)S(1)} collective-permute-done((bf16[1024,512]{1,0:T(8,128)(2,1)}, bf16[1024,512]{1,0:T(8,128)(2,1)S(1)}, u32[]{:S(2)}, u32[]{:S(2)}) %collective-permute-start.19) | collective-permute-done | bytes 1048608 | tf_op jit(solution)/shard_map/ppermute | solution.py:405
  332.1 22.6 %collective-permute-done.20 = bf16[1024,512]{1,0:T(8,128)(2,1)} collective-permute-done((bf16[1024,512]{1,0:T(8,128)(2,1)}, bf16[1024,512]{1,0:T(8,128)(2,1)}, u32[]{:S(2)}, u32[]{:S(2)}) %collective-permute-start.20) | collective-permute-done | bytes 1048608 | tf_op jit(solution)/shard_map/ppermute | solution.py:405
  354.7 3.2 multiply_reduce_fusion
  358.0 4.8 fusion.64
  367.1 9.1 %collective-permute-done.14 = bf16[1024,512]{1,0:T(8,128)(2,1)S(1)} collective-permute-done((bf16[1024,512]{1,0:T(8,128)(2,1)S(1)}, bf16[1024,512]{1,0:T(8,128)(2,1)S(1)}, u32[]{:S(2)}, u32[]{:S(2)}) %collective-permute-start.14) | collective-permute-done | bytes 1048608 | tf_op jit(solution)/shard_map/ppermute | solution.py:405
  383.6 19.0 %attend_back.3 = (f32[2048,128]{1,0:T(8,128)S(1)}, f32[2048,128]{1,0:T(8,128)S(1)}, f32[2048,128]{1,0:T(8,128)S(1)}) custom-call(s32[4]{0:T(128)S(1)} %slice.245.first_ref, s32[4]{0:T(128)S(1)} %slice.246.last_ref, bf16[2048,256]{1,0:T(8,128)(2,1)S(1)} %copy-done.11, bf16[2048,256]{1,0:T(8,128)(2,1)S(1)} %copy-done.13, bf16[2048,256]{1,0:T(8,128)(2,1)} %copy-done.14, ...), custom_call_target="tpu_custom_call" | custom-call | flops 13421772800 | bytes 5242880 | tf_op jit(solution)/shard_map/attend_back/pallas_call | solution.py:189
  402.5 19.1 %attend_back.2 = (f32[2048,128]{1,0:T(8,128)S(1)}, f32[2048,128]{1,0:T(8,128)S(1)}, f32[2048,128]{1,0:T(8,128)S(1)}) custom-call(s32[4]{0:T(128)S(1)} %slice.245.first_ref, s32[4]{0:T(128)S(1)} %slice.246.last_ref, bf16[2048,256]{1,0:T(8,128)(2,1)S(1)} %copy-done.11, bf16[2048,256]{1,0:T(8,128)(2,1)S(1)} %copy-done.13, bf16[2048,256]{1,0:T(8,128)(2,1)} %copy-done.14, ...), custom_call_target="tpu_custom_call" | custom-call | flops 13421772800 | bytes 5242880 | tf_op jit(solution)/shard_map/attend_back/pallas_call | solution.py:189
  421.7 14.9 %project_back.1 = (bf16[2048,512]{1,0:T(8,128)(2,1)}, bf16[2048,512]{1,0:T(8,128)(2,1)}, bf16[2048,512]{1,0:T(8,128)(2,1)}, f32[2048,128]{1,0:T(8,128)S(1)}, f32...) custom-call(f32[2048,128]{1,0:T(8,128)S(1)} %get-tuple-element.51.refs_0_, ...), custom_call_target="tpu_custom_call" | custom-call | flops 2147483648 | bytes 17825792 | tf_op jit(solution)/shard_map/project_back/pallas_call | solution.py:371
  453.8 3.6 pad_maximum_fusion.7
  458.2 2.3 convert_add_fusion
  461.6 135.1 %ring_sum.1 = (bf16[2,8,64,2816]{3,2,1,0:T(8,128)(2,1)}, bf16[1,8,64,512]{3,2,1,0:T(8,128)(2,1)}, f32[24,128]{1,0:T(8,128)}, bf16[1024,512]{1,0:T(8,128)(2,1)}, f32[1024,128]{1,0:T(8,128)}) custom-call(bf16[8,64,2816]{2,1,0:T(8,128)(2,1)} %bitcast.66, bf16[8,64,2816]{2,1,0:T(8,128)(2,1)} %bitcast.65, bf16[8,64,512]{2,1,0:T(8,128)(2,1)} %bitcast.73, ...), custom_call_target="tpu_custom_call" | custom-call | flops 12582912 | bytes 188743680 | tf_op jit(solution)/shard_map/ring_sum/pallas_call | solution.py:581
  596.7 3.3 fusion.65
  607.3 2.9 fusion.6
  614.2 2.5 maximum_convert_fusion.1
  616.7 2.5 maximum_convert_fusion
  (309 shorter events, 92.0 us)
Async XLA Ops:
  7.2 186.4 %all-gather.3.cloned.1.call-start = ((), (), s32[]{:S(2)}) async-start(), calls=%async_computation | async-start | bytes 2654208 | tf_op jit(solution)/shard_map/all_gather | solution.py:641
  11.2 75.7 %collective-permute-start.3 = (bf16[512,512]{1,0:T(8,128)(2,1)}, bf16[512,512]{1,0:T(8,128)(2,1)}, u32[]{:S(2)}, u32[]{:S(2)}) collective-permute-start(bf16[512,512]{1,0:T(8,128)(2,1)} %pad_maximum_fusion.18), channel_id=1, source_target_pairs={{0,2},{2,0},{1,3},{3,1},{4,6},{6,4},{5,7},{7,5},{8,10},{10,8},{9,1... | collective-permute-start | bytes 1572872 | tf_op jit(solution)/shard_map/ppermute | solution.py:405
  14.2 34.7 %collective-permute-start = (bf16[1024,512]{1,0:T(8,128)(2,1)S(1)}, bf16[1024,512]{1,0:T(8,128)(2,1)}, u32[]{:S(2)}, u32[]{:S(2)}) collective-permute-start(bf16[1024,512]{1,0:T(8,128)(2,1)S(1)} %constant_dynamic-slice_fusion.26), channel_id=1, source_target_pairs={{0,2},{2,0},{1,3},{3,1},{4,6},{6,4},{5,7},{7,5},{8,10},{10,8},{9,1... | collective-permute-start | bytes 3145736 | tf_op jit(solution)/shard_map/ppermute | solution.py:405
  14.3 64.5 %collective-permute-start.2 = (f32[2,512]{1,0:T(2,128)S(1)}, f32[2,512]{1,0:T(2,128)S(1)}, u32[]{:S(2)}, u32[]{:S(2)}) collective-permute-start(f32[2,512]{1,0:T(2,128)S(1)} %pad_maximum_fusion.26), channel_id=1, source_target_pairs={{0,2},{2,0},{1,3},{3,1},{4,6},{6,4},{5,7},{7,5},{8,10},{10,8},{9,1... | collective-permute-start | bytes 12296 | tf_op jit(solution)/shard_map/ppermute | solution.py:405
  51.4 15.7 %copy-start.54 = (bf16[512,512]{1,0:T(8,128)(2,1)S(1)}, bf16[512,512]{1,0:T(8,128)(2,1)}, u32[]{:S(2)}) copy-start(bf16[512,512]{1,0:T(8,128)(2,1)} %param.19) | copy-start | bytes 1572868
  51.4 13.2 %collective-permute-start.6 = (bf16[64,2304]{1,0:T(8,128)(2,1)S(1)}, bf16[64,2304]{1,0:T(8,128)(2,1)}, u32[]{:S(2)}, u32[]{:S(2)}) collective-permute-start(bf16[64,2304]{1,0:T(8,128)(2,1)S(1)} %fusion.44), channel_id=1, source_target_pairs={{0,2},{2,0},{1,3},{3,1},{4,6},{6,4},{5,7},{7,5},{8,10},{10,8},{9,1... | collective-permute-start | bytes 884744 | tf_op jit(solution)/shard_map/ppermute | solution.py:405
  54.2 8.6 %collective-permute-start.7 = (bf16[144,512]{1,0:T(8,128)(2,1)S(1)}, bf16[144,512]{1,0:T(8,128)(2,1)S(1)}, u32[]{:S(2)}, u32[]{:S(2)}) collective-permute-start(bf16[144,512]{1,0:T(8,128)(2,1)S(1)} %dynamic-slice_select_fusion), channel_id=1, source_target_pairs={{0,2},{2,0},{1,3},{3,1},{4,6},{6,4},{5,7},{7,5},{8,10},{10,8},{9,1... | collective-permute-start | bytes 442376 | tf_op jit(solution)/shard_map/ppermute | solution.py:405
  54.5 28.1 %collective-permute-start.1 = (bf16[1024,512]{1,0:T(8,128)(2,1)}, bf16[1024,512]{1,0:T(8,128)(2,1)}, u32[]{:S(2)}, u32[]{:S(2)}) collective-permute-start(bf16[1024,512]{1,0:T(8,128)(2,1)} %collective-permute-done), channel_id=1, source_target_pairs={{0,1},{1,0},{2,3},{3,2},{4,5},{5,4},{6,7},{7,6},{8,9},{9,8},{10,11... | collective-permute-start | bytes 3145736 | tf_op jit(solution)/shard_map/ppermute | solution.py:405
  68.2 12.6 %collective-permute-start.8 = (bf16[512,512]{1,0:T(8,128)(2,1)}, bf16[512,512]{1,0:T(8,128)(2,1)}, u32[]{:S(2)}, u32[]{:S(2)}) collective-permute-start(bf16[512,512]{1,0:T(8,128)(2,1)} %get-tuple-element.131), channel_id=1, source_target_pairs={{0,2},{2,0},{1,3},{3,1},{4,6},{6,4},{5,7},{7,5},{8,10},{10,8},{9,1... | collective-permute-start | bytes 1572872 | tf_op jit(solution)/shard_map/ppermute | solution.py:405
  78.9 144.3 %all-gather.5.cloned.1.call-start = ((), (), s32[]{:S(2)}) async-start(), calls=%async_computation.1 | async-start | bytes 1327104 | tf_op jit(solution)/shard_map/all_gather | solution.py:641
  82.7 48.0 %collective-permute-start.9 = (bf16[512,1024]{1,0:T(8,128)(2,1)}, bf16[512,1024]{1,0:T(8,128)(2,1)}, u32[]{:S(2)}, u32[]{:S(2)}) collective-permute-start(bf16[512,1024]{1,0:T(8,128)(2,1)} %constant_dynamic-update-slice_fusion), channel_id=1, source_target_pairs={{0,1},{1,0},{2,3},{3,2},{4,5},{5,4},{6,7},{7,6},{8,9},{9,8},{10,11... | collective-permute-start | bytes 3145736 | tf_op jit(solution)/shard_map/ppermute | solution.py:405
  86.9 13.5 %copy-start.8 = (s32[2048,1]{1,0:T(8,128)S(1)}, s32[2048,1]{1,0:T(8,128)}, u32[]{:S(2)}) copy-start(s32[2048,1]{1,0:T(8,128)} %copy.38.start_ref) | copy-start | bytes 24580
  100.4 11.6 %copy-start.10 = (bf16[2048,256]{1,0:T(8,128)(2,1)}, bf16[2048,256]{1,0:T(8,128)(2,1)S(1)}, u32[]{:S(2)}) copy-start(bf16[2048,256]{1,0:T(8,128)(2,1)S(1)} %get-tuple-element.44.q_ref) | copy-start | bytes 3145732
  100.4 11.6 %copy-start.12 = (bf16[2048,256]{1,0:T(8,128)(2,1)}, bf16[2048,256]{1,0:T(8,128)(2,1)S(1)}, u32[]{:S(2)}) copy-start(bf16[2048,256]{1,0:T(8,128)(2,1)S(1)} %get-tuple-element.45.k_ref) | copy-start | bytes 3145732
  100.4 11.6 %copy-start.14 = (bf16[2048,256]{1,0:T(8,128)(2,1)}, bf16[2048,256]{1,0:T(8,128)(2,1)S(1)}, u32[]{:S(2)}) copy-start(bf16[2048,256]{1,0:T(8,128)(2,1)S(1)} %get-tuple-element.46.v_ref) | copy-start | bytes 3145732
  111.3 11.6 %copy-start.15 = (f32[2048,128]{1,0:T(8,128)}, f32[2048,128]{1,0:T(8,128)S(1)}, u32[]{:S(2)}) copy-start(f32[2048,128]{1,0:T(8,128)S(1)} %get-tuple-element.49.raw_ref) | copy-start | bytes 3145732
  111.4 28.4 %copy-start.46 = (bf16[1024,128]{1,0:T(8,128)(2,1)}, bf16[1024,128]{1,0:T(8,128)(2,1)S(1)}, u32[]{:S(2)}) copy-start(bf16[1024,128]{1,0:T(8,128)(2,1)S(1)} %get-tuple-element.127) | copy-start | bytes 786436
  111.4 12.6 %collective-permute-start.4 = (bf16[1024,128]{1,0:T(8,128)(2,1)S(1)}, bf16[1024,128]{1,0:T(8,128)(2,1)S(1)}, u32[]{:S(2)}, u32[]{:S(2)}) collective-permute-start(bf16[1024,128]{1,0:T(8,128)(2,1)S(1)} %get-tuple-element.128), channel_id=1, source_target_pairs={{0,1},{1,0},{2,3},{3,2},{4,5},{5,4},{6,7},{7,6},{8,9},{9,8},{10,11... | collective-permute-start | bytes 786440 | tf_op jit(solution)/shard_map/ppermute | solution.py:405
  124.0 2.2 collective-permute-start.10
  124.8 14.9 %collective-permute-start.5 = (bf16[1024,256]{1,0:T(8,128)(2,1)S(1)}, bf16[1024,256]{1,0:T(8,128)(2,1)}, u32[]{:S(2)}, u32[]{:S(2)}) collective-permute-start(bf16[1024,256]{1,0:T(8,128)(2,1)S(1)} %pad_maximum_fusion.19), channel_id=1, source_target_pairs={{0,2},{2,0},{1,3},{3,1},{4,6},{6,4},{5,7},{7,5},{8,10},{10,8},{9,1... | collective-permute-start | bytes 1572872 | tf_op jit(solution)/shard_map/ppermute | solution.py:405
  127.2 12.6 %copy-start.59 = (bf16[1024,128]{1,0:T(8,128)(2,1)S(1)}, bf16[1024,128]{1,0:T(8,128)(2,1)}, u32[]{:S(2)}) copy-start(bf16[1024,128]{1,0:T(8,128)(2,1)} %copy-done.58) | copy-start | bytes 786436
  127.2 23.1 %collective-permute-start.11 = (bf16[1024,256]{1,0:T(8,128)(2,1)S(1)}, bf16[1024,256]{1,0:T(8,128)(2,1)S(1)}, u32[]{:S(2)}, u32[]{:S(2)}) collective-permute-start(bf16[1024,256]{1,0:T(8,128)(2,1)S(1)} %pad_maximum_fusion.20), channel_id=1, source_target_pairs={{0,2},{2,0},{1,3},{3,1},{4,6},{6,4},{5,7},{7,5},{8,10},{10,8},{9,1... | collective-permute-start | bytes 1572872 | tf_op jit(solution)/shard_map/ppermute | solution.py:405
  139.8 10.6 %copy-start.26 = (bf16[1024,512]{1,0:T(8,128)(2,1)S(1)}, bf16[1024,512]{1,0:T(8,128)(2,1)}, u32[]{:S(2)}) copy-start(bf16[1024,512]{1,0:T(8,128)(2,1)} %copy-done.25) | copy-start | bytes 3145732
  139.8 10.6 %copy-start.49 = (bf16[1024,128]{1,0:T(8,128)(2,1)S(1)}, bf16[1024,128]{1,0:T(8,128)(2,1)}, u32[]{:S(2)}) copy-start(bf16[1024,128]{1,0:T(8,128)(2,1)} %copy-done.48) | copy-start | bytes 786436
  156.2 37.4 %collective-permute-start.12 = (bf16[1024,1024]{1,0:T(8,128)(2,1)}, bf16[1024,1024]{1,0:T(8,128)(2,1)}, u32[]{:S(2)}, u32[]{:S(2)}) collective-permute-start(bf16[1024,1024]{1,0:T(8,128)(2,1)} %multiply_convert_fusion.6), channel_id=1, source_target_pairs={{0,1},{1,0},{2,3},{3,2},{4,5},{5,4},{6,7},{7,6},{8,9},{9,8},{10,11... | collective-permute-start | bytes 6291464 | tf_op jit(solution)/shard_map/ppermute | solution.py:405
  156.9 25.3 %collective-permute-start.16 = (bf16[1024,512]{1,0:T(8,128)(2,1)S(1)}, bf16[1024,512]{1,0:T(8,128)(2,1)S(1)}, u32[]{:S(2)}, u32[]{:S(2)}) collective-permute-start(bf16[1024,512]{1,0:T(8,128)(2,1)S(1)} %get-tuple-element.79), channel_id=1, source_target_pairs={{0,2},{2,0},{1,3},{3,1},{4,6},{6,4},{5,7},{7,5},{8,10},{10,8},{9,1... | collective-permute-start | bytes 3145736 | tf_op jit(solution)/shard_map/ppermute | solution.py:405
  184.7 38.4 %collective-permute-start.17 = (bf16[1024,1024]{1,0:T(8,128)(2,1)}, bf16[1024,1024]{1,0:T(8,128)(2,1)}, u32[]{:S(2)}, u32[]{:S(2)}) collective-permute-start(bf16[1024,1024]{1,0:T(8,128)(2,1)} %pad_maximum_fusion.10), channel_id=1, source_target_pairs={{0,1},{1,0},{2,3},{3,2},{4,5},{5,4},{6,7},{7,6},{8,9},{9,8},{10,11... | collective-permute-start | bytes 6291464 | tf_op jit(solution)/shard_map/ppermute | solution.py:405
  184.7 251.9 %all-reduce.2.cloned.1.call-start = ((), (), s32[]{:S(2)}) async-start(), calls=%async_computation.2 | async-start | bytes 4718592 | tf_op jit(solution)/shard_map/psum | solution.py:710
  193.6 29.6 %copy-start.44 = (bf16[1152,512]{1,0:T(8,128)(2,1)S(1)}, bf16[1152,512]{1,0:T(8,128)(2,1)}, u32[]{:S(2)}) copy-start(bf16[1152,512]{1,0:T(8,128)(2,1)} %constant_dynamic-slice_fusion.8) | copy-start | bytes 3538948
  223.1 9.0 %copy-start.67 = (bf16[1152,512]{1,0:T(8,128)(2,1)S(1)}, bf16[1152,512]{1,0:T(8,128)(2,1)}, u32[]{:S(2)}) copy-start(bf16[1152,512]{1,0:T(8,128)(2,1)} %all-gather.5.cloned.1.call-done) | copy-start | bytes 3538948
  236.9 79.2 %collective-permute-start.13 = (bf16[1024,1024]{1,0:T(8,128)(2,1)}, bf16[1024,1024]{1,0:T(8,128)(2,1)}, u32[]{:S(2)}, u32[]{:S(2)}) collective-permute-start(bf16[1024,1024]{1,0:T(8,128)(2,1)} %convolution_convert_fusion), channel_id=1, source_target_pairs={{0,1},{1,0},{2,3},{3,2},{4,5},{5,4},{6,7},{7,6},{8,9},{9,8},{10,11... | collective-permute-start | bytes 6291464 | tf_op jit(solution)/shard_map/ppermute | solution.py:405
  243.4 15.2 %copy-start.34 = (bf16[1024,512]{1,0:T(8,128)(2,1)S(1)}, bf16[1024,512]{1,0:T(8,128)(2,1)}, u32[]{:S(2)}) copy-start(bf16[1024,512]{1,0:T(8,128)(2,1)} %copy-done.33) | copy-start | bytes 3145732
  243.4 51.8 %collective-permute-start.18 = (bf16[1024,1024]{1,0:T(8,128)(2,1)}, bf16[1024,1024]{1,0:T(8,128)(2,1)S(1)}, u32[]{:S(2)}, u32[]{:S(2)}) collective-permute-start(bf16[1024,1024]{1,0:T(8,128)(2,1)} %fusion.14), channel_id=1, source_target_pairs={{0,1},{1,0},{2,3},{3,2},{4,5},{5,4},{6,7},{7,6},{8,9},{9,8},{10,11... | collective-permute-start | bytes 6291464 | tf_op jit(solution)/shard_map/ppermute | solution.py:405
  305.9 26.2 %collective-permute-start.19 = (bf16[1024,512]{1,0:T(8,128)(2,1)}, bf16[1024,512]{1,0:T(8,128)(2,1)S(1)}, u32[]{:S(2)}, u32[]{:S(2)}) collective-permute-start(bf16[1024,512]{1,0:T(8,128)(2,1)} %get-tuple-element.105), channel_id=1, source_target_pairs={{0,2},{2,0},{1,3},{3,1},{4,6},{6,4},{5,7},{7,5},{8,10},{10,8},{9,1... | collective-permute-start | bytes 3145736 | tf_op jit(solution)/shard_map/ppermute | solution.py:405
  307.4 47.3 %collective-permute-start.20 = (bf16[1024,512]{1,0:T(8,128)(2,1)}, bf16[1024,512]{1,0:T(8,128)(2,1)}, u32[]{:S(2)}, u32[]{:S(2)}) collective-permute-start(bf16[1024,512]{1,0:T(8,128)(2,1)} %get-tuple-element.106), channel_id=1, source_target_pairs={{0,2},{2,0},{1,3},{3,1},{4,6},{6,4},{5,7},{7,5},{8,10},{10,8},{9,1... | collective-permute-start | bytes 3145736 | tf_op jit(solution)/shard_map/ppermute | solution.py:405
  316.2 38.5 %copy-start.18 = (f32[1024,1024]{1,0:T(8,128)S(1)}, f32[1024,1024]{1,0:T(8,128)}, u32[]{:S(2)}) copy-start(f32[1024,1024]{1,0:T(8,128)} %copy-done.17) | copy-start | bytes 12582916
  316.2 38.5 %copy-start.20 = (f32[1024,1024]{1,0:T(8,128)S(1)}, f32[1024,1024]{1,0:T(8,128)}, u32[]{:S(2)}) copy-start(f32[1024,1024]{1,0:T(8,128)} %get-tuple-element.151) | copy-start | bytes 12582916
  322.4 32.3 %copy-start.30 = (bf16[1024,1024]{1,0:T(8,128)(2,1)S(1)}, bf16[1024,1024]{1,0:T(8,128)(2,1)}, u32[]{:S(2)}) copy-start(bf16[1024,1024]{1,0:T(8,128)(2,1)} %copy-done.29) | copy-start | bytes 6291460
  324.3 51.9 %collective-permute-start.14 = (bf16[1024,512]{1,0:T(8,128)(2,1)S(1)}, bf16[1024,512]{1,0:T(8,128)(2,1)S(1)}, u32[]{:S(2)}, u32[]{:S(2)}) collective-permute-start(bf16[1024,512]{1,0:T(8,128)(2,1)S(1)} %slice.427), channel_id=1, source_target_pairs={{0,2},{2,0},{1,3},{3,1},{4,6},{6,4},{5,7},{7,5},{8,10},{10,8},{9,1... | collective-permute-start | bytes 3145736 | tf_op jit(solution)/shard_map/ppermute | solution.py:405
  362.8 18.7 %collective-permute-start.21 = (bf16[1024,1024]{1,0:T(8,128)(2,1)S(1)}, bf16[1024,1024]{1,0:T(8,128)(2,1)S(1)}, u32[]{:S(2)}, u32[]{:S(2)}) collective-permute-start(bf16[1024,1024]{1,0:T(8,128)(2,1)S(1)} %get-tuple-element.77), channel_id=1, source_target_pairs={{0,1},{1,0},{2,3},{3,2},{4,5},{5,4},{6,7},{7,6},{8,9},{9,8},{10,11... | collective-permute-start | bytes 6291464 | tf_op jit(solution)/shard_map/ppermute | solution.py:405
  366.5 11.2 %collective-permute-start.23 = (bf16[512,512]{1,0:T(8,128)(2,1)S(1)}, bf16[512,512]{1,0:T(8,128)(2,1)S(1)}, u32[]{:S(2)}, u32[]{:S(2)}) collective-permute-start(bf16[512,512]{1,0:T(8,128)(2,1)S(1)} %pad_maximum_fusion.21), channel_id=1, source_target_pairs={{0,1},{1,0},{2,3},{3,2},{4,5},{5,4},{6,7},{7,6},{8,9},{9,8},{10,11... | collective-permute-start | bytes 1572872 | tf_op jit(solution)/shard_map/ppermute | solution.py:405
  367.1 9.8 %copy-start.38 = (bf16[512,1024]{1,0:T(8,128)(2,1)S(1)}, bf16[512,1024]{1,0:T(8,128)(2,1)}, u32[]{:S(2)}) copy-start(bf16[512,1024]{1,0:T(8,128)(2,1)} %constant_dynamic-update-slice_fusion) | copy-start | bytes 3145732
  376.8 2.7 collective-permute-start.15
  402.5 19.2 %copy-start.3 = (bf16[512,512]{1,0:T(8,128)(2,1)S(1)}, bf16[512,512]{1,0:T(8,128)(2,1)}, u32[]{:S(2)}) copy-start(bf16[512,512]{1,0:T(8,128)(2,1)} %pad_maximum_fusion.17.w_near_ref.refs_11_) | copy-start | bytes 1572868
  440.1 165.5 %collective-permute-start.26 = (bf16[1152,512]{1,0:T(8,128)(2,1)}, bf16[1152,512]{1,0:T(8,128)(2,1)}, u32[]{:S(2)}, u32[]{:S(2)}) collective-permute-start(bf16[1152,512]{1,0:T(8,128)(2,1)} %get-tuple-element.100), channel_id=1, source_target_pairs={{0,2},{2,0},{1,3},{3,1},{4,6},{6,4},{5,7},{7,5},{8,10},{10,8},{9,1... | collective-permute-start | bytes 3538952 | tf_op jit(solution)/shard_map/ppermute | solution.py:405
  441.7 15.7 %collective-permute-start.24 = (f32[1024,128]{1,0:T(8,128)S(1)}, f32[1024,128]{1,0:T(8,128)S(1)}, u32[]{:S(2)}, u32[]{:S(2)}) collective-permute-start(f32[1024,128]{1,0:T(8,128)S(1)} %constant_dynamic-slice_fusion.5), channel_id=1, source_target_pairs={{0,1},{1,0},{2,3},{3,2},{4,5},{5,4},{6,7},{7,6},{8,9},{9,8},{10,11... | collective-permute-start | bytes 1572872 | tf_op jit(solution)/shard_map/ppermute | solution.py:405
  445.1 13.1 %collective-permute-start.22 = (bf16[1024,1024]{1,0:T(8,128)(2,1)}, bf16[1024,1024]{1,0:T(8,128)(2,1)}, u32[]{:S(2)}, u32[]{:S(2)}) collective-permute-start(bf16[1024,1024]{1,0:T(8,128)(2,1)} %constant_dynamic-slice_fusion.6), channel_id=1, source_target_pairs={{0,1},{1,0},{2,3},{3,2},{4,5},{5,4},{6,7},{7,6},{8,9},{9,8},{10,11... | collective-permute-start | bytes 6291464 | tf_op jit(solution)/shard_map/ppermute | solution.py:405
  603.7 15.5 %collective-permute-start.25 = (bf16[1024,512]{1,0:T(8,128)(2,1)S(1)}, bf16[1024,512]{1,0:T(8,128)(2,1)S(1)}, u32[]{:S(2)}, u32[]{:S(2)}) collective-permute-start(bf16[1024,512]{1,0:T(8,128)(2,1)S(1)} %fusion.7), channel_id=1, source_target_pairs={{0,1},{1,0},{2,3},{3,2},{4,5},{5,4},{6,7},{7,6},{8,9},{9,8},{10,11... | collective-permute-start | bytes 3145736 | tf_op jit(solution)/shard_map/ppermute | solution.py:405
  (62 other events, 280.8 us)
Sparse Core Ops, SparseCore 0:
  79.0 52.3 all-gather.2
  184.9 38.2 all-gather.4
  315.0 107.4 all-reduce.1

commit v4 on v2

--- a/solution.py
+++ b/solution.py
@@ -12,6 +12,7 @@
 EPSILON = 1e-05
 ROPE_BASE = 1000000.0
 F32, BF16 = jnp.float32, jnp.bfloat16
+MESH = pl.DeviceIdType.MESH
 
 
 def dot(a, b, dims=(((1,), (0,)), ((), ()))):
@@ -106,102 +107,6 @@
         name="attend",
     )(first, last, q, k, v, starts[:, None])
 
-def attend_back_kernel(b, T, first_ref, last_ref, q_ref, k_ref, v_ref, grad_ref, raw_ref, lse_ref, start_ref,
-                       dq_ref, dk_ref, dv_ref, qs_ref, gs_ref, stat_ref, dqt_ref, dk_acc, dv_acc):
-    j = pl.program_id(1)
-    blocks = T // b
-
-    @pl.when(j == 0)
-    def _():
-        dqt_ref[...] = jnp.zeros_like(dqt_ref)
-        for i in range(blocks):
-            rows = slice(i * b, (i + 1) * b)
-            both = slice(i * 2 * b, (i + 1) * 2 * b)
-            qs_ref[both, :] = stacked(q_ref[rows, :])
-            grad = grad_ref[rows, :]
-            gs_ref[both, :] = stacked(grad)
-            prod = (grad.astype(F32) * raw_ref[rows, :]).T
-            stat_ref[i, 0:1, 0:b] = lse_ref[0, 0:1, rows]
-            stat_ref[i, 0:1, b:2 * b] = lse_ref[0, 1:2, rows]
-            stat_ref[i, 1:2, 0:b] = jnp.sum(prod[:64], axis=0, keepdims=True)
-            stat_ref[i, 1:2, b:2 * b] = jnp.sum(prod[64:], axis=0, keepdims=True)
-
-    k = k_ref[...]
-    v = v_ref[...]
-    kt = k.T[:64]
-    dk_acc[...] = jnp.zeros_like(dk_acc)
-    dv_acc[...] = jnp.zeros_like(dv_acc)
-    keys = j * b + lax.broadcasted_iota(jnp.int32, (b, 1), 0)
-
-    def step(i, masked):
-        at = pl.ds(pl.multiple_of(i * 2 * b, 2 * b), 2 * b)
-        qs = qs_ref[at, :]
-        gs = gs_ref[at, :]
-        st = dot(k, qs, NT)
-        pt = jnp.exp(st - stat_ref[i, 0:1, :])
-        if masked:
-            cols = i * b + lax.rem(lax.broadcasted_iota(jnp.int32, (1, 2 * b), 1), b)
-            begin = start_ref[0:1, pl.ds(pl.multiple_of(i * b, b), b)]
-            begin = jnp.concatenate([begin, begin], axis=1)
-            pt = jnp.where((keys <= cols) & (keys >= begin), pt, 0.0)
-        dv_acc[...] += dot(pt.astype(BF16), gs)
-        dpt = dot(v, gs, NT)
-        dst = (pt * (dpt - stat_ref[i, 1:2, :])).astype(BF16)
-        dk_acc[...] += dot(dst, qs)
-        part = dot(kt, dst)
-        to = pl.ds(pl.multiple_of(i * b, b), b)
-        dqt_ref[0:64, to] += part[:, :b]
-        dqt_ref[64:128, to] += part[:, b:]
-
-    step(j, True)
-
-    @pl.loop(j + 1, blocks)
-    def _(i):
-        whole = last_ref[i] <= j * b
-        none = first_ref[i] >= (j + 1) * b
-
-        @pl.when(whole)
-        def _():
-            step(i, False)
-
-        @pl.when(jnp.logical_not(whole | none))
-        def _():
-            step(i, True)
-
-    dk = dk_acc[...]
-    dv = dv_acc[...]
-    dk_ref[...] = dk + pltpu.roll(dk, 64, 1)
-    dv_ref[...] = dv + pltpu.roll(dv, 64, 1)
-    dq_ref[...] = dqt_ref[:, pl.ds(pl.multiple_of(j * b, b), b)].T * 0.125
-
-def attend_back(q, k, v, grad, raw, lse, starts, b=512):
-    T, width = q.shape
-    groups = width // 128
-    first, last = starts[::b], starts[b - 1::b]
-    blocks = T // b
-    col = pl.BlockSpec((T, 128), lambda g, j, *_: (0, g))
-    blk = pl.BlockSpec((b, 128), lambda g, j, *_: (j, g))
-    out = jax.ShapeDtypeStruct((T, width), F32)
-    pairs = T * (T + b) // 2
-    return pl.pallas_call(
-        functools.partial(attend_back_kernel, b, T),
-        out_shape=(out, out, out),
-        grid_spec=pltpu.PrefetchScalarGridSpec(
-            num_scalar_prefetch=2, grid=(groups, blocks),
-            in_specs=[col, blk, blk, col, col,
-                      pl.BlockSpec((1, 2, T), lambda g, j, *_: (g, 0, 0)),
-                      pl.BlockSpec((1, T), lambda g, j, *_: (0, 0))],
-            out_specs=[blk, blk, blk],
-            scratch_shapes=[pltpu.VMEM((2 * T, 128), BF16), pltpu.VMEM((2 * T, 128), BF16),
-                            pltpu.VMEM((blocks, 2, 2 * b), F32), pltpu.VMEM((128, T), F32),
-                            pltpu.VMEM((b, 128), F32), pltpu.VMEM((b, 128), F32)],
-        ),
-        compiler_params=pltpu.CompilerParams(vmem_limit_bytes=48 << 20),
-        cost_estimate=pl.CostEstimate(flops=10 * groups * 2 * pairs * 256, transcendentals=2 * groups * pairs,
-                                      bytes_accessed=20 * T * width),
-        name="attend_back",
-    )(first, last, q, k, v, grad, raw, lse, starts[None, :])
-
 
 def head_sums(x):
     first = lax.broadcasted_iota(jnp.int32, x.shape, 1) < HEAD_SIZE
@@ -314,16 +219,12 @@
         q_sum_ref[...] += total
         grads.append(part.astype(BF16))
     for n in range(groups // 2):
-        one = slice(2 * n * lanes, (2 * n + 1) * lanes)
-        two = slice((2 * n + 1) * lanes, (2 * n + 2) * lanes)
         at = groups * lanes + n * lanes
-        part, total = back(jnp.where(first, dk_ref[:, one], dk_ref[:, two]), raw_ref[:, at:at + lanes], k_gain_ref[...])
+        part, total = back(jnp.where(first, dk_ref[:, 2 * n * lanes:(2 * n + 1) * lanes], dk_ref[:, (2 * n + 1) * lanes:(2 * n + 2) * lanes]), raw_ref[:, at:at + lanes], k_gain_ref[...])
         k_sum_ref[...] += total
         grads.append(part.astype(BF16))
     for n in range(groups // 2):
-        one = slice(2 * n * lanes, (2 * n + 1) * lanes)
-        two = slice((2 * n + 1) * lanes, (2 * n + 2) * lanes)
-        grads.append(jnp.where(first, dv_ref[:, one], dv_ref[:, two]).astype(BF16))
+        grads.append(jnp.where(first, dv_ref[:, 2 * n * lanes:(2 * n + 1) * lanes], dv_ref[:, (2 * n + 1) * lanes:(2 * n + 2) * lanes]).astype(BF16))
     grads = jnp.concatenate(grads, axis=1)
     grads_ref[...] = grads
     to_near = dot(grads, w_near_ref[...], NT)
@@ -340,7 +241,7 @@
     near_sum_ref[...] += jnp.sum(near, axis=0, keepdims=True)
     far_sum_ref[...] += jnp.sum(far, axis=0, keepdims=True)
     stat = jnp.sum(near * gain_near_ref[...], axis=1, keepdims=True) + jnp.sum(far * gain_far_ref[...], axis=1, keepdims=True)
-    stat_ref[...] = jnp.broadcast_to(stat, stat_ref.shape)
+    stat_ref[...] = jnp.where(first, stat, inverse)
 
 
 def project_back(dq, dk, dv, raw, near, far, gain_near, gain_far, w_near, w_far, q_gain, k_gain, cosine, sine, rows=512):
@@ -369,7 +270,7 @@
         out_shape=(out(columns, BF16), out(half, BF16), out(half, BF16), out(lanes, F32), out(lanes, F32, 1), out(lanes, F32, 1),
                    out(half, F32, 1), out(half, F32, 1)),
         grid=(packed // rows,),
-        in_specs=[tile(width), tile(width), tile(width), tile(raw.shape[1]), tile(half), tile(half), *map(whole, small),
+        in_specs=[tile(width)] * 3 + [tile(raw.shape[1]), tile(half), tile(half), *map(whole, small),
                   tile(lanes), tile(lanes)],
         out_specs=(tile(columns), tile(half), tile(half), tile(lanes), kept(lanes), kept(lanes), kept(half), kept(half)),
         compiler_params=pltpu.CompilerParams(vmem_limit_bytes=44 << 20),
@@ -412,6 +313,581 @@
 
 def over_t(left, right):
     return dot(left, right, (((0,), (0,)), ((), ())))
+
+
+def feed_kernel(units, hidden_ref, cot_near_ref, cot_far_ref, gate_up_ref, down_ref, active_ref, grads_ref, result_ref, back_ref):
+    half = cot_near_ref.shape[1]
+    hidden = hidden_ref[...]
+    gate = dot(hidden, gate_up_ref[:, :units])
+    upward = dot(hidden, gate_up_ref[:, units:])
+    grad_active = dot(cot_near_ref[...], down_ref[:, :half], NT) + dot(cot_far_ref[...], down_ref[:, half:], NT)
+    sig = 1.0 / (1.0 + jnp.exp(-gate))
+    lifted = gate * sig
+    active = (lifted * upward).astype(BF16)
+    grad_gate = (grad_active * upward * (sig * (1.0 + gate * (1.0 - sig)))).astype(BF16)
+    grad_up = (grad_active * lifted).astype(BF16)
+    active_ref[...] = active
+    grads_ref[:, :units] = grad_gate
+    grads_ref[:, units:] = grad_up
+    result_ref[...] = dot(active, down_ref[...]).astype(BF16)
+    back = dot(grad_gate, gate_up_ref[:, :units], NT) + dot(grad_up, gate_up_ref[:, units:], NT)
+    back_ref[...] = back.astype(BF16)
+
+
+def feed(hidden, cot_near, cot_far, gate_up, down, rows=256):
+    packed, width = hidden.shape
+    units = down.shape[0]
+    rows = min(rows, packed)
+
+    def tile(n):
+        return pl.BlockSpec((rows, n), lambda i: (i, 0))
+
+    def whole(x):
+        return pl.BlockSpec(x.shape, lambda i: (0, 0), pipeline_mode=pl.Buffered(1))
+
+    def out(n):
+        return jax.ShapeDtypeStruct((packed, n), BF16)
+
+    return pl.pallas_call(
+        functools.partial(feed_kernel, units),
+        out_shape=(out(units), out(2 * units), out(width), out(width)),
+        grid=(packed // rows,),
+        in_specs=[tile(width), tile(width // 2), tile(width // 2), whole(gate_up), whole(down)],
+        out_specs=(tile(units), tile(2 * units), tile(width), tile(width)),
+        compiler_params=pltpu.CompilerParams(vmem_limit_bytes=56 << 20),
+        cost_estimate=pl.CostEstimate(flops=12 * packed * width * units, transcendentals=packed * units,
+                                      bytes_accessed=packed * (8 * width + 6 * units) + 6 * width * units),
+        name="feed",
+    )(hidden, cot_near, cot_far, gate_up, down)
+
+
+class Group:
+    def __init__(self, names, n):
+        self.n = n
+        self.dp, self.row, self.col = (lax.axis_index(name) for name in names)
+        side = self.dp % 2
+        self.place = (self.dp // 2) * (1 - side) + (n - 1 - self.dp // 2) * side
+        self.across = (self.dp, 1 - self.row, self.col)
+        self.beside = (self.dp, self.row, 1 - self.col)
+        self.opposite = (self.dp, 1 - self.row, 1 - self.col)
+        self.along = [((self.dp + k) % n, self.row, self.col) for k in range(1, n)]
+        self.ring = [(self.at(self.place + 1), self.row, self.col), (self.at(self.place - 1), self.row, self.col)]
+
+    def at(self, position):
+        position = (position + 2 * self.n) % self.n
+        back = position // (self.n // 2)
+        return (position * (1 - back) + (self.n - 1 - position) * back) * 2 + back
+
+    def arrive(self, targets):
+        barrier = pltpu.get_barrier_semaphore()
+        for target in targets:
+            pl.semaphore_signal(barrier, inc=1, device_id=target, device_id_type=MESH)
+        pl.semaphore_wait(barrier, len(targets))
+
+    def reduced(self, way, t):
+        return (self.place - t - 1 + 2 * self.n) % self.n if way == 0 else (self.place + t + 1) % self.n
+
+    def spread(self, way, t):
+        return (self.place - t + 2 * self.n) % self.n if way == 0 else (self.place + t) % self.n
+
+    def own(self, way):
+        return (self.place + 1) % self.n if way == 0 else (self.place + self.n - 1) % self.n
+
+
+def remote(src, dst, send, recv, target):
+    return pltpu.make_async_remote_copy(
+        src_ref=src, dst_ref=dst, send_sem=send, recv_sem=recv, device_id=target, device_id_type=MESH)
+
+
+class Reduce:
+    def __init__(self, me, parts, slots, send, recv):
+        self.me, self.parts, self.slots, self.send, self.recv = me, parts, slots, send, recv
+        self.columns = parts[0].shape[2] // 2
+
+    def local(self, s, chunk):
+        return self.parts[s // 2].at[chunk, :, pl.ds((s % 2) * self.columns, self.columns)]
+
+    def copy(self, s, t, src):
+        return remote(src, self.slots.at[s, t], self.send.at[s, t], self.recv.at[s, t], self.me.ring[s % 2])
+
+    def start(self):
+        for s in range(2 * len(self.parts)):
+            self.copy(s, 0, self.local(s, self.me.place)).start()
+
+    def step(self, t):
+        for s in range(2 * len(self.parts)):
+            slot = self.slots.at[s, t]
+            self.copy(s, t, slot).wait_recv()
+            slot[...] = (slot[...].astype(F32) + self.local(s, self.me.reduced(s % 2, t))[...].astype(F32)).astype(BF16)
+
+            @pl.when(t < self.me.n - 2)
+            def _():
+                self.copy(s, t + 1, slot).start()
+
+    def last(self, s):
+        return self.slots.at[s, self.me.n - 2]
+
+    def finish(self, t):
+        for s in range(2 * len(self.parts)):
+            self.copy(s, t, self.slots.at[s, t]).wait_send()
+
+
+class Spread:
+    def __init__(self, me, full, send, recv):
+        self.me, self.full, self.send, self.recv = me, full, send, recv
+        self.lone = len(full.shape) == 3
+        self.columns = full.shape[-1] // 2
+        self.streams = (0, 1) if self.lone else (2, 3, 0, 1)
+
+    def piece(self, s, chunk, quarter=None):
+        lanes = pl.ds((s % 2) * self.columns, self.columns)
+        if self.lone:
+            return self.full.at[chunk, :, lanes]
+        if quarter is None:
+            quarter = 1 - self.me.row if s < 2 else self.me.row
+        return self.full.at[quarter, chunk, :, lanes]
+
+    def copy(self, s, t, chunk, src=None):
+        piece = self.piece(s, chunk)
+        return remote(piece if src is None else src, piece, self.send.at[s, t], self.recv.at[s, t], self.me.ring[s % 2])
+
+    def start(self, s, src=None):
+        self.copy(s, 0, self.me.own(s % 2), src).start()
+
+    def step(self, t):
+        for s in self.streams:
+            chunk = self.me.spread(s % 2, t)
+            self.copy(s, t, chunk).wait_recv()
+
+            @pl.when(t < self.me.n - 2)
+            def _():
+                self.copy(s, t + 1, chunk).start()
+
+    def finish(self, t):
+        for s in self.streams:
+            self.copy(s, t, 0).wait_send()
+
+
+def steps(begin, end, *rings):
+    def step(t, carry):
+        for ring in rings:
+            ring.step(t)
+        return carry
+
+    lax.fori_loop(begin, end, step, 0)
+
+
+def finish(n, *rings):
+    def each(t, carry):
+        for ring in rings:
+            ring.finish(t)
+        return carry
+
+    lax.fori_loop(0, n - 1, each, 0)
+
+
+def turn_kernel(n, names, pieces, near_ref, far_ref, down_near_ref, down_far_ref, back_ref, middle_ref, cot_near_ref,
+                cot_far_ref, gain_ref, branch_ref, keep_ref, gain_sum_ref, done_ref, down_done_ref,
+                slots, down_slots, beside_in, across_out, across_in, rs_send, rs_recv, down_send, down_recv,
+                cross_send, cross_recv, beside_send, beside_recv, across_send, across_recv, branch_send, branch_recv):
+    me = Group(names, n)
+    me.arrive([*me.ring, me.across, me.beside])
+    half = cot_near_ref.shape[1]
+    tokens = middle_ref.shape[0]
+    rows = tokens // pieces
+    wide = Reduce(me, (far_ref, near_ref), slots, rs_send, rs_recv)
+    down = Reduce(me, (down_far_ref, down_near_ref), down_slots, down_send, down_recv)
+
+    def place_of(core, k):
+        return pl.ds(pl.multiple_of(core * tokens + k * rows, rows), rows)
+
+    wide.start()
+    down.start()
+    besides = [remote(back_ref.at[place_of(1 - me.col, k), :], beside_in.at[k], beside_send.at[k], beside_recv.at[k], me.beside)
+               for k in range(pieces)]
+    for each in besides:
+        each.start()
+    acrosses = [remote(across_out.at[k], across_in.at[k], across_send.at[k], across_recv.at[k], me.across)
+                for k in range(pieces)]
+    for k in range(pieces):
+        besides[k].wait()
+        chip = (back_ref[place_of(me.col, k), :].astype(F32) + beside_in[k].astype(F32)).astype(BF16)
+        across_out[k, :, :half] = chip[:, half:]
+        across_out[k, :, half:] = chip[:, :half]
+        acrosses[k].start()
+
+    gain_sum_ref[...] = jnp.zeros_like(gain_sum_ref)
+    branches = [remote(branch_ref.at[place_of(me.col, k), :], branch_ref.at[place_of(me.col, k), :],
+                       branch_send.at[k], branch_recv.at[k], me.beside) for k in range(pieces)]
+    for k in range(pieces):
+        steps(k * (n - 1) // pieces, (k + 1) * (n - 1) // pieces, wide, down)
+        acrosses[k].wait()
+        mine = place_of(me.col, k)
+        grad = back_ref[mine, :].astype(F32) + beside_in[k].astype(F32) + across_in[k].astype(F32)
+        middle = middle_ref[k * rows:(k + 1) * rows, :]
+        inverse = lax.rsqrt(jnp.sum(middle * middle, axis=1, keepdims=True) / (2 * half) + EPSILON)
+        normal = middle * inverse
+        weighed = grad * normal
+        gain_sum_ref[...] += jnp.sum(weighed, axis=0, keepdims=True)
+        stat = jnp.sum(weighed * gain_ref[...], axis=1, keepdims=True) / (2 * half)
+        part = inverse * (grad * gain_ref[...] - normal * stat)
+        near = cot_near_ref[mine, :].astype(F32) + part[:, :half]
+        far = cot_far_ref[mine, :].astype(F32) + part[:, half:]
+        keep_ref[k * rows:(k + 1) * rows, :] = near
+        branch_ref[mine, :half] = near.astype(BF16)
+        branch_ref[mine, half:] = far.astype(BF16)
+        branches[k].start()
+
+    crosses = [remote(ring.last(s), out.at[s], cross_send.at[2 * k + s], cross_recv.at[2 * k + s], me.across)
+               for k, (ring, out) in enumerate(((wide, done_ref), (down, down_done_ref))) for s in range(2)]
+    for cross in crosses:
+        cross.start()
+    for s in (2, 3):
+        done_ref[s] = wide.last(s)[...]
+        down_done_ref[s] = down.last(s)[...]
+    for each in branches + crosses:
+        each.wait()
+    finish(n, wide, down)
+
+
+def turn(near, far, down_near, down_far, back, middle, cot_near, cot_far, gain, names, n, pieces=4):
+    packed, width = back.shape
+    tokens = middle.shape[0]
+    vmem = pl.BlockSpec(memory_space=pltpu.VMEM)
+    dma = pltpu.SemaphoreType.DMA
+    exchange = pltpu.VMEM((pieces, tokens // pieces, width), BF16)
+
+    def streams(x):
+        return x.shape[1], x.shape[2] // 2
+
+    return pl.pallas_call(
+        functools.partial(turn_kernel, n, names, pieces),
+        out_shape=(jax.ShapeDtypeStruct((packed, width), BF16), jax.ShapeDtypeStruct((tokens, width // 2), F32),
+                   jax.ShapeDtypeStruct((1, width), F32), jax.ShapeDtypeStruct((4, *streams(near)), BF16),
+                   jax.ShapeDtypeStruct((4, *streams(down_near)), BF16)),
+        in_specs=[vmem] * 9,
+        out_specs=(vmem,) * 5,
+        scratch_shapes=[
+            pltpu.VMEM((4, n - 1, *streams(near)), BF16), pltpu.VMEM((4, n - 1, *streams(down_near)), BF16),
+            exchange, exchange, exchange, *[dma((4, n - 1))] * 4, dma((4,)), dma((4,)), *[dma((pieces,))] * 6,
+        ],
+        compiler_params=pltpu.CompilerParams(collective_id=1, has_side_effects=True, vmem_limit_bytes=60 << 20),
+        cost_estimate=pl.CostEstimate(flops=40 * back.size, transcendentals=tokens, bytes_accessed=150 << 20),
+        name="turn",
+    )(near, far, down_near, down_far, back, middle, cot_near, cot_far, gain)
+
+
+def retreat_kernel(n, names, b, packed, q_ref, k_ref, v_ref, grad_ref, raw_ref, lse_ref, start_ref,
+                   done_ref, down_done_ref, result_ref, middle_ref,
+                   dq_ref, dk_ref, dv_ref, wide_ref, down_ref, output_ref,
+                   qs_ref, gs_ref, stat_ref, dqt_ref, dk_acc, dv_acc,
+                   sums, beside_in, across_out, across_in, wide_send, wide_recv, down_send, down_recv,
+                   beside_send, beside_recv, across_send, across_recv, last_send, last_recv, load_sem, keep_sem):
+    g, j = pl.program_id(0), pl.program_id(1)
+    blocks = packed // b
+    me = Group(names, n)
+    half = output_ref.shape[1]
+    count = packed // 2
+    wide = Spread(me, wide_ref, wide_send, wide_recv)
+    down = Spread(me, down_ref, down_send, down_recv)
+    own_rows = pl.ds(pl.multiple_of(me.col * count, count), count)
+    other_rows = pl.ds(pl.multiple_of((1 - me.col) * count, count), count)
+    sides = (pl.ds(half, half), pl.ds(0, half))
+    besides = [remote(result_ref.at[other_rows, side], beside_in.at[k], beside_send.at[k], beside_recv.at[k], me.beside)
+               for k, side in enumerate(sides)]
+    loads = [pltpu.make_async_copy(result_ref.at[own_rows, side], sums.at[k], load_sem.at[k]) for k, side in enumerate(sides)]
+    across = remote(across_out, across_in, across_send, across_recv, me.across)
+    last = remote(across_out, output_ref.at[own_rows, :], last_send, last_recv, me.beside)
+    last_here = pltpu.make_async_copy(across_out, output_ref.at[own_rows, :], keep_sem.at[8])
+    keeps = [pltpu.make_async_copy(src.at[s], ring.piece(s, me.own(s % 2)), keep_sem.at[4 * k + s])
+             for k, (ring, src) in enumerate(((wide, done_ref), (down, down_done_ref))) for s in range(4)]
+
+    @pl.when((g == 0) & (j == 0))
+    def _():
+        me.arrive([*me.ring, me.across, me.beside])
+        for ring, src in ((wide, done_ref), (down, down_done_ref)):
+            for s in range(4):
+                ring.start(s, src.at[s])
+        for each in besides + loads + keeps:
+            each.start()
+
+    @pl.when((g == 0) & (j == 1))
+    def _():
+        for each in besides + loads:
+            each.wait()
+        across_out[...] = (sums[0].astype(F32) + beside_in[0].astype(F32)).astype(BF16)
+        across.start()
+
+    @pl.when((g == 1) & (j == 1))
+    def _():
+        across.wait()
+        total = middle_ref[...] + (sums[1].astype(F32) + beside_in[1].astype(F32) + across_in[...].astype(F32))
+        across_out[...] = total.astype(BF16)
+        last.start()
+        last_here.start()
+
+    @pl.when(j == 0)
+    def _():
+        dqt_ref[...] = jnp.zeros_like(dqt_ref)
+        for i in range(blocks):
+            rows = slice(i * b, (i + 1) * b)
+            both = slice(i * 2 * b, (i + 1) * 2 * b)
+            qs_ref[both, :] = stacked(q_ref[rows, :])
+            grad = grad_ref[rows, :]
+            gs_ref[both, :] = stacked(grad)
+            prod = (grad.astype(F32) * raw_ref[rows, :]).T
+            stat_ref[i, 0:1, 0:b] = lse_ref[0, 0:1, rows]
+            stat_ref[i, 0:1, b:2 * b] = lse_ref[0, 1:2, rows]
+            stat_ref[i, 1:2, 0:b] = jnp.sum(prod[:64], axis=0, keepdims=True)
+            stat_ref[i, 1:2, b:2 * b] = jnp.sum(prod[64:], axis=0, keepdims=True)
+
+    k = k_ref[...]
+    v = v_ref[...]
+    kt = k.T[:64]
+    dk_acc[...] = jnp.zeros_like(dk_acc)
+    dv_acc[...] = jnp.zeros_like(dv_acc)
+    keys = j * b + lax.broadcasted_iota(jnp.int32, (b, 1), 0)
+    every = blocks * (blocks + 1)
+    before = g * (every // 2) + j * blocks - (j * (j - 1)) // 2
+
+    def step(i, diagonal):
+        at = pl.ds(pl.multiple_of(i * 2 * b, 2 * b), 2 * b)
+        qs = qs_ref[at, :]
+        gs = gs_ref[at, :]
+        st = dot(k, qs, NT)
+        pt = jnp.exp(st - stat_ref[i, 0:1, :])
+        begin = start_ref[0:1, pl.ds(pl.multiple_of(i * b, b), b)]
+        allowed = keys >= jnp.concatenate([begin, begin], axis=1)
+        if diagonal:
+            cols = i * b + lax.rem(lax.broadcasted_iota(jnp.int32, (1, 2 * b), 1), b)
+            allowed = allowed & (keys <= cols)
+        pt = jnp.where(allowed, pt, 0.0)
+        dv_acc[...] += dot(pt.astype(BF16), gs)
+        dpt = dot(v, gs, NT)
+        dst = (pt * (dpt - stat_ref[i, 1:2, :])).astype(BF16)
+        dk_acc[...] += dot(dst, qs)
+        part = dot(kt, dst)
+        to = pl.ds(pl.multiple_of(i * b, b), b)
+        dqt_ref[0:64, to] += part[:, :b]
+        dqt_ref[64:128, to] += part[:, b:]
+        at = before + i - j
+        steps((at * (n - 1)) // every, ((at + 1) * (n - 1)) // every, wide, down)
+
+    step(j, True)
+
+    @pl.loop(j + 1, blocks)
+    def _(i):
+        step(i, False)
+
+    dk = dk_acc[...]
+    dv = dv_acc[...]
+    dk_ref[...] = dk + pltpu.roll(dk, 64, 1)
+    dv_ref[...] = dv + pltpu.roll(dv, 64, 1)
+    dq_ref[...] = dqt_ref[:, pl.ds(pl.multiple_of(j * b, b), b)].T * HEAD_SIZE ** (-0.5)
+
+    @pl.when((g == 1) & (j == blocks - 1))
+    def _():
+        for each in keeps:
+            each.wait()
+        last_here.wait()
+        last.wait()
+        finish(n, wide, down)
+
+
+def retreat(q, k, v, grad, raw, lse, starts, done, down_done, result, middle, names, n, b=512):
+    packed, width = q.shape
+    groups, lanes = width // 128, 128
+    b = min(b, packed)
+    blocks = packed // b
+    half = middle.shape[1]
+    col = pl.BlockSpec((packed, lanes), lambda g, j: (0, g))
+    blk = pl.BlockSpec((b, lanes), lambda g, j: (j, g))
+    some = pl.BlockSpec(memory_space=pl.ANY)
+    out = jax.ShapeDtypeStruct((packed, width), F32)
+    pairs = packed * (packed + b) // 2
+    dma = pltpu.SemaphoreType.DMA
+
+    def full(x):
+        return jax.ShapeDtypeStruct((2, n, x.shape[1], 2 * x.shape[2]), BF16)
+
+    exchange = pltpu.VMEM((packed // 2, half), BF16)
+    two = pltpu.VMEM((2, packed // 2, half), BF16)
+    return pl.pallas_call(
+        functools.partial(retreat_kernel, n, names, b, packed),
+        out_shape=(out, out, out, full(done), full(down_done), jax.ShapeDtypeStruct((packed, half), BF16)),
+        grid=(groups, blocks),
+        in_specs=[col, blk, blk, col, col, pl.BlockSpec((1, 2, packed), lambda g, j: (g, 0, 0)),
+                  pl.BlockSpec((1, packed), lambda g, j: (0, 0)), some, some, some,
+                  pl.BlockSpec(middle.shape, lambda g, j: (0, 0), pipeline_mode=pl.Buffered(1))],
+        out_specs=(blk, blk, blk, some, some, some),
+        scratch_shapes=[
+            pltpu.VMEM((2 * packed, lanes), BF16), pltpu.VMEM((2 * packed, lanes), BF16),
+            pltpu.VMEM((blocks, 2, 2 * b), F32), pltpu.VMEM((lanes, packed), F32),
+            pltpu.VMEM((b, lanes), F32), pltpu.VMEM((b, lanes), F32),
+            two, two, exchange, exchange, *[dma((4, n - 1))] * 4, dma((2,)), dma((2,)), *[dma] * 4, dma((2,)), dma((9,)),
+        ],
+        compiler_params=pltpu.CompilerParams(collective_id=3, has_side_effects=True, vmem_limit_bytes=60 << 20),
+        cost_estimate=pl.CostEstimate(flops=10 * groups * 2 * pairs * 256, transcendentals=2 * groups * pairs,
+                                      bytes_accessed=20 * packed * width),
+        name="retreat",
+    )(q, k, v, grad, raw, lse, starts[None, :], done, down_done, result, middle)
+
+
+def close_kernel(n, names, near_ref, far_ref, out_ref, to_near_ref, to_far_ref, stat_ref, keep_ref, tokens_ref, gain_ref,
+                 vector_ref, thin_ref, lone_ref, sums_ref, grad_ref,
+                 slots, lone_slots, beside_in, beside_stat, across_out, across_in, stat_out, stat_in, group_in, ring_in, mine,
+                 rs_send, rs_recv, ag_send, ag_recv, lone_send, lone_recv, lone_out_send, lone_out_recv, cross_send, cross_recv,
+                 group_send, group_recv, all_send, all_recv, beside_send, beside_recv, across_send, across_recv,
+                 last_send, last_recv):
+    me = Group(names, n)
+    me.arrive([*me.along, me.across, me.beside, me.opposite])
+    half = tokens_ref.shape[1]
+    count = keep_ref.shape[0]
+    thin = Reduce(me, (far_ref, near_ref), slots, rs_send, rs_recv)
+    lone = Reduce(me, (out_ref,), lone_slots, lone_send, lone_recv)
+    thin_out = Spread(me, thin_ref, ag_send, ag_recv)
+    lone_out = Spread(me, lone_ref, lone_out_send, lone_out_recv)
+
+    own_rows = pl.ds(pl.multiple_of(me.col * count, count), count)
+    other_rows = pl.ds(pl.multiple_of((1 - me.col) * count, count), count)
+    besides = [remote(src.at[other_rows, :], dst, beside_send.at[k], beside_recv.at[k], me.beside)
+               for k, (src, dst) in enumerate(((to_far_ref, beside_in.at[0]), (stat_ref, beside_stat), (to_near_ref, beside_in.at[1])))]
+    for each in besides:
+        each.start()
+    thin.start()
+    lone.start()
+    gathers = [remote(vector_ref, group_in.at[k], group_send.at[k], group_recv.at[k], target)
+               for k, target in enumerate((me.across, me.beside, me.opposite))]
+    for gather in gathers:
+        gather.start()
+
+    acrosses = [remote(src, dst, across_send.at[k], across_recv.at[k], me.across)
+                for k, (src, dst) in enumerate(((across_out, across_in), (stat_out, stat_in)))]
+    besides[0].wait()
+    across_out[...] = (to_far_ref[own_rows, :].astype(F32) + beside_in[0].astype(F32)).astype(BF16)
+    acrosses[0].start()
+    besides[1].wait()
+    stat_out[...] = stat_ref[own_rows, :] + beside_stat[...]
+    acrosses[1].start()
+
+    for gather in gathers:
+        gather.wait()
+    mine[...] = vector_ref[...] + group_in[0] + group_in[1] + group_in[2]
+    spreads = [remote(mine, ring_in.at[k], all_send.at[k], all_recv.at[k], target) for k, target in enumerate(me.along)]
+    for spread in spreads:
+        spread.start()
+    steps(0, n - 1, thin, lone)
+
+    crosses = [remote(thin.last(s), thin_out.piece(s, me.own(s % 2), me.row), cross_send.at[s], cross_recv.at[s], me.across)
+               for s in range(2)]
+    for cross in crosses:
+        cross.start()
+    for s in (2, 3):
+        thin_out.piece(s, me.own(s % 2))[...] = thin.last(s)[...]
+        thin_out.start(s)
+    for s in range(2):
+        lone_out.piece(s, me.own(s % 2))[...] = lone.last(s)[...]
+        lone_out.start(s)
+    for s in range(2):
+        crosses[s].wait()
+        thin_out.start(s)
+
+    besides[2].wait()
+    acrosses[0].wait()
+    acrosses[1].wait()
+    grad = to_near_ref[own_rows, :].astype(F32) + beside_in[1].astype(F32) + across_in[...].astype(F32)
+    inverse = stat_ref[own_rows, pl.ds(HEAD_SIZE, 1)]
+    stat = (stat_out[:, :1] + stat_in[:, :1]) / (2 * half)
+    near = tokens_ref[own_rows, :].astype(F32) * inverse
+    grad_ref[own_rows, :] = (inverse * (grad * gain_ref[...] - near * stat) + keep_ref[...]).astype(BF16)
+    last = remote(grad_ref.at[own_rows, :], grad_ref.at[own_rows, :], last_send, last_recv, me.beside)
+    last.start()
+
+    steps(0, n - 1, thin_out, lone_out)
+
+    total = mine[...]
+    for spread in spreads:
+        spread.wait()
+    for k in range(n - 1):
+        total = total + ring_in[k]
+    sums_ref[...] = total
+    last.wait()
+    finish(n, thin, lone, thin_out, lone_out)
+
+
+def close(near, far, out, to_near, to_far, stat, keep, tokens, gain, vector, names, n):
+    packed, half = tokens.shape
+    count = packed // 2
+    rows, thin, lone = near.shape[1], near.shape[2] // 2, out.shape[2] // 2
+    vmem = pl.BlockSpec(memory_space=pltpu.VMEM)
+    dma = pltpu.SemaphoreType.DMA
+
+    def shape(*dims, dtype=BF16):
+        return jax.ShapeDtypeStruct(dims, dtype)
+
+    exchange = pltpu.VMEM((count, half), BF16)
+    stats = pltpu.VMEM((count, stat.shape[1]), F32)
+    return pl.pallas_call(
+        functools.partial(close_kernel, n, names),
+        out_shape=(shape(2, n, rows, 2 * thin), shape(n, rows, 2 * lone), shape(*vector.shape, dtype=F32), shape(packed, half)),
+        in_specs=[vmem] * 10,
+        out_specs=(vmem,) * 4,
+        scratch_shapes=[
+            pltpu.VMEM((4, n - 1, rows, thin), BF16), pltpu.VMEM((2, n - 1, rows, lone), BF16),
+            pltpu.VMEM((2, count, half), BF16), stats, exchange, exchange, stats, stats,
+            pltpu.VMEM((3, *vector.shape), F32), pltpu.VMEM((n - 1, *vector.shape), F32), pltpu.VMEM(vector.shape, F32),
+            *[dma((4, n - 1))] * 4, *[dma((2, n - 1))] * 4, dma((2,)), dma((2,)), dma((3,)), dma((3,)), dma((n - 1,)), dma((n - 1,)),
+            dma((3,)), dma((3,)), dma((2,)), dma((2,)), dma, dma,
+        ],
+        compiler_params=pltpu.CompilerParams(collective_id=2, has_side_effects=True, vmem_limit_bytes=60 << 20),
+        cost_estimate=pl.CostEstimate(flops=40 * packed * half, transcendentals=0, bytes_accessed=200 << 20),
+        name="close",
+    )(near, far, out, to_near, to_far, stat, keep, tokens, gain, vector)
+
+
+def widen_kernel(widths, units, wide_ref, down_ref, thin_ref, lone_ref, gate_out, up_out, down_out, q_out, k_out, v_out, lone_out):
+    for part in range(2):
+        for out, begin in ((gate_out, 0), (up_out, units)):
+            out[:, part * units:(part + 1) * units] = wide_ref[part, :, begin:begin + units].astype(F32)
+        begin = 0
+        for out, columns in zip((q_out, k_out, v_out), widths):
+            out[:, part * columns:(part + 1) * columns] = thin_ref[part, :, begin:begin + columns].astype(F32)
+            begin += columns
+    down_out[...] = down_ref[...].astype(F32)
+    lone_out[...] = lone_ref[...].astype(F32)
+
+
+def widen(wide, down, thin, lone, widths, parts=8):
+    half = lone.shape[0]
+    units = wide.shape[2] // 2
+    rows, down_rows = half // parts, down.shape[0] // parts
+
+    def one(rows, columns):
+        return pl.BlockSpec((rows, columns), lambda i: (i, 0))
+
+    def two(columns):
+        return pl.BlockSpec((2, rows, columns), lambda i: (0, i, 0))
+
+    shapes = [(half, 2 * units)] * 2 + [down.shape] + [(half, 2 * columns) for columns in widths] + [lone.shape]
+    return pl.pallas_call(
+        functools.partial(widen_kernel, widths, units),
+        out_shape=tuple(jax.ShapeDtypeStruct(shape, F32) for shape in shapes),
+        grid=(parts,),
+        in_specs=[two(2 * units), one(down_rows, down.shape[1]), two(thin.shape[2]), one(rows, lone.shape[1])],
+        out_specs=tuple(one(down_rows if k == 2 else rows, shape[1]) for k, shape in enumerate(shapes)),
+        compiler_params=pltpu.CompilerParams(vmem_limit_bytes=40 << 20),
+        cost_estimate=pl.CostEstimate(flops=0, transcendentals=0, bytes_accessed=6 * (wide.size + down.size + thin.size + lone.size)),
+        name="widen",
+    )(wide, down, thin, lone)
+
+
+def gated(x, *deps):
+    late = functools.reduce(jnp.logical_or, [dep != dep for dep in deps])
+    return jnp.where(late, jnp.zeros_like(x), x)
+
+
+def corner(x):
+    return x[(0,) * x.ndim].astype(F32)
 
 
 def shards(
@@ -444,30 +920,28 @@
     qkv_far = swap(qkv_sent, "row")
     gains = jnp.stack([attn_gain, ffn_gain])
     gains_far = swap(gains, "row")
-    far_other = swap(far_own, "col")
-    far = ordered(far_own, far_other, col)
-    cot_own = part_of(cotangent, col, 0)
+    far = ordered(far_own, swap(far_own, "col"), col)
 
     def far_weight(sent):
-        piece = swap(part_of(sent, group, 0, parts), "row")
-        return lax.all_gather(piece, "dp", axis=0, tiled=True)
+        piece = swap(gated(part_of(sent, group, 0, parts), corner(far_own)), "row")
+        return lax.all_gather(piece, "dp", axis=0, tiled=True), corner(piece)
 
     gate_up_near = jnp.concatenate([part_of(gate_weight, row, 1), part_of(up_weight, row, 1)], axis=1)
-    gate_up_far = far_weight(jnp.concatenate([part_of(gate_weight, 1 - row, 1), part_of(up_weight, 1 - row, 1)], axis=1))
+    gate_up_far, sign_one = far_weight(
+        jnp.concatenate([part_of(gate_weight, 1 - row, 1), part_of(up_weight, 1 - row, 1)], axis=1))
     down_near = part_of(down_weight, row, 0)
-    down_far = far_weight(part_of(down_weight, 1 - row, 0))
+    down_far, sign_two = far_weight(part_of(down_weight, 1 - row, 0))
     units = down_near.shape[0]
 
-    out_far = swap(out_weight, "row")
+    out_far = swap(gated(out_weight, sign_one, sign_two), "row")
     out_c = jnp.concatenate([out_weight, out_far], axis=1)
     out_n = swap(out_c, "col")
     out_own = part_of(out_c, row, 0)
     out_all = jnp.concatenate(
         [out_own, part_of(out_n, row, 0), part_of(out_c, 1 - row, 0), part_of(out_n, 1 - row, 0)], axis=0)
 
-    cot_far_own = swap(cot_own, "row")
-    cot_o = swap(jnp.concatenate([cot_own, cot_far_own], axis=1), "col")
-    cot_c = jnp.concatenate([cot_own, cot_far_own], axis=1)
+    cot_far_own = swap(gated(part_of(cotangent, col, 0), corner(out_far)), "row")
+    cot_far = ordered(cot_far_own, swap(cot_far_own, "col"), col)
 
     starts = layout(seq_lengths[0], packed)
     cosine, sine = rope_tables(jnp.arange(packed, dtype=jnp.int32) - starts)
@@ -475,6 +949,7 @@
     k_gain = jnp.tile(key_gain, 2)[None, :]
     small = (attn_gain[None, :], gains_far[0][None, :], qkv, qkv_far, q_gain, k_gain)
     hid_near, hid_far, raw, q, k, v = project(tokens, far, *small, cosine, sine)
+
     low, attended_raw, totals = attend(q, k, v, starts)
 
     chip = jnp.concatenate([part_of(low, col, 0), swap(part_of(low, 1 - col, 0), "col")], axis=1)
@@ -485,122 +960,63 @@
     normal_two = middle * inverse_two
     gain_two = jnp.concatenate([ffn_gain, gains_far[1]])[None, :]
     hidden_c = (normal_two * gain_two).astype(BF16)
-    hidden_o = swap(hidden_c, "col")
+    hidden = ordered(hidden_c, swap(hidden_c, "col"), col)
     gate_up = jnp.concatenate([gate_up_near, gate_up_far], axis=0)
     down = jnp.concatenate([down_near, down_far], axis=1)
-
-    def feed(hidden, cot):
-        both = dot(hidden, gate_up)
-        grad_active = dot(cot, down, NT)
-        gate, upward = both[:, :units], both[:, units:]
-        sig = 1.0 / (1.0 + jnp.exp(-gate))
-        lifted = gate * sig
-        active = (lifted * upward).astype(BF16)
-        grad_gate = (grad_active * upward * (sig * (1.0 + gate * (1.0 - sig)))).astype(BF16)
-        grad_up = (grad_active * lifted).astype(BF16)
-        return active, jnp.concatenate([grad_gate, grad_up], axis=1)
-
-    active_o, grads_o = feed(hidden_o, cot_o)
-    active_c, grads_c = feed(hidden_c, cot_c)
-    back_o = swap(dot(grads_o, gate_up, NT).astype(BF16), "col")
-    back_c = dot(grads_c, gate_up, NT) + back_o.astype(F32)
-    back_low = back_c.astype(BF16)
-    grad_hidden = back_c + jnp.concatenate(swap((back_low[:, half:], back_low[:, :half]), "row"), axis=1).astype(F32)
-
-    grad_down = over_t(active_c, cot_c) + over_t(active_o, cot_o)
-    grad_gate_up = over_t(hidden_c, grads_c) + over_t(hidden_o, grads_o)
-
-    result_o = swap(dot(active_o, down).astype(BF16), "col")
-    result_c = dot(active_c, down) + result_o.astype(F32)
-    result = middle[:, :half] + result_c[:, :half] + swap(result_c[:, half:].astype(BF16), "row").astype(F32)
-    result = result.astype(BF16)
-    output = ordered(result, swap(result, "col"), col)
-
-    ffn_gain_sum = jnp.sum(grad_hidden * normal_two, axis=0)
-    inner = grad_hidden * gain_two
-    stat = jnp.sum(inner * normal_two, axis=1, keepdims=True) / width
-    grad_middle = cot_c.astype(F32) + inverse_two * (inner - normal_two * stat)
-    branch_c = grad_middle.astype(BF16)
-    branch_o = swap(branch_c, "col")
-    grad_attended = ordered(dot(branch_c, out_own, NT).astype(BF16), dot(branch_o, out_own, NT).astype(BF16), col)
-    grad_out = over_t(attended, branch_c[:, :half])
-    quarter = grad_out.shape[0] // 4
+    active, feed_grads, result, back = feed(hidden, cotangent, cot_far, gate_up, down)
+
+    grad_down_near, grad_down_far = (
+        over_t(active, cot).astype(BF16).reshape(parts, units // parts, -1) for cot in (cotangent, cot_far))
+    grad_gate_up = over_t(hidden, feed_grads).astype(BF16).reshape(2, parts, half // parts, -1)
+    names = ("dp", "row", "col")
+    branch, keep, ffn_sum, done, down_done = turn(
+        grad_gate_up[0], grad_gate_up[1], grad_down_near, grad_down_far, back, middle, cotangent, cot_far, gain_two, names, parts)
+
+    grad_attended = (dot(branch[:, :half], out_own[:, :half], NT) + dot(branch[:, half:], out_own[:, half:], NT)).astype(BF16)
+    grad_out = over_t(attended, part_of(branch[:, :half], col, 0))
+    quarter = out_own.shape[0]
     kept = jnp.concatenate([grad_out[:quarter], grad_out[2 * quarter:3 * quarter]], axis=0)
     sent = jnp.concatenate([grad_out[quarter:2 * quarter], grad_out[3 * quarter:]], axis=0)
     grad_out = kept + swap(sent.astype(BF16), "col").astype(F32)
-    grad_out = ordered(grad_out[:quarter], grad_out[quarter:], row).astype(BF16)
-
-    dq, dk, dv = attend_back(q, k, v, grad_attended, attended_raw, totals, starts)
+    grad_out = ordered(grad_out[:quarter], grad_out[quarter:], row).astype(BF16).reshape(parts, half // parts, -1)
+
+    dq, dk, dv, wide_full, down_full, output = retreat(
+        q, k, v, grad_attended, attended_raw, totals, starts, done, down_done, result, middle[:, :half], names, parts)
     grads, to_near, to_far, stat_one, q_sum, k_sum, near_sum, far_sum = project_back(
         dq, dk, dv, raw, tokens, far, *small, cosine, sine)
-    grad_qkv = jnp.concatenate([over_t(hid_near, grads), over_t(hid_far, grads)], axis=0)
-
-    to_all = jnp.concatenate([to_near, to_far], axis=1)
-    stat_one = stat_one[:, 0]
-    sent_o, sent_stat = swap((part_of(to_all, 1 - col, 0), part_of(stat_one, 1 - col, 0)), "col")
-    chip_sum = part_of(to_all, col, 0).astype(F32) + sent_o.astype(F32)
-    chip_stat = part_of(stat_one, col, 0) + sent_stat
-    other_sum, other_stat = swap((chip_sum[:, half:].astype(BF16), chip_stat), "row")
-    inner_one = (chip_sum[:, :half] + other_sum.astype(F32)) * attn_gain[None, :]
-    mine = mine.astype(F32)
-    inverse_one = lax.rsqrt(jnp.sum(mine * mine, axis=1, keepdims=True) / width + EPSILON)
-    stat_one = (chip_stat + other_stat)[:, None] / width
-    grad_inputs = inverse_one * (inner_one - mine[:, :half] * inverse_one * stat_one) + grad_middle[:, :half]
-    grad_inputs = grad_inputs.astype(BF16)
-    grad_tokens = ordered(grad_inputs, swap(grad_inputs, "col"), col)
-
-    def reduced(x, axis):
-        return lax.psum_scatter(x, "dp", scatter_dimension=axis, tiled=True)
-
-    def gathered(x, axis):
-        return lax.all_gather(x, "dp", axis=axis, tiled=True)
-
-    def columns_split(grad):
-        piece = reduced(grad.astype(BF16).reshape(2, half, -1), 1)
-        other = swap(piece[1], "row")
-        full = gathered(ordered(piece[0][None], other[None], row), 1)
-        return full.astype(F32)
-
-    def rows_split(grad):
-        piece = reduced(grad.astype(BF16), 0)
-        other = swap(piece[:, half:], "row")
-        full = gathered(ordered(piece[:, :half][None], other[None], row), 1)
-        return full.astype(F32).reshape(-1, half)
-
-    def side(full, begin, end):
-        return jnp.concatenate([full[0][:, begin:end], full[1][:, begin:end]], axis=1)
-
-    down_full = rows_split(grad_down)
-    gate_up_full = columns_split(grad_gate_up)
-    qkv_full = columns_split(grad_qkv)
-    out_full = lax.psum(grad_out, "dp").astype(F32)
-    q_cols, k_cols = query_weight.shape[1] // 2, key_matrix.shape[1] // 2
-
-    def slots(x_near, x_far):
-        return ordered(x_near, x_far, row)
+    near_grads, far_grads = (
+        over_t(hid, grads).astype(BF16).reshape(parts, half // parts, -1) for hid in (hid_near, hid_far))
 
     def folded(x):
         return x[0, :HEAD_SIZE] + x[0, HEAD_SIZE:]
 
-    ffn_slots = slots(ffn_gain_sum[:half], ffn_gain_sum[half:]) * 0.5
-    sums = lax.psum(
-        jnp.concatenate([slots(near_sum[0], far_sum[0]), ffn_slots, folded(q_sum), folded(k_sum)]), ("dp", "row", "col"))
-    attn_sum = part_of(sums[:width], row, 0)
-    ffn_sum = part_of(sums[width:2 * width], row, 0)
+    vector = jnp.concatenate([
+        ordered(near_sum[0], far_sum[0], row), ordered(ffn_sum[0, :half], ffn_sum[0, half:], row) * 0.5,
+        folded(q_sum), folded(k_sum)])
+    length = vector.shape[0]
+    lines = -(-length // 1024) * 8
+    vector = jnp.concatenate([vector, jnp.zeros((lines * 128 - length,), F32)]).reshape(lines, 128)
+    thin_full, out_full, sums, grad_tokens = close(
+        near_grads, far_grads, grad_out, to_near, to_far, stat_one, keep, tokens, attn_gain[None, :], vector, names, parts)
+    sums = sums.reshape(-1)
+    widths = (query_weight.shape[1] // 2, key_matrix.shape[1] // 2, value_matrix.shape[1] // 2)
+    gate_sum, up_sum, down_sum, q_weight_sum, k_weight_sum, v_weight_sum, out_sum = widen(
+        wide_full.reshape(2, half, -1), down_full.reshape(2 * units, half), thin_full.reshape(2, half, -1),
+        out_full.reshape(half, -1), widths)
     return (
         output,
         grad_tokens,
-        side(qkv_full, 0, q_cols),
-        side(qkv_full, q_cols, q_cols + k_cols),
-        side(qkv_full, q_cols + k_cols, q_cols + 2 * k_cols),
-        out_full,
-        side(gate_up_full, 0, units),
-        side(gate_up_full, units, 2 * units),
-        down_full,
-        attn_sum,
-        ffn_sum,
+        q_weight_sum,
+        k_weight_sum,
+        v_weight_sum,
+        out_sum,
+        gate_sum,
+        up_sum,
+        down_sum,
+        part_of(sums[:width], row, 0),
+        part_of(sums[width:2 * width], row, 0),
         sums[2 * width:2 * width + HEAD_SIZE],
-        sums[2 * width + HEAD_SIZE:],
+        sums[2 * width + HEAD_SIZE:2 * width + 2 * HEAD_SIZE],
     )
 
 

time: 842 us -> 562 us (0.67)
  waiting for transfers between devices: 421 us -> 67.1 us
  Pallas kernels: 85.2 us -> 332 us
  matrix products: 115 us -> 38.5 us
  blocking collectives: 54.6 us -> 0 us
  other arithmetic: 70.2 us -> 38.2 us
  starting transfers between devices: 26 us -> 12.1 us
    pallas_call x1 -> x5, Pallas kernels: 37.4 us -> 285 us  [the longest x1 91.7 us: turn(): pl.pallas_call(functools.partial(turn_kernel, n, names, pieces), out_shap...]
    reduce_scatter x3 -> x0, waiting for transfers between devices: 122 us -> none  [reduced(): return lax.psum_scatter(x, 'dp', scatter_dimension=axis, tiled=True)]
    all_gather x5 -> x2, waiting for transfers between devices: 118 us -> 0.01 us  [far_weight(): return (lax.all_gather(piece, 'dp', axis=0, tiled=True), corner(piece))]
    ppermute x29 -> x14, waiting for transfers between devices: 153 us -> 67.1 us  [swap(): lax.ppermute(part, axis, [(0, 1), (1, 0)])]
    dot_general x18 -> x9, matrix products: 115 us -> 38.5 us  [dot(): return lax.dot_general(a, b, dims, preferred_element_type=F32)]
    psum x1 -> x0, blocking collectives: 54.6 us -> none  [shards(): lax.psum(jnp.concatenate([slots(near_sum[0], far_sum[0]), ffn_slots, fold...]
    psum x1 -> x0, waiting for transfers between devices: 27.8 us -> none  [shards(): out_full = lax.psum(grad_out, 'dp').astype(F32)]
    convert_element_type x8 -> x1, other arithmetic: 21.1 us -> 0.93 us  [shards(): ordered(grad_out[:quarter], grad_out[quarter:], row).astype(BF16)]
  transfers between devices with their start and end apart: 38 -> 16, of which waited for: 16 -> 4; matrix products, arithmetic and copies ran while one was open for 20% -> 10% of each run, Pallas kernels for 10% -> 6%
where the time goes in v4:
time: 562 us; the launch traced here: 555 us
  Pallas kernels  332 us (59%)
  waiting for transfers between devices  67.1 us (12%)
  local copies, waits for them, and re-layouts  46.6 us (8%)
  matrix products  38.5 us (7%)
  other arithmetic  38.2 us (7%)
  between operations  20.3 us (4%)
  starting transfers between devices  12.1 us (2%)
    pallas_call x1, Pallas kernels, turn(): pl.pallas_call(functools.partial(turn_kernel, n, names, pieces), out_shap...  91.7 us
    pallas_call x1, Pallas kernels, retreat(): pl.pallas_call(functools.partial(retreat_kernel, n, names, b, packed), ou...  74.9 us
    pallas_call x1, Pallas kernels, close(): pl.pallas_call(functools.partial(close_kernel, n, names), out_shape=(shap...  72.4 us
    ppermute x14, waiting for transfers between devices, swap(): lax.ppermute(part, axis, [(0, 1), (1, 0)])  67.1 us
    pallas_call x1, Pallas kernels, feed(): pl.pallas_call(functools.partial(feed_kernel, units), out_shape=(out(unit...  39.7 us
    dot_general x9, matrix products, dot(): return lax.dot_general(a, b, dims, preferred_element_type=F32)  38.5 us
    pallas_call x1, Pallas kernels, attend(): pl.pallas_call(kern, out_shape=(jax.ShapeDtypeStruct((T, width), BF16), j...  21.7 us
    unnamed x102, local copies, waits for them, and re-layouts  16.2 us
  transfers between devices with their start and end apart: 16, of which 4 were waited for; matrix products, arithmetic and copies ran while one was open for 10% of the time, Pallas kernels for 6%

profile of v4, /device:TPU:0, one launch (start us, length us, event | category | flops | bytes accessed | tf_op | source)
XLA Modules:
  0.0 555.2 jit_solution(584077768054217222)
XLA Ops:
  8.5 1.8 constant_dynamic-slice_fusion.11
  11.2 2.9 collective-permute-start.3
  15.2 2.1 collective-permute-start.2
  18.0 1.3 copy.30.start_ref
  19.4 3.7 fusion.16
  23.1 2.7 pad_maximum_fusion.3
  25.8 1.8 constant_dynamic-slice_fusion.1
  27.6 21.3 %collective-permute-done = bf16[1024,512]{1,0:T(8,128)(2,1)} collective-permute-done((bf16[1024,512]{1,0:T(8,128)(2,1)}, bf16[1024,512]{1,0:T(8,128)(2,1)}, u32[]{:S(2)}, u32[]{:S(2)}) %collective-permute-start) | collective-permute-done | bytes 1048608 | tf_op jit(solution)/shard_map/ppermute | solution.py:302
  52.3 1.8 collective-permute-start.6
  55.4 9.6 %collective-permute-done.7 = bf16[144,512]{1,0:T(8,128)(2,1)} collective-permute-done((bf16[144,512]{1,0:T(8,128)(2,1)S(1)}, bf16[144,512]{1,0:T(8,128)(2,1)}, u32[]{:S(2)}, u32[]{:S(2)}) %collective-permute-start.7) | collective-permute-done | bytes 147488 | tf_op jit(solution)/shard_map/ppermute | solution.py:302
  70.6 2.1 broadcast_select_fusion
  72.7 1.7 collective-permute-start.8
  74.5 4.1 maximum_select_fusion.1.far_ref
  78.6 10.5 %project.1 = (bf16[2048,512]{1,0:T(8,128)(2,1)S(1)}, bf16[2048,512]{1,0:T(8,128)(2,1)S(1)}, f32[2048,384]{1,0:T(8,128)}, bf16[2048,256]{1,0:T(8,128)(2,1)S(1)}, ...) custom-call(bf16[2048,512]{1,0:T(8,128)(2,1)S(1)} %copy-done, ...), custom_call_target="tpu_custom_call" | custom-call | flops 2147483648 | bytes 13631488 | tf_op jit(solution)/shard_map/project/pallas_call | solution.py:182
  89.1 1.4 copy-done.8
  90.5 1.3 copy-done.9
  91.8 21.7 %attend.1 = (bf16[2048,256]{1,0:T(8,128)(2,1)S(1)}, f32[2048,256]{1,0:T(8,128)S(1)}, f32[2,2,2048]{2,1,0:T(2,128)S(1)}) custom-call(s32[4]{0:T(128)S(1)} %slice.107.first_ref, s32[4]{0:T(128)S(1)} %slice.108.last_ref, bf16[2048,256]{1,0:T(8,128)(2,1)S(1)} %get-tuple-element.56.q_ref, bf16[2048,256]{1,0:T(8,128)(2,1)S(1)} %get-tuple-element.57.k_ref, ...), custom_call_target="tpu_custom_call" | custom-call | flops 10737418240 | bytes 5242880 | tf_op jit(solution)/shard_map/attend/pallas_call | solution.py:85
  115.3 2.1 constant_dynamic-update-slice_fusion
  122.4 1.8 collective-permute-start.11
  124.3 21.0 %collective-permute-done.5 = bf16[1024,512]{1,0:T(8,128)(2,1)S(1)} collective-permute-done((bf16[1024,512]{1,0:T(8,128)(2,1)S(1)}, bf16[1024,512]{1,0:T(8,128)(2,1)S(1)}, u32[]{:S(2)}, u32[]{:S(2)}) %collective-permute-start.5) | collective-permute-done | bytes 1048608 | tf_op jit(solution)/shard_map/ppermute | solution.py:302
  145.3 4.5 multiply_reduce_fusion
  150.3 1.5 copy-done.21
  151.8 15.2 %collective-permute-done.11 = bf16[1024,512]{1,0:T(8,128)(2,1)} collective-permute-done((bf16[1024,512]{1,0:T(8,128)(2,1)S(1)}, bf16[1024,512]{1,0:T(8,128)(2,1)}, u32[]{:S(2)}, u32[]{:S(2)}) %collective-permute-start.11) | collective-permute-done | bytes 1048608 | tf_op jit(solution)/shard_map/ppermute | solution.py:302
  167.0 2.4 constant_dynamic-slice_fusion
  169.4 3.5 pad_maximum_fusion.1.down_ref
  172.9 1.5 slice.147.middle_ref
  174.4 4.3 maximum_select_fusion.2.cot_far_ref
  178.7 4.8 pad_maximum_fusion.gate_up_ref
  183.5 4.8 maximum_select_fusion.hidden_ref
  188.4 39.7 %feed.1 = (bf16[2048,1152]{1,0:T(8,128)(2,1)}, bf16[2048,2304]{1,0:T(8,128)(2,1)}, bf16[2048,1024]{1,0:T(8,128)(2,1)}, bf16[2048,1024]{1,0:T(8,128)(2,1)}) custom-call(bf16[2048,1024]{1,0:T(8,128)(2,1)} %maximum_select_fusion.hidden_ref, bf16[2048,512]{1,0:T(8,128)(2,1)} %cot_near_ref.3, bf16[2048,512]{1,0:T(8,128)(2,1)} %maximum_select_fusion.2.cot_far_ref, ...), custom_call_target="tpu_custom_call" | custom-call | flops 28991029248 | bytes 38010880 | tf_op jit(solution)/shard_map/feed/pallas_call | solution.py:351
  228.1 6.2 %convolution_convert_fusion.1 = bf16[1152,512]{1,0:T(8,128)(2,1)} fusion(bf16[2048,1152]{1,0:T(8,128)(2,1)} %get-tuple-element.61, bf16[2048,512]{1,0:T(8,128)(2,1)S(1)} %copy-done.24), kind=kOutput, calls=%fused_computation.6 | convolution fusion | flops 2416508928 | bytes 7995392 | tf_op jit(solution)/shard_map/dot_general | solution.py:19
  234.3 3.7 convolution_convert_fusion.2
  238.0 11.2 %convolution_convert_fusion = bf16[1024,2304]{1,0:T(8,128)(2,1)S(1)} fusion(bf16[2048,1024]{1,0:T(8,128)(2,1)S(1)} %copy-done.27, bf16[2048,2304]{1,0:T(8,128)(2,1)S(1)} %bitcast.79), kind=kOutput, calls=%fused_computation | convolution fusion | flops 9666035712 | bytes 18350080 | tf_op jit(solution)/shard_map/dot_general | solution.py:19
  249.2 2.5 fusion.31
  251.7 91.7 %turn.1 = (bf16[2048,1024]{1,0:T(8,128)(2,1)}, f32[1024,512]{1,0:T(8,128)}, f32[1,1024]{1,0:T(1,128)}, bf16[4,64,1152]{2,1,0:T(8,128)(2,1)}, bf16[4,144,256]{2,1,0:T(8,128)(2,1)}) custom-call(bf16[8,64,2304]{2,1,0:T(8,128)(2,1)} %bitcast.62, bf16[8,64,2304]{2,1,0:T(8,128)(2,1)} %bitcast.61, bf16[8,144,512]{2,1,0:T(8,128)(2,1)} %bitcast.67, ...), custom_call_target="tpu_custom_call" | custom-call | flops 83886080 | bytes 157286400 | tf_op jit(solution)/shard_map/turn/pallas_call | solution.py:563
  344.3 3.2 slice.116
  347.5 1.7 fusion.9
  349.2 2.7 fusion.grad_ref
  351.9 74.9 %retreat.1 = (f32[2048,256]{1,0:T(8,128)}, f32[2048,256]{1,0:T(8,128)}, f32[2048,256]{1,0:T(8,128)}, bf16[2,8,64,2304]{3,2,1,0:T(8,128)(2,1)}, bf16[2,8,144,512]...) custom-call(bf16[2048,256]{1,0:T(8,128)(2,1)} %copy-done.16, bf16[2048,256]{1,0:T(8,128)(2,1)} %copy-done.17, ...), custom_call_target="tpu_custom_call" | custom-call | flops 26843545600 | bytes 10485760 | tf_op jit(solution)/shard_map/retreat/pallas_call | solution.py:715
  428.1 15.2 %project_back.1 = (bf16[2048,512]{1,0:T(8,128)(2,1)S(1)}, bf16[2048,512]{1,0:T(8,128)(2,1)S(1)}, bf16[2048,512]{1,0:T(8,128)(2,1)}, f32[2048,128]{1,0:T(8,128)S(...) custom-call(f32[2048,256]{1,0:T(8,128)} %get-tuple-element.71.dq_ref, ...), custom_call_target="tpu_custom_call" | custom-call | flops 2147483648 | bytes 17825792 | tf_op jit(solution)/shard_map/project_back/pallas_call | solution.py:268
  444.3 2.7 fusion.38
  448.9 2.1 convolution_convert_fusion.3
  451.6 3.7 convolution_convert_fusion.4
  457.5 72.4 %close.1 = (bf16[2,8,64,512]{3,2,1,0:T(8,128)(2,1)}, bf16[8,64,512]{2,1,0:T(8,128)(2,1)}, f32[24,128]{1,0:T(8,128)}, bf16[2048,512]{1,0:T(8,128)(2,1)}) custom-call(bf16[8,64,512]{2,1,0:T(8,128)(2,1)} %bitcast.64, bf16[8,64,512]{2,1,0:T(8,128)(2,1)} %bitcast.63, bf16[8,64,512]{2,1,0:T(8,128)(2,1)} %bitcast.65, bf16[2048,512]{1,0:T(8,128)(2,1)} %copy-done.5, ...), custom_call_target="tpu_custom_call" | custom-call | flops 41943040 | bytes 209715200 | tf_op jit(solution)/shard_map/close/pallas_call | solution.py:830
  531.9 1.3 fusion.35
  533.2 2.3 copy-done.1
  537.8 6.4 %widen.1 = (f32[512,2304]{1,0:T(8,128)}, f32[512,2304]{1,0:T(8,128)}, f32[2304,512]{1,0:T(8,128)}, f32[512,512]{1,0:T(8,128)}, f32[512,256]{1,0:T(8,128)}, /*index=5*/f32[512,256]{1,0:T(8,128)}, f32[512,512]{1,0:T(8,128)}) custom-call(bf16[2,512,2304]{2,1,0:T(8,128)(2,1)S(1)} %bitcast.51, bf16[2304,512]{1,0:T(8,128)(2,1)S(1)} %bitcast.52, ...), custom_call_target="tpu_custom_call" | custom-call | bytes 25952256 | tf_op jit(solution)/shard_map/widen/pallas_call | solution.py:872
  544.3 1.3 copy.34
  (171 shorter events, 30.6 us)
Async XLA Ops:
  7.2 7.0 %copy-start = (bf16[2048,512]{1,0:T(8,128)(2,1)S(1)}, bf16[2048,512]{1,0:T(8,128)(2,1)}, u32[]{:S(2)}) copy-start(bf16[2048,512]{1,0:T(8,128)(2,1)} %tokens_ref.1) | copy-start | bytes 6291460
  7.2 162.2 %all-gather.5.cloned.1.call-start = ((), (), s32[]{:S(2)}) async-start(), calls=%async_computation.1 | async-start | bytes 1327104 | tf_op jit(solution)/shard_map/all_gather | solution.py:927
  8.5 6.7 %copy-start.15 = (f32[512]{0:T(512)S(1)}, f32[512]{0:T(512)}, u32[]{:S(2)}) copy-start(f32[512]{0:T(512)} %param.23) | copy-start | bytes 6148
  8.5 6.7 %copy-start.40 = (f32[512]{0:T(512)S(1)}, f32[512]{0:T(512)}, u32[]{:S(2)}) copy-start(f32[512]{0:T(512)} %param.24) | copy-start | bytes 6148
  8.5 8.8 %copy-start.43 = (s32[1,2]{1,0:T(1,128)S(1)}, s32[1,2]{1,0:T(1,128)}, u32[]{:S(2)}) copy-start(s32[1,2]{1,0:T(1,128)} %param.15) | copy-start | bytes 28
  8.5 9.3 %copy-start.44 = (f32[64]{0:T(128)S(1)}, f32[64]{0:T(128)}, u32[]{:S(2)}) copy-start(f32[64]{0:T(128)} %param.25) | copy-start | bytes 772
  8.5 9.4 %copy-start.45 = (f32[64]{0:T(128)S(1)}, f32[64]{0:T(128)}, u32[]{:S(2)}) copy-start(f32[64]{0:T(128)} %param.26) | copy-start | bytes 772
  11.2 67.4 %collective-permute-start.3 = (bf16[512,512]{1,0:T(8,128)(2,1)}, bf16[512,512]{1,0:T(8,128)(2,1)}, u32[]{:S(2)}, u32[]{:S(2)}) collective-permute-start(bf16[512,512]{1,0:T(8,128)(2,1)} %pad_maximum_fusion.9), channel_id=1, source_target_pairs={{0,2},{2,0},{1,3},{3,1},{4,6},{6,4},{5,7},{7,5},{8,10},{10,8},{9,1... | collective-permute-start | bytes 1572872 | tf_op jit(solution)/shard_map/ppermute | solution.py:302
  15.2 33.7 %collective-permute-start = (bf16[1024,512]{1,0:T(8,128)(2,1)}, bf16[1024,512]{1,0:T(8,128)(2,1)}, u32[]{:S(2)}, u32[]{:S(2)}) collective-permute-start(bf16[1024,512]{1,0:T(8,128)(2,1)} %constant_dynamic-slice_fusion.17), channel_id=1, source_target_pairs={{0,2},{2,0},{1,3},{3,1},{4,6},{6,4},{5,7},{7,5},{8,10},{10,8},{9,1... | collective-permute-start | bytes 3145736 | tf_op jit(solution)/shard_map/ppermute | solution.py:302
  15.2 40.2 %collective-permute-start.2 = (f32[2,512]{1,0:T(2,128)S(1)}, f32[2,512]{1,0:T(2,128)S(1)}, u32[]{:S(2)}, u32[]{:S(2)}) collective-permute-start(f32[2,512]{1,0:T(2,128)S(1)} %pad_maximum_fusion.11), channel_id=1, source_target_pairs={{0,2},{2,0},{1,3},{3,1},{4,6},{6,4},{5,7},{7,5},{8,10},{10,8},{9,1... | collective-permute-start | bytes 12296 | tf_op jit(solution)/shard_map/ppermute | solution.py:302
  17.6 8.1 %copy-start.38 = (s32[2048]{0:T(1024)}, s32[2048]{0:T(1024)S(1)}, u32[]{:S(2)}) copy-start(s32[2048]{0:T(1024)S(1)} %fusion.22) | copy-start | bytes 24580
  25.8 23.1 %copy-start.36 = (bf16[512,128]{1,0:T(8,128)(2,1)S(1)}, bf16[512,128]{1,0:T(8,128)(2,1)}, u32[]{:S(2)}) copy-start(bf16[512,128]{1,0:T(8,128)(2,1)} %get-tuple-element.124) | copy-start | bytes 393220
  25.8 23.1 %copy-start.37 = (bf16[512,128]{1,0:T(8,128)(2,1)S(1)}, bf16[512,128]{1,0:T(8,128)(2,1)}, u32[]{:S(2)}) copy-start(bf16[512,128]{1,0:T(8,128)(2,1)} %get-tuple-element.140) | copy-start | bytes 393220
  48.9 25.6 %collective-permute-start.1 = (bf16[1024,512]{1,0:T(8,128)(2,1)}, bf16[1024,512]{1,0:T(8,128)(2,1)}, u32[]{:S(2)}, u32[]{:S(2)}) collective-permute-start(bf16[1024,512]{1,0:T(8,128)(2,1)} %collective-permute-done), channel_id=1, source_target_pairs={{0,1},{1,0},{2,3},{3,2},{4,5},{5,4},{6,7},{7,6},{8,9},{9,8},{10,11... | collective-permute-start | bytes 3145736 | tf_op jit(solution)/shard_map/ppermute | solution.py:302
  52.3 15.8 %collective-permute-start.6 = (bf16[64,2304]{1,0:T(8,128)(2,1)S(1)}, bf16[64,2304]{1,0:T(8,128)(2,1)}, u32[]{:S(2)}, u32[]{:S(2)}) collective-permute-start(bf16[64,2304]{1,0:T(8,128)(2,1)S(1)} %fusion.18), channel_id=1, source_target_pairs={{0,2},{2,0},{1,3},{3,1},{4,6},{6,4},{5,7},{7,5},{8,10},{10,8},{9,1... | collective-permute-start | bytes 884744 | tf_op jit(solution)/shard_map/ppermute | solution.py:302
  55.1 10.0 %collective-permute-start.7 = (bf16[144,512]{1,0:T(8,128)(2,1)S(1)}, bf16[144,512]{1,0:T(8,128)(2,1)}, u32[]{:S(2)}, u32[]{:S(2)}) collective-permute-start(bf16[144,512]{1,0:T(8,128)(2,1)S(1)} %dynamic-slice_select_fusion.1), channel_id=1, source_target_pairs={{0,2},{2,0},{1,3},{3,1},{4,6},{6,4},{5,7},{7,5},{8,10},{10,8},{9,1... | collective-permute-start | bytes 442376 | tf_op jit(solution)/shard_map/ppermute | solution.py:302
  67.6 111.1 %all-gather.3.cloned.1.call-start = ((), (), s32[]{:S(2)}) async-start(), calls=%async_computation | async-start | bytes 2654208 | tf_op jit(solution)/shard_map/all_gather | solution.py:927
  72.7 5.9 %copy-start.2 = (f32[2048,128]{1,0:T(8,128)S(1)}, f32[2048,128]{1,0:T(8,128)}, u32[]{:S(2)}) copy-start(f32[2048,128]{1,0:T(8,128)} %get-tuple-element.143.sin_ref) | copy-start | bytes 3145732
  72.7 5.9 %copy-start.6 = (bf16[512,512]{1,0:T(8,128)(2,1)S(1)}, bf16[512,512]{1,0:T(8,128)(2,1)}, u32[]{:S(2)}) copy-start(bf16[512,512]{1,0:T(8,128)(2,1)} %pad_maximum_fusion.8.w_near_ref) | copy-start | bytes 1572868
  72.7 42.6 %collective-permute-start.8 = (bf16[512,512]{1,0:T(8,128)(2,1)}, bf16[512,512]{1,0:T(8,128)(2,1)}, u32[]{:S(2)}, u32[]{:S(2)}) collective-permute-start(bf16[512,512]{1,0:T(8,128)(2,1)} %get-tuple-element.117), channel_id=1, source_target_pairs={{0,2},{2,0},{1,3},{3,1},{4,6},{6,4},{5,7},{7,5},{8,10},{10,8},{9,1... | collective-permute-start | bytes 1572872 | tf_op jit(solution)/shard_map/ppermute | solution.py:302
  78.6 13.2 %copy-start.13 = (s32[2048,1]{1,0:T(8,128)S(1)}, s32[2048,1]{1,0:T(8,128)}, u32[]{:S(2)}) copy-start(s32[2048,1]{1,0:T(8,128)} %copy.30.start_ref) | copy-start | bytes 24580
  91.8 21.7 %copy-start.16 = (bf16[2048,256]{1,0:T(8,128)(2,1)}, bf16[2048,256]{1,0:T(8,128)(2,1)S(1)}, u32[]{:S(2)}) copy-start(bf16[2048,256]{1,0:T(8,128)(2,1)S(1)} %get-tuple-element.56.q_ref) | copy-start | bytes 3145732
  91.8 21.7 %copy-start.17 = (bf16[2048,256]{1,0:T(8,128)(2,1)}, bf16[2048,256]{1,0:T(8,128)(2,1)S(1)}, u32[]{:S(2)}) copy-start(bf16[2048,256]{1,0:T(8,128)(2,1)S(1)} %get-tuple-element.57.k_ref) | copy-start | bytes 3145732
  91.8 21.7 %copy-start.18 = (bf16[2048,256]{1,0:T(8,128)(2,1)}, bf16[2048,256]{1,0:T(8,128)(2,1)S(1)}, u32[]{:S(2)}) copy-start(bf16[2048,256]{1,0:T(8,128)(2,1)S(1)} %get-tuple-element.58.v_ref) | copy-start | bytes 3145732
  114.1 5.1 copy-start.19
  115.2 2.6 collective-permute-start.4
  115.3 6.9 %copy-start.25 = (bf16[2048,512]{1,0:T(8,128)(2,1)S(1)}, bf16[2048,512]{1,0:T(8,128)(2,1)}, u32[]{:S(2)}) copy-start(bf16[2048,512]{1,0:T(8,128)(2,1)} %cot_near_ref.3) | copy-start | bytes 6291460
  117.4 6.7 %copy-start.28 = (bf16[512,1024]{1,0:T(8,128)(2,1)S(1)}, bf16[512,1024]{1,0:T(8,128)(2,1)}, u32[]{:S(2)}) copy-start(bf16[512,1024]{1,0:T(8,128)(2,1)} %constant_dynamic-update-slice_fusion) | copy-start | bytes 3145732
  117.4 6.8 %collective-permute-start.9 = (bf16[512,1024]{1,0:T(8,128)(2,1)}, bf16[512,1024]{1,0:T(8,128)(2,1)S(1)}, u32[]{:S(2)}, u32[]{:S(2)}) collective-permute-start(bf16[512,1024]{1,0:T(8,128)(2,1)} %constant_dynamic-update-slice_fusion), channel_id=1, source_target_pairs={{0,1},{1,0},{2,3},{3,2},{4,5},{5,4},{6,7},{7,6},{8,9},{9,8},{10,11... | collective-permute-start | bytes 3145736 | tf_op jit(solution)/shard_map/ppermute | solution.py:302
  119.2 26.1 %collective-permute-start.5 = (bf16[1024,512]{1,0:T(8,128)(2,1)S(1)}, bf16[1024,512]{1,0:T(8,128)(2,1)S(1)}, u32[]{:S(2)}, u32[]{:S(2)}) collective-permute-start(bf16[1024,512]{1,0:T(8,128)(2,1)S(1)} %pad_maximum_fusion.5), channel_id=1, source_target_pairs={{0,2},{2,0},{1,3},{3,1},{4,6},{6,4},{5,7},{7,5},{8,10},{10,8},{9,1... | collective-permute-start | bytes 3145736 | tf_op jit(solution)/shard_map/ppermute | solution.py:302
  119.6 30.3 %copy-start.39 = (f32[1024]{0:T(1024)}, f32[1024]{0:T(1024)S(1)}, u32[]{:S(2)}) copy-start(f32[1024]{0:T(1024)S(1)} %pad_maximum_fusion.12) | copy-start | bytes 12292
  122.3 23.0 %copy-start.34 = (bf16[1024,256]{1,0:T(8,128)(2,1)S(1)}, bf16[1024,256]{1,0:T(8,128)(2,1)}, u32[]{:S(2)}) copy-start(bf16[1024,256]{1,0:T(8,128)(2,1)} %get-tuple-element.109) | copy-start | bytes 1572868
  122.4 44.7 %collective-permute-start.11 = (bf16[1024,512]{1,0:T(8,128)(2,1)S(1)}, bf16[1024,512]{1,0:T(8,128)(2,1)}, u32[]{:S(2)}, u32[]{:S(2)}) collective-permute-start(bf16[1024,512]{1,0:T(8,128)(2,1)S(1)} %dynamic-slice_select_fusion), channel_id=1, source_target_pairs={{0,2},{2,0},{1,3},{3,1},{4,6},{6,4},{5,7},{7,5},{8,10},{10,8},{9,1... | collective-permute-start | bytes 3145736 | tf_op jit(solution)/shard_map/ppermute | solution.py:302
  145.3 4.6 copy-start.41
  151.8 31.7 %collective-permute-start.10 = (bf16[1024,1024]{1,0:T(8,128)(2,1)S(1)}, bf16[1024,1024]{1,0:T(8,128)(2,1)}, u32[]{:S(2)}, u32[]{:S(2)}) collective-permute-start(bf16[1024,1024]{1,0:T(8,128)(2,1)S(1)} %multiply_convert_fusion), channel_id=1, source_target_pairs={{0,1},{1,0},{2,3},{3,2},{4,5},{5,4},{6,7},{7,6},{8,9},{9,8},{10,11... | collective-permute-start | bytes 6291464 | tf_op jit(solution)/shard_map/ppermute | solution.py:302
  167.0 7.4 %collective-permute-start.12 = (bf16[1024,512]{1,0:T(8,128)(2,1)}, bf16[1024,512]{1,0:T(8,128)(2,1)}, u32[]{:S(2)}, u32[]{:S(2)}) collective-permute-start(bf16[1024,512]{1,0:T(8,128)(2,1)} %collective-permute-done.11), channel_id=1, source_target_pairs={{0,1},{1,0},{2,3},{3,2},{4,5},{5,4},{6,7},{7,6},{8,9},{9,8},{10,11... | collective-permute-start | bytes 3145736 | tf_op jit(solution)/shard_map/ppermute | solution.py:302
  188.4 39.7 %copy-start.24 = (bf16[2048,512]{1,0:T(8,128)(2,1)S(1)}, bf16[2048,512]{1,0:T(8,128)(2,1)}, u32[]{:S(2)}) copy-start(bf16[2048,512]{1,0:T(8,128)(2,1)} %maximum_select_fusion.2.cot_far_ref) | copy-start | bytes 6291460
  228.0 6.2 %copy-start.26 = (bf16[2048,512]{1,0:T(8,128)(2,1)S(1)}, bf16[2048,512]{1,0:T(8,128)(2,1)}, u32[]{:S(2)}) copy-start(bf16[2048,512]{1,0:T(8,128)(2,1)} %cot_near_ref.3) | copy-start | bytes 6291460
  228.1 6.2 %copy-start.46 = (bf16[2048,1152]{1,0:T(8,128)(2,1)S(1)}, bf16[2048,1152]{1,0:T(8,128)(2,1)}, u32[]{:S(2)}) copy-start(bf16[2048,1152]{1,0:T(8,128)(2,1)} %get-tuple-element.61) | copy-start | bytes 14155780
  228.1 9.9 %slice-start = ((s8[9437184]{0:T(1024)(128)(4,1)}), s8[4194304]{0:T(1024)(128)(4,1)S(1)}, s32[]{:S(2)}) async-start(s8[9437184]{0:T(1024)(128)(4,1)} %bitcast.78), calls=%async_computation.2 | async-start | bytes 8388608
  228.1 9.9 %slice-start.1 = ((s8[9437184]{0:T(1024)(128)(4,1)}), s8[4194304]{0:T(1024)(128)(4,1)S(1)}, s32[]{:S(2)}) async-start(s8[9437184]{0:T(1024)(128)(4,1)} %bitcast.78), calls=%async_computation.3 | async-start | bytes 8388608
  351.9 74.9 %copy-start.7 = (bf16[512,512]{1,0:T(8,128)(2,1)S(1)}, bf16[512,512]{1,0:T(8,128)(2,1)}, u32[]{:S(2)}) copy-start(bf16[512,512]{1,0:T(8,128)(2,1)} %pad_maximum_fusion.8.w_near_ref) | copy-start | bytes 1572868
  428.0 16.3 %copy-start.32 = (bf16[2048,512]{1,0:T(8,128)(2,1)S(1)}, bf16[2048,512]{1,0:T(8,128)(2,1)}, u32[]{:S(2)}) copy-start(bf16[2048,512]{1,0:T(8,128)(2,1)} %slice.116) | copy-start | bytes 6291460
  428.1 16.3 %copy-start.35 = (bf16[1024,256]{1,0:T(8,128)(2,1)S(1)}, bf16[1024,256]{1,0:T(8,128)(2,1)}, u32[]{:S(2)}) copy-start(bf16[1024,256]{1,0:T(8,128)(2,1)} %get-tuple-element.109) | copy-start | bytes 1572868
  428.1 16.3 %copy-start.42 = (bf16[1024,512]{1,0:T(8,128)(2,1)S(1)}, bf16[1024,512]{1,0:T(8,128)(2,1)}, u32[]{:S(2)}) copy-start(bf16[1024,512]{1,0:T(8,128)(2,1)} %copy-done.41) | copy-start | bytes 3145732
  448.0 7.3 %collective-permute-start.13 = (bf16[512,512]{1,0:T(8,128)(2,1)}, bf16[512,512]{1,0:T(8,128)(2,1)}, u32[]{:S(2)}, u32[]{:S(2)}) collective-permute-start(bf16[512,512]{1,0:T(8,128)(2,1)} %pad_maximum_fusion.10), channel_id=1, source_target_pairs={{0,1},{1,0},{2,3},{3,2},{4,5},{5,4},{6,7},{7,6},{8,9},{9,8},{10,11... | collective-permute-start | bytes 1572872 | tf_op jit(solution)/shard_map/ppermute | solution.py:302
  457.5 75.7 %copy-start.4 = (bf16[2,8,144,512]{3,2,1,0:T(8,128)(2,1)S(1)}, bf16[2,8,144,512]{3,2,1,0:T(8,128)(2,1)}, u32[]{:S(2)}) copy-start(bf16[2,8,144,512]{3,2,1,0:T(8,128)(2,1)} %get-tuple-element.88) | copy-start | bytes 7077892
  537.8 6.4 %copy-start.31 = (bf16[2048,512]{1,0:T(8,128)(2,1)S(1)}, bf16[2048,512]{1,0:T(8,128)(2,1)}, u32[]{:S(2)}) copy-start(bf16[2048,512]{1,0:T(8,128)(2,1)} %get-tuple-element.159) | copy-start | bytes 6291460
  (18 other events, 39.4 us)
Sparse Core Ops, SparseCore 0:
  67.7 42.6 all-gather.4
  115.4 48.3 all-gather.2

commit v5 on v4

--- a/solution.py
+++ b/solution.py
@@ -26,87 +26,6 @@
     zero = jnp.zeros_like(x)
     return jnp.concatenate([jnp.where(first, x, zero), jnp.where(first, zero, x)], axis=0)
 
-def attend_kernel(bq, bk, first_ref, last_ref, q_ref, k_ref, v_ref, start_ref, low_ref, raw_ref, lse_ref, acc_ref, mass_ref):
-    i = pl.program_id(1)
-    qs = stacked(q_ref[...])
-    starts = start_ref[...]
-    starts = jnp.concatenate([starts, starts], axis=0)
-    acc_ref[...] = jnp.zeros_like(acc_ref)
-    mass_ref[...] = jnp.zeros_like(mass_ref)
-    rows = i * bq + lax.rem(lax.broadcasted_iota(jnp.int32, (2 * bq, 1), 0), bq)
-
-    def step(j, masked):
-        k0 = pl.multiple_of(j * bk, bk)
-        s = dot(qs, k_ref[pl.ds(k0, bk), :], NT)
-        p = jnp.exp(s)
-        if masked:
-            cols = j * bk + lax.broadcasted_iota(jnp.int32, (1, bk), 1)
-            p = jnp.where((cols <= rows) & (cols >= starts), p, 0.0)
-        mass = p[:, :128]
-        for n in range(1, bk // 128):
-            mass = mass + p[:, n * 128:(n + 1) * 128]
-        mass_ref[...] += mass
-        acc_ref[...] += dot(p.astype(BF16), v_ref[pl.ds(k0, bk), :])
-
-    low = first_ref[i] // bk
-    clear = jnp.maximum((last_ref[i] + bk - 1) // bk, low)
-    diagonal = (i * bq) // bk
-    end = ((i + 1) * bq + bk - 1) // bk
-    clear = jnp.minimum(clear, diagonal)
-
-    @pl.loop(low, clear)
-    def _(j):
-        step(j, True)
-
-    @pl.loop(clear, diagonal)
-    def _(j):
-        step(j, False)
-
-    @pl.loop(diagonal, end)
-    def _(j):
-        step(j, True)
-
-    mass = jnp.sum(mass_ref[...], axis=1, keepdims=True)
-    out = acc_ref[...] / mass
-    first = lax.broadcasted_iota(jnp.int32, (bq, 128), 1) < 64
-    out = jnp.where(first, out[:bq], out[bq:])
-    raw_ref[...] = out
-    low_ref[...] = out.astype(BF16)
-    total = jnp.log(jnp.sum(mass_ref[...].T, axis=0, keepdims=True))
-    lse_ref[0, 0:1, :] = total[:, :bq]
-    lse_ref[0, 1:2, :] = total[:, bq:]
-
-def attend(q, k, v, starts, bq=512, bk=512):
-    T, width = q.shape
-    groups = width // 128
-    first, last = starts[::bq], starts[bq - 1::bq]
-    kern = functools.partial(attend_kernel, bq, bk)
-    pairs = T * (T + bk) // 2
-    return pl.pallas_call(
-        kern,
-        out_shape=(jax.ShapeDtypeStruct((T, width), BF16), jax.ShapeDtypeStruct((T, width), F32),
-                   jax.ShapeDtypeStruct((groups, 2, T), F32)),
-        grid_spec=pltpu.PrefetchScalarGridSpec(
-            num_scalar_prefetch=2, grid=(groups, T // bq),
-            in_specs=[
-                pl.BlockSpec((bq, 128), lambda g, i, *_: (i, g)),
-                pl.BlockSpec((T, 128), lambda g, i, *_: (0, g)),
-                pl.BlockSpec((T, 128), lambda g, i, *_: (0, g)),
-                pl.BlockSpec((bq, 1), lambda g, i, *_: (i, 0)),
-            ],
-            out_specs=[
-                pl.BlockSpec((bq, 128), lambda g, i, *_: (i, g)),
-                pl.BlockSpec((bq, 128), lambda g, i, *_: (i, g)),
-                pl.BlockSpec((1, 2, bq), lambda g, i, *_: (g, 0, i)),
-            ],
-            scratch_shapes=[pltpu.VMEM((2 * bq, 128), F32), pltpu.VMEM((2 * bq, 128), F32)],
-        ),
-        compiler_params=pltpu.CompilerParams(vmem_limit_bytes=40 << 20),
-        cost_estimate=pl.CostEstimate(flops=4 * groups * 2 * pairs * 256, transcendentals=2 * groups * pairs,
-                                      bytes_accessed=10 * T * width),
-        name="attend",
-    )(first, last, q, k, v, starts[:, None])
-
 
 def head_sums(x):
     first = lax.broadcasted_iota(jnp.int32, x.shape, 1) < HEAD_SIZE
@@ -126,81 +45,15 @@
     return jnp.where(first, x, other), jnp.where(first, other, x)
 
 
-def project_kernel(groups, near_ref, far_ref, gain_near_ref, gain_far_ref, w_near_ref, w_far_ref, q_gain_ref, k_gain_ref,
-                   cos_ref, sin_ref, hid_near_ref, hid_far_ref, raw_ref, q_ref, k_ref, v_ref):
-    near = near_ref[...].astype(F32)
-    far = far_ref[...].astype(F32)
-    width = near.shape[1] + far.shape[1]
-    total = jnp.sum(near * near, axis=1, keepdims=True) + jnp.sum(far * far, axis=1, keepdims=True)
-    inverse = lax.rsqrt(total / width + EPSILON)
-    hid_near = (near * inverse * gain_near_ref[...]).astype(BF16)
-    hid_far = (far * inverse * gain_far_ref[...]).astype(BF16)
-    hid_near_ref[...] = hid_near
-    hid_far_ref[...] = hid_far
-    raw = dot(hid_near, w_near_ref[...]) + dot(hid_far, w_far_ref[...])
-    cosine, sine = cos_ref[...], sin_ref[...]
-
-    def prepared(x, gain):
-        normed = x * lax.rsqrt(head_sums(x * x) / HEAD_SIZE + EPSILON) * gain
-        return normed * cosine + swapped(normed) * sine
-
-    lanes = 2 * HEAD_SIZE
-    kv = groups * HEAD_SIZE
-    raw_ref[...] = raw[:, :groups * lanes + kv]
-    for n in range(groups):
-        cut = slice(n * lanes, (n + 1) * lanes)
-        q_ref[:, cut] = (prepared(raw[:, cut], q_gain_ref[...]).astype(BF16) * HEAD_SIZE ** (-0.5)).astype(BF16)
-    for n in range(groups // 2):
-        at = groups * lanes + n * lanes
-        twice = doubled(prepared(raw[:, at:at + lanes], k_gain_ref[...]))
-        for m in range(2):
-            k_ref[:, (2 * n + m) * lanes:(2 * n + m + 1) * lanes] = twice[m].astype(BF16)
-        at += kv
-        twice = doubled(raw[:, at:at + lanes])
-        for m in range(2):
-            v_ref[:, (2 * n + m) * lanes:(2 * n + m + 1) * lanes] = twice[m].astype(BF16)
-
-
-def project(near, far, gain_near, gain_far, w_near, w_far, q_gain, k_gain, cosine, sine, rows=512):
-    packed, half = near.shape
-    columns = w_near.shape[1]
-    groups = columns // (4 * HEAD_SIZE)
-    width = groups * 2 * HEAD_SIZE
-    kv = groups * HEAD_SIZE
-    rows = min(rows, packed)
-
-    def tile(n):
-        return pl.BlockSpec((rows, n), lambda i: (i, 0))
-
-    def whole(x):
-        return pl.BlockSpec(x.shape, lambda i: (0, 0))
-
-    def out(n, dtype):
-        return jax.ShapeDtypeStruct((packed, n), dtype)
-
-    small = (gain_near, gain_far, w_near, w_far, q_gain, k_gain)
-    return pl.pallas_call(
-        functools.partial(project_kernel, groups),
-        out_shape=(out(half, BF16), out(half, BF16), out(width + kv, F32), out(width, BF16), out(width, BF16), out(width, BF16)),
-        grid=(packed // rows,),
-        in_specs=[tile(half), tile(half), *map(whole, small), tile(2 * HEAD_SIZE), tile(2 * HEAD_SIZE)],
-        out_specs=(tile(half), tile(half), tile(width + kv), tile(width), tile(width), tile(width)),
-        compiler_params=pltpu.CompilerParams(vmem_limit_bytes=40 << 20),
-        cost_estimate=pl.CostEstimate(flops=4 * packed * half * columns, transcendentals=packed * 8,
-                                      bytes_accessed=packed * (8 * half + 10 * width)),
-        name="project",
-    )(near, far, *small, cosine, sine)
-
-
 def project_back_kernel(groups, dq_ref, dk_ref, dv_ref, raw_ref, near_ref, far_ref, gain_near_ref, gain_far_ref,
-                        w_near_ref, w_far_ref, q_gain_ref, k_gain_ref, cos_ref, sin_ref,
+                        w_near_ref, w_far_ref, q_gain_ref, k_gain_ref, table_ref,
                         grads_ref, to_near_ref, to_far_ref, stat_ref, q_sum_ref, k_sum_ref, near_sum_ref, far_sum_ref):
     @pl.when(pl.program_id(0) == 0)
     def _():
         for ref in (q_sum_ref, k_sum_ref, near_sum_ref, far_sum_ref):
             ref[...] = jnp.zeros_like(ref)
 
-    cosine, sine = cos_ref[...], sin_ref[...]
+    cosine, sine = rope_block(table_ref, slice(None))
     lanes = 2 * HEAD_SIZE
     first = lax.broadcasted_iota(jnp.int32, cosine.shape, 1) < HEAD_SIZE
 
@@ -244,7 +97,7 @@
     stat_ref[...] = jnp.where(first, stat, inverse)
 
 
-def project_back(dq, dk, dv, raw, near, far, gain_near, gain_far, w_near, w_far, q_gain, k_gain, cosine, sine, rows=512):
+def project_back(dq, dk, dv, raw, near, far, gain_near, gain_far, w_near, w_far, q_gain, k_gain, table, rows=512):
     packed, half = near.shape
     columns = w_near.shape[1]
     groups = columns // (4 * HEAD_SIZE)
@@ -271,13 +124,13 @@
                    out(half, F32, 1), out(half, F32, 1)),
         grid=(packed // rows,),
         in_specs=[tile(width)] * 3 + [tile(raw.shape[1]), tile(half), tile(half), *map(whole, small),
-                  tile(lanes), tile(lanes)],
+                  pl.BlockSpec((table.shape[0], rows), lambda i: (0, i))],
         out_specs=(tile(columns), tile(half), tile(half), tile(lanes), kept(lanes), kept(lanes), kept(half), kept(half)),
         compiler_params=pltpu.CompilerParams(vmem_limit_bytes=44 << 20),
         cost_estimate=pl.CostEstimate(flops=4 * packed * half * columns, transcendentals=packed * 8,
                                       bytes_accessed=packed * (8 * half + 18 * width)),
         name="project_back",
-    )(dq, dk, dv, raw, near, far, *small, cosine, sine)
+    )(dq, dk, dv, raw, near, far, *small, table)
 
 
 def layout(lengths, packed):
@@ -290,12 +143,11 @@
     return jnp.sum(jnp.where(member[:, None] == numbers[None, :], begins[None, :], 0), axis=1)
 
 
-def rope_tables(position):
+def rope_table(position):
     half = HEAD_SIZE // 2
     inverse = jnp.exp(jnp.arange(half, dtype=F32) * (-2.0 * math.log(ROPE_BASE) / HEAD_SIZE))
-    angles = position.astype(F32)[:, None] * inverse[None, :]
-    cosine, sine = jnp.cos(angles), jnp.sin(angles)
-    return jnp.concatenate([cosine] * 4, axis=1), jnp.concatenate([-sine, sine] * 2, axis=1)
+    angles = position.astype(F32)[None, :] * inverse[:, None]
+    return jnp.concatenate([jnp.cos(angles), jnp.sin(angles)], axis=0)
 
 
 def swap(x, axis):
@@ -315,12 +167,13 @@
     return dot(left, right, (((0,), (0,)), ((), ())))
 
 
-def feed_kernel(units, hidden_ref, cot_near_ref, cot_far_ref, gate_up_ref, down_ref, active_ref, grads_ref, result_ref, back_ref):
+def feed_kernel(units, row_ref, hidden_ref, cot_near_ref, cot_far_ref, gate_ref, up_ref, far_ref, down_near_ref, down_far_ref,
+                active_ref, grads_ref, result_ref, back_ref):
     half = cot_near_ref.shape[1]
-    hidden = hidden_ref[...]
-    gate = dot(hidden, gate_up_ref[:, :units])
-    upward = dot(hidden, gate_up_ref[:, units:])
-    grad_active = dot(cot_near_ref[...], down_ref[:, :half], NT) + dot(cot_far_ref[...], down_ref[:, half:], NT)
+    near, far = hidden_ref[:, :half], hidden_ref[:, half:]
+    gate = dot(near, gate_ref[...]) + dot(far, far_ref[:, :units])
+    upward = dot(near, up_ref[...]) + dot(far, far_ref[:, units:])
+    grad_active = dot(cot_near_ref[...], down_near_ref[...], NT) + dot(cot_far_ref[...], down_far_ref[...], NT)
     sig = 1.0 / (1.0 + jnp.exp(-gate))
     lifted = gate * sig
     active = (lifted * upward).astype(BF16)
@@ -329,54 +182,61 @@
     active_ref[...] = active
     grads_ref[:, :units] = grad_gate
     grads_ref[:, units:] = grad_up
-    result_ref[...] = dot(active, down_ref[...]).astype(BF16)
-    back = dot(grad_gate, gate_up_ref[:, :units], NT) + dot(grad_up, gate_up_ref[:, units:], NT)
-    back_ref[...] = back.astype(BF16)
-
-
-def feed(hidden, cot_near, cot_far, gate_up, down, rows=256):
+    result_ref[:, :half] = dot(active, down_near_ref[...]).astype(BF16)
+    result_ref[:, half:] = dot(active, down_far_ref[...]).astype(BF16)
+    back_ref[:, :half] = (dot(grad_gate, gate_ref[...], NT) + dot(grad_up, up_ref[...], NT)).astype(BF16)
+    back_ref[:, half:] = (dot(grad_gate, far_ref[:, :units], NT) + dot(grad_up, far_ref[:, units:], NT)).astype(BF16)
+
+
+def feed(row, hidden, cot_near, cot_far, gate, up, far, down, down_far, rows=256):
     packed, width = hidden.shape
-    units = down.shape[0]
+    units, half = down_far.shape
     rows = min(rows, packed)
 
     def tile(n):
-        return pl.BlockSpec((rows, n), lambda i: (i, 0))
-
-    def whole(x):
-        return pl.BlockSpec(x.shape, lambda i: (0, 0), pipeline_mode=pl.Buffered(1))
+        return pl.BlockSpec((rows, n), lambda i, row: (i, 0))
+
+    def once(shape, place):
+        return pl.BlockSpec(shape, place, pipeline_mode=pl.Buffered(1))
 
     def out(n):
         return jax.ShapeDtypeStruct((packed, n), BF16)
 
+    columns = once((half, units), lambda i, row: (0, row[0]))
     return pl.pallas_call(
         functools.partial(feed_kernel, units),
         out_shape=(out(units), out(2 * units), out(width), out(width)),
-        grid=(packed // rows,),
-        in_specs=[tile(width), tile(width // 2), tile(width // 2), whole(gate_up), whole(down)],
-        out_specs=(tile(units), tile(2 * units), tile(width), tile(width)),
+        grid_spec=pltpu.PrefetchScalarGridSpec(
+            num_scalar_prefetch=1, grid=(packed // rows,),
+            in_specs=[tile(width), tile(half), tile(half), columns, columns, once(far.shape, lambda i, row: (0, 0)),
+                      once((units, half), lambda i, row: (row[0], 0)), once(down_far.shape, lambda i, row: (0, 0))],
+            out_specs=(tile(units), tile(2 * units), tile(width), tile(width)),
+        ),
         compiler_params=pltpu.CompilerParams(vmem_limit_bytes=56 << 20),
         cost_estimate=pl.CostEstimate(flops=12 * packed * width * units, transcendentals=packed * units,
                                       bytes_accessed=packed * (8 * width + 6 * units) + 6 * width * units),
         name="feed",
-    )(hidden, cot_near, cot_far, gate_up, down)
+    )(row, hidden, cot_near, cot_far, gate, up, far, down, down_far)
 
 
 class Group:
-    def __init__(self, names, n):
+    def __init__(self, names, total, n=None):
+        n = total if n is None else n
         self.n = n
         self.dp, self.row, self.col = (lax.axis_index(name) for name in names)
-        side = self.dp % 2
-        self.place = (self.dp // 2) * (1 - side) + (n - 1 - self.dp // 2) * side
+        self.base, member = (self.dp // n) * n, self.dp % n
+        side = member % 2
+        self.place = (member // 2) * (1 - side) + (n - 1 - member // 2) * side
         self.across = (self.dp, 1 - self.row, self.col)
         self.beside = (self.dp, self.row, 1 - self.col)
         self.opposite = (self.dp, 1 - self.row, 1 - self.col)
-        self.along = [((self.dp + k) % n, self.row, self.col) for k in range(1, n)]
+        self.along = [((self.dp + k) % total, self.row, self.col) for k in range(1, total)]
         self.ring = [(self.at(self.place + 1), self.row, self.col), (self.at(self.place - 1), self.row, self.col)]
 
     def at(self, position):
         position = (position + 2 * self.n) % self.n
         back = position // (self.n // 2)
-        return (position * (1 - back) + (self.n - 1 - position) * back) * 2 + back
+        return self.base + (position * (1 - back) + (self.n - 1 - position) * back) * 2 + back
 
     def arrive(self, targets):
         barrier = pltpu.get_barrier_semaphore()
@@ -484,6 +344,341 @@
         return carry
 
     lax.fori_loop(0, n - 1, each, 0)
+
+
+def begin_kernel(n, m, names, b, token_ref, cot_ref, wq_ref, wk_ref, wv_ref, gate_ref, up_ref, down_ref, wo_ref, gains_ref,
+                 q_gain_ref, k_gain_ref, table_ref, starts_ref,
+                 far_out, gate_up_out, down_out, cot_out, gains_out, hid_near_out, hid_far_out, raw_out, q_out, k_out, v_out,
+                 heads_out, totals_out, attended_out, middle_out, hidden_out, wo_out, w_near_out, w_far_out,
+                 near, far, w_near, w_far, wo_far, wo_all, hid_near, hid_far, raw, q_all, k_all, v_all, low, heads, attended,
+                 middle, hidden, acc_ref, mass_ref,
+                 local_sem, store_sem, token_send, token_recv, pass_send, pass_recv, piece_send, piece_recv, cot_send, cot_recv,
+                 qkv_send, qkv_recv, wide_send, wide_recv, thin_send, thin_recv, out_send, out_recv, wo_send, wo_recv,
+                 low_send, low_recv, hidden_send, hidden_recv):
+    me = Group(names, n, m)
+    packed, half = token_ref.shape
+    count = packed // 2
+    row, col = me.row, me.col
+    lanes = 2 * HEAD_SIZE
+    groups = q_all.shape[1] // lanes
+    width = groups * lanes
+    kv = groups * HEAD_SIZE
+    units = gate_ref.shape[1] // 2
+    chunk = half // m
+    down_chunk = units // m
+    pieces = 4
+    rows = count // pieces
+    me.arrive([*me.ring, me.across, me.beside, me.opposite])
+
+    def at(begin, size):
+        return pl.ds(pl.multiple_of(begin, size), size)
+
+    def own_rows(k):
+        return at(col * count + k * rows, rows)
+
+    def other_rows(k):
+        return at((1 - col) * count + k * rows, rows)
+
+    def piece(k, src, dst):
+        return remote(src, dst, piece_send.at[k], piece_recv.at[k], me.across)
+
+    up_chunk, low_chunk = me.own(0), me.own(1)
+    first_rows, second_rows = at(up_chunk * chunk, chunk), at(low_chunk * chunk, chunk)
+    qkv_pieces = [
+        piece(0, wq_ref.at[first_rows, at((1 - row) * width, width)], w_far.at[up_chunk, :, pl.ds(0, width)]),
+        piece(1, wk_ref.at[second_rows, at((1 - row) * kv, kv)], w_far.at[low_chunk, :, pl.ds(width, kv)]),
+        piece(2, wv_ref.at[second_rows, at((1 - row) * kv, kv)], w_far.at[low_chunk, :, pl.ds(width + kv, kv)]),
+        piece(3, gains_ref, gains_out),
+    ]
+    down_first = at((1 - row) * units + up_chunk * down_chunk, down_chunk)
+    down_second = at((1 - row) * units + low_chunk * down_chunk, down_chunk)
+    late_pieces = [
+        piece(4, wo_ref.at[first_rows, pl.ds(0, half // 2)], wo_far.at[up_chunk, :, pl.ds(0, half // 2)]),
+        piece(5, wo_ref.at[second_rows, pl.ds(half // 2, half // 2)], wo_far.at[low_chunk, :, pl.ds(half // 2, half // 2)]),
+        piece(6, gate_ref.at[first_rows, at((1 - row) * units, units)], gate_up_out.at[up_chunk, :, pl.ds(0, units)]),
+        piece(7, up_ref.at[second_rows, at((1 - row) * units, units)], gate_up_out.at[low_chunk, :, pl.ds(units, units)]),
+        piece(8, down_ref.at[down_first, pl.ds(0, half // 2)], down_out.at[up_chunk, :, pl.ds(0, half // 2)]),
+        piece(9, down_ref.at[down_second, pl.ds(half // 2, half // 2)], down_out.at[low_chunk, :, pl.ds(half // 2, half // 2)]),
+    ]
+    token_copies = [remote(token_ref.at[own_rows(k), :], far.at[own_rows(k), :], token_send.at[k], token_recv.at[k], me.across)
+                    for k in range(pieces)]
+    passes = [remote(far.at[own_rows(k), :], far.at[own_rows(k), :], pass_send.at[k], pass_recv.at[k], me.beside)
+              for k in range(pieces)]
+    cots = [remote(cot_ref.at[own_rows(k), :], cot_out.at[own_rows(k), :], cot_send.at[0, k], cot_recv.at[0, k], me.across)
+            for k in range(pieces)]
+    cot_passes = [remote(cot_out.at[own_rows(k), :], cot_out.at[own_rows(k), :], cot_send.at[1, k], cot_recv.at[1, k], me.beside)
+                  for k in range(pieces)]
+    for each in qkv_pieces + token_copies:
+        each.start()
+
+    def fetch(k, src, dst):
+        return pltpu.make_async_copy(src, dst, local_sem.at[k])
+
+    quarter = half // 2
+    mine_rows, other_quarter = at(row * quarter, quarter), at((1 - row) * quarter, quarter)
+    fetches = [
+        fetch(0, token_ref, near),
+        fetch(1, wq_ref.at[:, at(row * width, width)], w_near.at[:, pl.ds(0, width)]),
+        fetch(2, wk_ref.at[:, at(row * kv, kv)], w_near.at[:, pl.ds(width, kv)]),
+        fetch(3, wv_ref.at[:, at(row * kv, kv)], w_near.at[:, pl.ds(width + kv, kv)]),
+        fetch(4, wo_ref.at[mine_rows, :], wo_all.at[pl.ds(0, quarter), pl.ds(0, half)]),
+        fetch(5, wo_ref.at[other_quarter, :], wo_all.at[pl.ds(2 * quarter, quarter), pl.ds(0, half)]),
+    ]
+    for each in fetches:
+        each.start()
+
+    def wo_copy(k, src, rows_at, side):
+        return remote(src, wo_all.at[pl.ds(rows_at, quarter), pl.ds(side, half)], wo_send.at[k], wo_recv.at[k], me.beside)
+
+    wo_copies = [wo_copy(0, wo_ref.at[mine_rows, :], quarter, 0), wo_copy(1, wo_ref.at[other_quarter, :], 3 * quarter, 0)]
+    for each in wo_copies:
+        each.start()
+
+    qkv = Spread(me, w_far, qkv_send, qkv_recv)
+    wide = Spread(me, gate_up_out, wide_send, wide_recv)
+    thin = Spread(me, down_out, thin_send, thin_recv)
+    wo = Spread(me, wo_far, out_send, out_recv)
+    for each in qkv_pieces:
+        each.wait()
+    for s in range(2):
+        qkv.start(s)
+    for k in range(pieces):
+        steps(k * (m - 1) // pieces, (k + 1) * (m - 1) // pieces, qkv)
+        token_copies[k].wait()
+        passes[k].start()
+        if k == pieces // 2:
+            for each in late_pieces:
+                each.start()
+    for each in cots:
+        each.start()
+    for each in fetches:
+        each.wait()
+
+    def prepared(x, gain, cosine, sine):
+        normed = x * lax.rsqrt(head_sums(x * x) / HEAD_SIZE + EPSILON) * gain
+        return normed * cosine + swapped(normed) * sine
+
+    far_gains = gains_out
+
+    def project_block(k):
+        block = at(((col * pieces + 2 * k) % (2 * pieces)) * rows, 2 * rows)
+        x_near = near[block, :].astype(F32)
+        x_far = far[block, :].astype(F32)
+        total = jnp.sum(x_near * x_near, axis=1, keepdims=True) + jnp.sum(x_far * x_far, axis=1, keepdims=True)
+        inverse = lax.rsqrt(total / (2 * half) + EPSILON)
+        h_near = (x_near * inverse * gains_ref[0:1, :]).astype(BF16)
+        h_far = (x_far * inverse * far_gains[0:1, :]).astype(BF16)
+        hid_near[block, :] = h_near
+        hid_far[block, :] = h_far
+        out = dot(h_near, w_near[...]) + dot(h_far, w_far[...].reshape(half, w_far.shape[2]))
+        raw[block, :] = out[:, :width + kv]
+        cosine, sine = rope_block(table_ref, block)
+        for g in range(groups):
+            cut = slice(g * lanes, (g + 1) * lanes)
+            part = prepared(out[:, cut], q_gain_ref[...], cosine, sine).astype(BF16)
+            q_all[block, cut] = (part * HEAD_SIZE ** (-0.5)).astype(BF16)
+        for g in range(groups // 2):
+            begin = width + g * lanes
+            twice = doubled(prepared(out[:, begin:begin + lanes], k_gain_ref[...], cosine, sine))
+            value = doubled(out[:, begin + kv:begin + kv + lanes])
+            for h in range(2):
+                cut = slice((2 * g + h) * lanes, (2 * g + h + 1) * lanes)
+                k_all[block, cut] = twice[h].astype(BF16)
+                v_all[block, cut] = value[h].astype(BF16)
+
+    rings = (wide, thin, wo)
+    slots = 3 + groups * (packed // b) * (packed // b + 1) // 2
+
+    def tick(k):
+        steps((k * (m - 1)) // slots, ((k + 1) * (m - 1)) // slots, *rings)
+
+    project_block(0)
+    for each in late_pieces:
+        each.wait()
+    for ring in rings:
+        for s in range(2):
+            ring.start(s)
+    project_block(1)
+    tick(0)
+    for k in range(pieces):
+        passes[k].wait()
+        if k % 2 == 1:
+            project_block(2 + k // 2)
+            tick(1 + k // 2)
+
+    def store(k, src, dst):
+        return pltpu.make_async_copy(src, dst, store_sem.at[k])
+
+    stores = [store(k, src, dst) for k, (src, dst) in enumerate((
+        (far, far_out), (hid_near, hid_near_out), (hid_far, hid_far_out), (raw, raw_out), (q_all, q_out), (k_all, k_out),
+        (v_all, v_out)))]
+    for each in stores:
+        each.start()
+
+    blocks = packed // b
+    per_half = blocks // 2
+
+    def low_copy(kind, g, i, target):
+        slot = (2, 1, 3)[kind] * width + g * lanes
+        return remote(low.at[at(i * b, b), pl.ds(g * lanes, lanes)],
+                      attended.at[at((i % per_half) * b, b), pl.ds(slot, lanes)],
+                      low_send.at[kind, g, i % per_half], low_recv.at[kind, g, i % per_half], target)
+
+    for g in range(groups):
+        cut = slice(g * lanes, (g + 1) * lanes)
+
+        def query_block(i, carry, g=g, cut=cut):
+            place = at(i * b, b)
+            qs = stacked(q_all[place, cut])
+            begins = starts_ref[place, :]
+            begins = jnp.concatenate([begins, begins], axis=0)
+            acc_ref[...] = jnp.zeros_like(acc_ref)
+            mass_ref[...] = jnp.zeros_like(mass_ref)
+            base = 3 + g * (blocks * (blocks + 1) // 2) + (i * (i + 1)) // 2
+
+            def key_block(j, diagonal):
+                keys = at(j * b, b)
+                s = dot(qs, k_all[keys, cut], NT)
+                columns = j * b + lax.broadcasted_iota(jnp.int32, (1, b), 1)
+                allowed = columns >= begins
+                if diagonal:
+                    lines = i * b + lax.rem(lax.broadcasted_iota(jnp.int32, (2 * b, 1), 0), b)
+                    allowed = allowed & (columns <= lines)
+                p = jnp.where(allowed, jnp.exp(s), 0.0)
+                mass = p[:, :128]
+                for part in range(1, b // 128):
+                    mass = mass + p[:, part * 128:(part + 1) * 128]
+                mass_ref[...] += mass
+                acc_ref[...] += dot(p.astype(BF16), v_all[keys, cut])
+                tick(base + j)
+
+            @pl.loop(0, i)
+            def _(j):
+                key_block(j, False)
+
+            key_block(i, True)
+            mass = jnp.sum(mass_ref[...], axis=1, keepdims=True)
+            out = acc_ref[...] / mass
+            first = lax.broadcasted_iota(jnp.int32, (b, lanes), 1) < HEAD_SIZE
+            out = jnp.where(first, out[:b], out[b:])
+            heads[place, cut] = out
+            low[place, cut] = out.astype(BF16)
+            total = jnp.log(jnp.sum(mass_ref[...].T, axis=0, keepdims=True))
+            totals_out[g, 0:1, place] = total[:, :b]
+            totals_out[g, 1:2, place] = total[:, b:]
+
+            @pl.when(i // per_half == col)
+            def _():
+                attended[at((i % per_half) * b, b), cut] = out.astype(BF16)
+                low_copy(0, g, i, me.across).start()
+
+            @pl.when(i // per_half != col)
+            def _():
+                low_copy(1, g, i, me.beside).start()
+                low_copy(2, g, i, me.opposite).start()
+            return carry
+
+        lax.fori_loop(0, blocks, query_block, 0)
+    heads_store = store(7, heads, heads_out)
+    heads_store.start()
+    w_stores = [store(8 + 3 * per_half, w_near, w_near_out), store(9 + 3 * per_half, w_far, w_far_out)]
+    for each in w_stores:
+        each.start()
+
+    local_far = []
+    per = quarter // chunk
+    for p, begin in ((0, row), (2, 1 - row)):
+        for k in range(per):
+            local_far.append(pltpu.make_async_copy(
+                wo_far.at[begin * per + k], wo_all.at[pl.ds(p * quarter + k * chunk, chunk), pl.ds(half, half)],
+                local_sem.at[6 + len(local_far)]))
+    remote_far = []
+    for p, begin in ((1, row), (3, 1 - row)):
+        for k in range(per):
+            remote_far.append(remote(
+                wo_far.at[begin * per + k], wo_all.at[pl.ds(p * quarter + k * chunk, chunk), pl.ds(half, half)],
+                wo_send.at[2 + len(remote_far)], wo_recv.at[2 + len(remote_far)], me.beside))
+    for each in local_far + remote_far:
+        each.start()
+    for k in range(pieces):
+        cots[k].wait()
+        cot_passes[k].start()
+    for each in local_far + remote_far + wo_copies:
+        each.wait()
+    w_stores.append(store(10 + 3 * per_half, wo_all.at[pl.ds(0, quarter), :], wo_out))
+    w_stores[-1].start()
+
+    gain = jnp.concatenate([gains_ref[1:2, :], far_gains[1:2, :]], axis=1)
+    hidden_stores = []
+    for k in range(per_half):
+        for g in range(groups):
+            for kind in range(3):
+                low_copy(kind, g, k, me.beside).wait()
+        part = slice(k * b, (k + 1) * b)
+        place = at(col * count + k * b, b)
+        tokens = jnp.concatenate([near[place, :], far[place, :]], axis=1).astype(F32)
+        total = tokens + dot(attended[part, :], wo_all[...])
+        middle[part, :] = total
+        inverse = lax.rsqrt(jnp.sum(total * total, axis=1, keepdims=True) / (2 * half) + EPSILON)
+        hidden[part, :] = (total * inverse * gain).astype(BF16)
+        hidden_stores += [
+            remote(hidden.at[pl.ds(k * b, b), :], hidden_out.at[place, :], hidden_send.at[k], hidden_recv.at[k], me.beside),
+            pltpu.make_async_copy(hidden.at[pl.ds(k * b, b), :], hidden_out.at[place, :], store_sem.at[8 + 3 * k]),
+            pltpu.make_async_copy(middle.at[pl.ds(k * b, b), :], middle_out.at[pl.ds(k * b, b), :], store_sem.at[9 + 3 * k]),
+            pltpu.make_async_copy(attended.at[pl.ds(k * b, b), :], attended_out.at[pl.ds(k * b, b), :], store_sem.at[10 + 3 * k]),
+        ]
+        for each in hidden_stores[-4:]:
+            each.start()
+    for each in stores + [heads_store] + w_stores + hidden_stores + cot_passes:
+        each.wait()
+    finish(m, qkv, *rings)
+
+
+def rope_block(table_ref, block):
+    half = HEAD_SIZE // 2
+    cosine, sine = table_ref[:half, block], table_ref[half:, block]
+    return jnp.concatenate([cosine] * 4, axis=0).T, jnp.concatenate([-sine, sine] * 2, axis=0).T
+
+
+def begin(tokens, cot, wq, wk, wv, gate, up, down, wo, gains, q_gain, k_gain, table, starts, names, n, b=512):
+    packed, half = tokens.shape
+    b = min(b, packed // 2)
+    m = math.gcd(n, 8)
+    width, kv, units = wq.shape[1] // 2, wk.shape[1] // 2, gate.shape[1] // 2
+    groups = width // (2 * HEAD_SIZE)
+    count = packed // 2
+    vmem = pl.BlockSpec(memory_space=pltpu.VMEM)
+    some = pl.BlockSpec(memory_space=pl.ANY)
+    dma = pltpu.SemaphoreType.DMA
+
+    outs = [((packed, half), BF16, some), ((m, half // m, 2 * units), BF16, some), ((m, units // m, half), BF16, some),
+            ((packed, half), BF16, some), (gains.shape, F32, vmem), ((packed, half), BF16, some), ((packed, half), BF16, some),
+            ((packed, width + kv), F32, some), ((packed, width), BF16, some), ((packed, width), BF16, some),
+            ((packed, width), BF16, some), ((packed, width), F32, some), ((groups, 2, packed), F32, vmem),
+            ((count, 2 * half), BF16, some), ((count, 2 * half), F32, some), ((packed, 2 * half), BF16, some),
+            ((half // 2, 2 * half), BF16, some), ((half, width + 2 * kv), BF16, some), ((m, half // m, width + 2 * kv), BF16, some)]
+    scratch = [((packed, half), BF16), ((packed, half), BF16), ((half, width + 2 * kv), BF16), ((m, half // m, width + 2 * kv), BF16),
+               ((m, half // m, half), BF16), ((2 * half, 2 * half), BF16), ((packed, half), BF16), ((packed, half), BF16),
+               ((packed, width + kv), F32), ((packed, width), BF16), ((packed, width), BF16), ((packed, width), BF16),
+               ((packed, width), BF16), ((packed, width), F32), ((count, 2 * half), BF16), ((count, 2 * half), F32),
+               ((count, 2 * half), BF16), ((2 * b, 2 * HEAD_SIZE), F32), ((2 * b, 2 * HEAD_SIZE), F32)]
+    per_half = count // b
+    ring = [dma((2, m - 1))] * 8
+    return pl.pallas_call(
+        functools.partial(begin_kernel, n, m, names, b),
+        out_shape=tuple(jax.ShapeDtypeStruct(shape, dtype) for shape, dtype, _ in outs),
+        in_specs=[some] * 9 + [vmem] * 5,
+        out_specs=tuple(spec for *_, spec in outs),
+        scratch_shapes=[
+            *[pltpu.VMEM(shape, dtype) for shape, dtype in scratch],
+            dma((6 + m,)), dma((11 + 3 * per_half,)), dma((4,)), dma((4,)), dma((4,)), dma((4,)), dma((10,)), dma((10,)),
+            dma((2, 4)), dma((2, 4)), *ring, dma((2 + m,)), dma((2 + m,)),
+            dma((3, groups, per_half)), dma((3, groups, per_half)), dma((per_half,)), dma((per_half,)),
+        ],
+        compiler_params=pltpu.CompilerParams(collective_id=4, has_side_effects=True, vmem_limit_bytes=62 << 20),
+        cost_estimate=pl.CostEstimate(flops=20 << 30, transcendentals=0, bytes_accessed=100 << 20),
+        name="begin",
+    )(tokens, cot, wq, wk, wv, gate, up, down, wo, gains, q_gain, k_gain, table, starts)
 
 
 def turn_kernel(n, names, pieces, near_ref, far_ref, down_near_ref, down_far_ref, back_ref, middle_ref, cot_near_ref,
@@ -881,15 +1076,6 @@
     )(wide, down, thin, lone)
 
 
-def gated(x, *deps):
-    late = functools.reduce(jnp.logical_or, [dep != dep for dep in deps])
-    return jnp.where(late, jnp.zeros_like(x), x)
-
-
-def corner(x):
-    return x[(0,) * x.ndim].astype(F32)
-
-
 def shards(
     tokens,
     seq_lengths,
@@ -911,64 +1097,25 @@
     parts = lax.axis_size("dp")
     width = 2 * half
 
-    near_own = part_of(tokens, col, 0)
-    far_own = swap(near_own, "row")
-    qkv = jnp.concatenate(
-        [part_of(w, row, 1) for w in (query_weight, key_matrix, value_matrix)], axis=1)
-    qkv_sent = jnp.concatenate(
-        [part_of(w, 1 - row, 1) for w in (query_weight, key_matrix, value_matrix)], axis=1)
-    qkv_far = swap(qkv_sent, "row")
-    gains = jnp.stack([attn_gain, ffn_gain])
-    gains_far = swap(gains, "row")
-    far = ordered(far_own, swap(far_own, "col"), col)
-
-    def far_weight(sent):
-        piece = swap(gated(part_of(sent, group, 0, parts), corner(far_own)), "row")
-        return lax.all_gather(piece, "dp", axis=0, tiled=True), corner(piece)
-
-    gate_up_near = jnp.concatenate([part_of(gate_weight, row, 1), part_of(up_weight, row, 1)], axis=1)
-    gate_up_far, sign_one = far_weight(
-        jnp.concatenate([part_of(gate_weight, 1 - row, 1), part_of(up_weight, 1 - row, 1)], axis=1))
-    down_near = part_of(down_weight, row, 0)
-    down_far, sign_two = far_weight(part_of(down_weight, 1 - row, 0))
-    units = down_near.shape[0]
-
-    out_far = swap(gated(out_weight, sign_one, sign_two), "row")
-    out_c = jnp.concatenate([out_weight, out_far], axis=1)
-    out_n = swap(out_c, "col")
-    out_own = part_of(out_c, row, 0)
-    out_all = jnp.concatenate(
-        [out_own, part_of(out_n, row, 0), part_of(out_c, 1 - row, 0), part_of(out_n, 1 - row, 0)], axis=0)
-
-    cot_far_own = swap(gated(part_of(cotangent, col, 0), corner(out_far)), "row")
-    cot_far = ordered(cot_far_own, swap(cot_far_own, "col"), col)
-
+    names = ("dp", "row", "col")
     starts = layout(seq_lengths[0], packed)
-    cosine, sine = rope_tables(jnp.arange(packed, dtype=jnp.int32) - starts)
+    table = rope_table(jnp.arange(packed, dtype=jnp.int32) - starts)
     q_gain = jnp.tile(query_gain, 2)[None, :]
     k_gain = jnp.tile(key_gain, 2)[None, :]
-    small = (attn_gain[None, :], gains_far[0][None, :], qkv, qkv_far, q_gain, k_gain)
-    hid_near, hid_far, raw, q, k, v = project(tokens, far, *small, cosine, sine)
-
-    low, attended_raw, totals = attend(q, k, v, starts)
-
-    chip = jnp.concatenate([part_of(low, col, 0), swap(part_of(low, 1 - col, 0), "col")], axis=1)
-    attended = jnp.concatenate([chip, swap(chip, "row")], axis=1)
-    mine = jnp.concatenate([near_own, far_own], axis=1)
-    middle = mine.astype(F32) + dot(attended, out_all)
-    inverse_two = lax.rsqrt(jnp.sum(middle * middle, axis=1, keepdims=True) / width + EPSILON)
-    normal_two = middle * inverse_two
+    gains = jnp.stack([attn_gain, ffn_gain])
+    (far, gate_up_far, down_far, cot_far, gains_far, hid_near, hid_far, raw, q, k, v, attended_raw, totals, attended, middle,
+     hidden, out_own, qkv, qkv_far) = begin(
+        tokens, cotangent, query_weight, key_matrix, value_matrix, gate_weight, up_weight, down_weight, out_weight, gains,
+        q_gain, k_gain, table, starts[:, None], names, parts)
     gain_two = jnp.concatenate([ffn_gain, gains_far[1]])[None, :]
-    hidden_c = (normal_two * gain_two).astype(BF16)
-    hidden = ordered(hidden_c, swap(hidden_c, "col"), col)
-    gate_up = jnp.concatenate([gate_up_near, gate_up_far], axis=0)
-    down = jnp.concatenate([down_near, down_far], axis=1)
-    active, feed_grads, result, back = feed(hidden, cotangent, cot_far, gate_up, down)
+    units = down_weight.shape[0] // 2
+    active, feed_grads, result, back = feed(
+        row[None], hidden, cotangent, cot_far, gate_weight, up_weight, gate_up_far.reshape(half, -1), down_weight,
+        down_far.reshape(units, half))
 
     grad_down_near, grad_down_far = (
         over_t(active, cot).astype(BF16).reshape(parts, units // parts, -1) for cot in (cotangent, cot_far))
     grad_gate_up = over_t(hidden, feed_grads).astype(BF16).reshape(2, parts, half // parts, -1)
-    names = ("dp", "row", "col")
     branch, keep, ffn_sum, done, down_done = turn(
         grad_gate_up[0], grad_gate_up[1], grad_down_near, grad_down_far, back, middle, cotangent, cot_far, gain_two, names, parts)
 
@@ -983,7 +1130,7 @@
     dq, dk, dv, wide_full, down_full, output = retreat(
         q, k, v, grad_attended, attended_raw, totals, starts, done, down_done, result, middle[:, :half], names, parts)
     grads, to_near, to_far, stat_one, q_sum, k_sum, near_sum, far_sum = project_back(
-        dq, dk, dv, raw, tokens, far, *small, cosine, sine)
+        dq, dk, dv, raw, tokens, far, attn_gain[None, :], gains_far[:1], qkv, qkv_far.reshape(half, -1), q_gain, k_gain, table)
     near_grads, far_grads = (
         over_t(hid, grads).astype(BF16).reshape(parts, half // parts, -1) for hid in (hid_near, hid_far))
 

time: 562 us -> 476 us (0.85)
  waiting for transfers between devices: 67.1 us -> 0.01 us
  Pallas kernels: 332 us -> 397 us
  other arithmetic: 38.2 us -> 8.43 us
  local copies, waits for them, and re-layouts: 46.6 us -> 25.5 us
  between operations: 20.3 us -> 1.44 us
  starting transfers between devices: 12.1 us -> 0.01 us
    ppermute x14 -> x1, waiting for transfers between devices: 67.1 us -> 0.01 us  [swap(): lax.ppermute(part, axis, [(0, 1), (1, 0)])]
    pallas_call x2 -> x1, Pallas kernels: 32.1 us -> 98.7 us  [begin(): pl.pallas_call(functools.partial(begin_kernel, n, m, names, b), out_shape...]
    select_n x4 -> x1, other arithmetic: 13.3 us -> 0.01 us  [ordered(): jnp.where(index == 0, jnp.concatenate([own, other], axis), jnp.concatenat...]
    concatenate x6 -> x1, other arithmetic: 14 us -> 0.83 us  [rope_table(): return jnp.concatenate([jnp.cos(angles), jnp.sin(angles)], axis=0)]
    ppermute x14 -> x1, starting transfers between devices: 11.6 us -> 0.01 us  [swap(): lax.ppermute(part, axis, [(0, 1), (1, 0)])]
    dynamic_slice x10 -> x2, local copies, waits for them, and re-layouts: 10.9 us -> 1.3 us  [part_of(): return lax.dynamic_slice_in_dim(x, index * size, size, axis)]
    unnamed x102 -> x58, local copies, waits for them, and re-layouts: 16.2 us -> 10.8 us
    dot_general x9 -> x8, matrix products: 38.5 us -> 35 us  [dot(): return lax.dot_general(a, b, dims, preferred_element_type=F32)]
  transfers between devices with their start and end apart: 16 -> 1, of which waited for: 4 -> 0; matrix products, arithmetic and copies ran while one was open for 10% -> 2% of each run, Pallas kernels for 6% -> 19%
where the time goes in v5:
time: 476 us; the launch traced here: 468 us
  Pallas kernels  397 us (83%)
  matrix products  35 us (7%)
  local copies, waits for them, and re-layouts  25.5 us (5%)
  other arithmetic  8.43 us (2%)
    pallas_call x1, Pallas kernels, begin(): pl.pallas_call(functools.partial(begin_kernel, n, m, names, b), out_shape...  98.7 us
    pallas_call x1, Pallas kernels, turn(): pl.pallas_call(functools.partial(turn_kernel, n, names, pieces), out_shap...  91.9 us
    pallas_call x1, Pallas kernels, retreat(): pl.pallas_call(functools.partial(retreat_kernel, n, names, b, packed), ou...  73.8 us
    pallas_call x1, Pallas kernels, close(): pl.pallas_call(functools.partial(close_kernel, n, names), out_shape=(shap...  72.3 us
    pallas_call x1, Pallas kernels, feed(): pl.pallas_call(functools.partial(feed_kernel, units), out_shape=(out(unit...  39.3 us
    dot_general x8, matrix products, dot(): return lax.dot_general(a, b, dims, preferred_element_type=F32)  35 us
    pallas_call x1, Pallas kernels, project_back(): pl.pallas_call(functools.partial(project_back_kernel, groups), out_shape=...  14.6 us
    unnamed x58, local copies, waits for them, and re-layouts  10.8 us
  transfers between devices with their start and end apart: 1, of which 0 were waited for; matrix products, arithmetic and copies ran while one was open for 2% of the time, Pallas kernels for 19%

profile of v5, /device:TPU:0, one launch (start us, length us, event | category | flops | bytes accessed | tf_op | source)
XLA Modules:
  0.0 467.5 jit_solution(12797631516285359856)
XLA Ops:
  0.7 0.8 fusion.11
  1.4 0.7 fusion.12
  2.1 0.1 fusion.8
  2.2 0.7 tile.4
  2.8 0.6 broadcast_in_dim_tile.6.q_gain_ref
  3.4 0.7 tile.5
  4.1 0.6 broadcast_in_dim_tile.7.k_gain_ref
  4.7 0.1 fusion.9
  4.8 1.3 copy.28.starts_ref
  6.2 1.3 pad_maximum_fusion.2.gains_ref
  7.5 1.0 multiply_cosine_fusion
  8.4 0.8 pad_maximum_fusion.table_ref
  9.3 98.7 %begin.1 = (bf16[2048,512]{1,0:T(8,128)(2,1)}, bf16[8,64,2304]{2,1,0:T(8,128)(2,1)}, bf16[8,144,512]{2,1,0:T(8,128)(2,1)}, bf16[2048,512]{1,0:T(8,128)(2,1)}, f3...) custom-call(bf16[2048,512]{1,0:T(8,128)(2,1)} %tokens_ref.1, ...), custom_call_target="tpu_custom_call" | custom-call | flops 21474836480 | bytes 104857600 | tf_op jit(solution)/shard_map/begin/pallas_call | solution.py:667
  108.0 39.3 %feed.1 = (bf16[2048,1152]{1,0:T(8,128)(2,1)}, bf16[2048,2304]{1,0:T(8,128)(2,1)}, bf16[2048,1024]{1,0:T(8,128)(2,1)}, bf16[2048,1024]{1,0:T(8,128)(2,1)}) custom-call(s32[1]{0:T(128)} %bitcast.6.row_ref, bf16[2048,1024]{1,0:T(8,128)(2,1)} %get-tuple-element.69.hidden_ref, bf16[2048,512]{1,0:T(8,128)(2,1)} %cot_near_ref.3, ...), custom_call_target="tpu_custom_call" | custom-call | flops 28991029248 | bytes 38010880 | tf_op jit(solution)/shard_map/feed/pallas_call | solution.py:206
  147.4 6.1 %convolution_convert_fusion.2 = bf16[1152,512]{1,0:T(8,128)(2,1)} fusion(bf16[2048,1152]{1,0:T(8,128)(2,1)} %get-tuple-element.74, bf16[2048,512]{1,0:T(8,128)(2,1)S(1)} %copy-done.20), kind=kOutput, calls=%fused_computation.2 | convolution fusion | flops 2416508928 | bytes 7995392 | tf_op jit(solution)/shard_map/dot_general | solution.py:19
  153.5 3.7 convolution_convert_fusion.1
  157.2 13.8 %convolution_convert_fusion = bf16[1024,2304]{1,0:T(8,128)(2,1)S(1)} fusion(bf16[2048,1024]{1,0:T(8,128)(2,1)} %get-tuple-element.69.hidden_ref, bf16[2048,2304]{1,0:T(8,128)(2,1)} %get-tuple-element.73), kind=kOutput, calls=%fused_computation | convolution fusion | flops 9666035712 | bytes 18350080 | tf_op jit(solution)/shard_map/dot_general | solution.py:19
  171.0 2.5 fusion.15
  173.5 0.6 pad_maximum_fusion.3
  174.1 91.9 %turn.1 = (bf16[2048,1024]{1,0:T(8,128)(2,1)}, f32[1024,512]{1,0:T(8,128)}, f32[1,1024]{1,0:T(1,128)}, bf16[4,64,1152]{2,1,0:T(8,128)(2,1)}, bf16[4,144,256]{2,1,0:T(8,128)(2,1)}) custom-call(bf16[8,64,2304]{2,1,0:T(8,128)(2,1)} %bitcast.64, bf16[8,64,2304]{2,1,0:T(8,128)(2,1)} %bitcast.63, bf16[8,144,512]{2,1,0:T(8,128)(2,1)} %bitcast.68, ...), custom_call_target="tpu_custom_call" | custom-call | flops 83886080 | bytes 157286400 | tf_op jit(solution)/shard_map/turn/pallas_call | solution.py:758
  266.1 1.7 slice.90
  267.8 3.0 fusion.22
  270.9 0.8 pad_maximum_fusion.1
  271.7 1.5 slice.94.middle_ref
  273.2 1.5 copy-done.13
  274.7 0.7 fusion.6
  275.5 1.7 fusion.grad_ref
  277.2 1.0 fusion.16
  278.3 73.8 %retreat.1 = (f32[2048,256]{1,0:T(8,128)}, f32[2048,256]{1,0:T(8,128)}, f32[2048,256]{1,0:T(8,128)}, bf16[2,8,64,2304]{3,2,1,0:T(8,128)(2,1)}, bf16[2,8,144,512]...) custom-call(bf16[2048,256]{1,0:T(8,128)(2,1)} %get-tuple-element.66.q_ref, bf16[2048,256]{1,0:T(8,128)(2,1)} %get-tuple-element.67.k_ref, ...), custom_call_target="tpu_custom_call" | custom-call | flops 26843545600 | bytes 10485760 | tf_op jit(solution)/shard_map/retreat/pallas_call | solution.py:910
  352.2 14.6 %project_back.1 = (bf16[2048,512]{1,0:T(8,128)(2,1)S(1)}, bf16[2048,512]{1,0:T(8,128)(2,1)S(1)}, bf16[2048,512]{1,0:T(8,128)(2,1)S(1)}, f32[2048,128]{1,0:T(8,12...) custom-call(f32[2048,256]{1,0:T(8,128)} %get-tuple-element.87.dq_ref, ...), custom_call_target="tpu_custom_call" | custom-call | flops 2147483648 | bytes 17825792 | tf_op jit(solution)/shard_map/project_back/pallas_call | solution.py:121
  366.9 1.0 copy-done.5
  367.8 2.2 convolution_convert_fusion.4
  370.1 0.7 concatenate.41
  370.8 3.8 convolution_convert_fusion.3
  374.6 1.2 maximum_add_fusion
  375.8 0.9 fusion.2
  376.8 72.3 %close.1 = (bf16[2,8,64,512]{3,2,1,0:T(8,128)(2,1)}, bf16[8,64,512]{2,1,0:T(8,128)(2,1)}, f32[24,128]{1,0:T(8,128)}, bf16[2048,512]{1,0:T(8,128)(2,1)}) custom-call(bf16[8,64,512]{2,1,0:T(8,128)(2,1)} %bitcast.65, bf16[8,64,512]{2,1,0:T(8,128)(2,1)} %bitcast.66, bf16[8,64,512]{2,1,0:T(8,128)(2,1)} %bitcast.67, bf16[2048,512]{1,0:T(8,128)(2,1)} %copy-done.2, ...), custom_call_target="tpu_custom_call" | custom-call | flops 41943040 | bytes 209715200 | tf_op jit(solution)/shard_map/close/pallas_call | solution.py:1025
  449.1 0.7 slice_bitcast_fusion
  449.7 0.7 dynamic_slice.10
  450.4 0.6 dynamic_slice.11
  451.0 1.3 fusion.19
  452.4 2.3 copy-done
  454.7 1.2 copy-done.6
  456.0 1.0 copy-done.9
  457.0 6.4 %widen.1 = (f32[512,2304]{1,0:T(8,128)}, f32[512,2304]{1,0:T(8,128)}, f32[2304,512]{1,0:T(8,128)}, f32[512,512]{1,0:T(8,128)}, f32[512,256]{1,0:T(8,128)}, /*index=5*/f32[512,256]{1,0:T(8,128)}, f32[512,512]{1,0:T(8,128)}) custom-call(bf16[2,512,2304]{2,1,0:T(8,128)(2,1)S(1)} %bitcast.53, bf16[2304,512]{1,0:T(8,128)(2,1)S(1)} %bitcast.54, ...), custom_call_target="tpu_custom_call" | custom-call | bytes 25952256 | tf_op jit(solution)/shard_map/widen/pallas_call | solution.py:1067
  463.4 1.3 copy.31
  464.8 1.0 copy-done.17
  465.8 1.3 copy.32
  (61 shorter events, 0.3 us)
Async XLA Ops:
  4.8 103.2 %copy-start.23 = (s32[2048]{0:T(1024)}, s32[2048]{0:T(1024)S(1)}, u32[]{:S(2)}) copy-start(s32[2048]{0:T(1024)S(1)} %fusion.9) | copy-start | bytes 24580
  108.0 39.3 %copy-start.20 = (bf16[2048,512]{1,0:T(8,128)(2,1)S(1)}, bf16[2048,512]{1,0:T(8,128)(2,1)}, u32[]{:S(2)}) copy-start(bf16[2048,512]{1,0:T(8,128)(2,1)} %cot_near_ref.3) | copy-start | bytes 6291460
  147.4 6.2 %copy-start.21 = (bf16[2048,512]{1,0:T(8,128)(2,1)S(1)}, bf16[2048,512]{1,0:T(8,128)(2,1)}, u32[]{:S(2)}) copy-start(bf16[2048,512]{1,0:T(8,128)(2,1)} %get-tuple-element.70.cot_far_ref) | copy-start | bytes 6291460
  147.4 6.2 %copy-start.27 = (bf16[2048,1152]{1,0:T(8,128)(2,1)S(1)}, bf16[2048,1152]{1,0:T(8,128)(2,1)}, u32[]{:S(2)}) copy-start(bf16[2048,1152]{1,0:T(8,128)(2,1)} %get-tuple-element.74) | copy-start | bytes 14155780
  171.0 2.5 copy-start.26
  171.0 2.5 copy-start.24
  267.8 3.9 copy-start.14
  270.9 2.3 copy-start.22
  271.7 3.0 copy-start.13
  271.7 102.8 %collective-permute-start = (bf16[512,512]{1,0:T(8,128)(2,1)}, bf16[512,512]{1,0:T(8,128)(2,1)}, u32[]{:S(2)}, u32[]{:S(2)}) collective-permute-start(bf16[512,512]{1,0:T(8,128)(2,1)} %pad_maximum_fusion.1), channel_id=1, source_target_pairs={{0,1},{1,0},{2,3},{3,2},{4,5},{5,4},{6,7},{7,6},{8,9},{9,8},{10,11... | collective-permute-start | bytes 1572872 | tf_op jit(solution)/shard_map/ppermute | solution.py:154
  277.2 1.0 copy-start.25
  278.2 73.9 %copy-start.4 = (f32[64,2048]{1,0:T(8,128)S(1)}, f32[64,2048]{1,0:T(8,128)}, u32[]{:S(2)}) copy-start(f32[64,2048]{1,0:T(8,128)} %pad_maximum_fusion.table_ref) | copy-start | bytes 1572868
  278.2 73.9 %copy-start.7 = (bf16[512,512]{1,0:T(8,128)(2,1)S(1)}, bf16[512,512]{1,0:T(8,128)(2,1)}, u32[]{:S(2)}) copy-start(bf16[512,512]{1,0:T(8,128)(2,1)} %get-tuple-element.92.w_near_ref) | copy-start | bytes 1572868
  278.2 73.9 %copy-start.8 = (bf16[8,64,512]{2,1,0:T(8,128)(2,1)S(1)}, bf16[8,64,512]{2,1,0:T(8,128)(2,1)}, u32[]{:S(2)}) copy-start(bf16[8,64,512]{2,1,0:T(8,128)(2,1)} %get-tuple-element.93) | copy-start | bytes 1572868
  278.2 73.9 %copy-start.10 = (f32[512]{0:T(512)S(1)}, f32[512]{0:T(512)}, u32[]{:S(2)}) copy-start(f32[512]{0:T(512)} %param.23) | copy-start | bytes 6148
  278.3 73.9 %copy-start.11 = (f32[1,128]{1,0:T(1,128)S(1)}, f32[1,128]{1,0:T(1,128)}, u32[]{:S(2)}) copy-start(f32[1,128]{1,0:T(1,128)} %broadcast_in_dim_tile.6.q_gain_ref) | copy-start | bytes 1540
  278.3 73.9 %copy-start.12 = (f32[1,128]{1,0:T(1,128)S(1)}, f32[1,128]{1,0:T(1,128)}, u32[]{:S(2)}) copy-start(f32[1,128]{1,0:T(1,128)} %broadcast_in_dim_tile.7.k_gain_ref) | copy-start | bytes 1540
  352.2 15.6 %copy-start.16 = (bf16[2048,512]{1,0:T(8,128)(2,1)S(1)}, bf16[2048,512]{1,0:T(8,128)(2,1)}, u32[]{:S(2)}) copy-start(bf16[2048,512]{1,0:T(8,128)(2,1)} %get-tuple-element.86) | copy-start | bytes 6291460
  366.9 1.0 copy-start.5
  367.8 2.2 copy-start.2
  367.8 2.2 copy-start.3
  370.8 3.8 copy-start.18
  370.8 3.8 copy-start.19
  376.8 75.6 %copy-start.1 = (bf16[2,8,144,512]{3,2,1,0:T(8,128)(2,1)S(1)}, bf16[2,8,144,512]{3,2,1,0:T(8,128)(2,1)}, u32[]{:S(2)}) copy-start(bf16[2,8,144,512]{3,2,1,0:T(8,128)(2,1)} %get-tuple-element.108) | copy-start | bytes 7077892
  452.4 2.3 copy-start
  454.7 1.2 copy-start.6
  455.9 1.0 copy-start.9
  457.0 6.4 %copy-start.15 = (bf16[2048,512]{1,0:T(8,128)(2,1)S(1)}, bf16[2048,512]{1,0:T(8,128)(2,1)}, u32[]{:S(2)}) copy-start(bf16[2048,512]{1,0:T(8,128)(2,1)} %get-tuple-element.156) | copy-start | bytes 6291460
  463.4 2.3 copy-start.17
